TPU v7x, 32 devices: a whole 2x2x4 slice. The times are simulated.
32 devices in a mesh: dp: 2 (over x), sp: 4 (over y, core), fs: 4 (over z).
Axes of the slice: x: 2, y: 2, z: 4, core: 2. Of those that a mesh axis runs over, the one named last changes fastest.
Arguments:
- tokens: bfloat16 [8, 2048, 768], P('dp', ('sp', 'fs')), may hold values from -6 to 6
- expert_ids: int32 [8, 2048, 2], P('dp', ('sp', 'fs')), may hold values from 0 to 15, all different within a row
- fill_order: int32 [8, 2048], P('dp', ('sp', 'fs')), may hold values from 0 to 511
- attention_gain: bfloat16 [768], P(('sp', 'fs')), may hold values from 0.5 to 1.5
- query_weight: bfloat16 [768, 768], P(('sp', 'fs')), may hold values from -0.21875 to 0.21875
- key_weight: bfloat16 [768, 768], P(('sp', 'fs')), may hold values from -0.21875 to 0.21875
- value_weight: bfloat16 [768, 768], P(('sp', 'fs')), may hold values from -0.21875 to 0.21875
- output_weight: bfloat16 [768, 768], P(('sp', 'fs')), may hold values from -1.25 to 1.25
- mixer_gain: bfloat16 [768], P(('sp', 'fs')), may hold values from 0.5 to 1.5
- router_weight: bfloat16 [768, 16], P(('sp', 'fs')), may hold values from -0.15625 to 0.15625
- shared_gate: bfloat16 [768, 2048], P(('sp', 'fs')), may hold values from -0.21875 to 0.21875
- shared_up: bfloat16 [768, 2048], P(('sp', 'fs')), may hold values from -0.21875 to 0.21875
- shared_down: bfloat16 [2048, 768], P(('sp', 'fs')), may hold values from -0.125 to 0.125
- expert_gate: bfloat16 [16, 768, 2048], P('fs', 'sp'), may hold values from -0.21875 to 0.21875
- expert_up: bfloat16 [16, 768, 2048], P('fs', 'sp'), may hold values from -0.21875 to 0.21875
- expert_down: bfloat16 [16, 768, 2048], P('fs', 'sp'), may hold values from -0.125 to 0.125
- cotangent: bfloat16 [8, 2048, 768], P('dp', ('sp', 'fs')), may hold values from -6 to 6
Outputs:
- output: bfloat16 [8, 2048, 768], P('dp', ('sp', 'fs'))
- grad_tokens: float32 [8, 2048, 768], P('dp', ('sp', 'fs'))
- grad_attention_gain: float32 [768], P(('sp', 'fs'))
- grad_query_weight: float32 [768, 768], P(('sp', 'fs'))
- grad_key_weight: float32 [768, 768], P(('sp', 'fs'))
- grad_value_weight: float32 [768, 768], P(('sp', 'fs'))
- grad_output_weight: float32 [768, 768], P(('sp', 'fs'))
- grad_mixer_gain: float32 [768], P(('sp', 'fs'))
- grad_router_weight: float32 [768, 16], P(('sp', 'fs'))
- grad_shared_gate: float32 [768, 2048], P(('sp', 'fs'))
- grad_shared_up: float32 [768, 2048], P(('sp', 'fs'))
- grad_shared_down: float32 [2048, 768], P(('sp', 'fs'))
- grad_expert_gate: float32 [16, 768, 2048], P('fs', 'sp')
- grad_expert_up: float32 [16, 768, 2048], P('fs', 'sp')
- grad_expert_down: float32 [16, 768, 2048], P('fs', 'sp')
Inputs may be any that keep to these rules, and one draw needn't show every extreme that they name: `expert_ids`: the 2 ids of one token differ.
All inputs are finite; a program needn't handle non-finite values.
Results may differ from a plain program's by a relative error of at most 0.024.
Values may be sent and summed in bfloat16 or wider, within the bound.
A program may use at most 320 MiB of HBM per device.

v0:
```python
import math

import jax
import jax.numpy as jnp
from jax import lax
from jax.sharding import PartitionSpec as P

HEADS = 12
HEAD_DIM = 64
EXPERTS = 16
TOPK = 2
CAP = 72


EPSILON = 1e-06
MASKED = -1e30


def norm_apply(values, gain_row):
    inverse_root = lax.rsqrt(jnp.mean(values * values, axis=-1, keepdims=True) + EPSILON)
    return values * inverse_root * gain_row


def swish(values):
    return values * jax.nn.sigmoid(values)


def glu_product(gate_part, up_part):
    return swish(gate_part) * up_part


def rotate(values, positions):
    half_dim = values.shape[-1] // 2
    frequency = 10000.0 ** (-jnp.arange(half_dim, dtype=jnp.float32) / half_dim)
    angles = positions.astype(jnp.float32)[:, None] * frequency[None, :]
    cosine_table = jnp.cos(angles)[:, None, :]
    sine_table = jnp.sin(angles)[:, None, :]
    front_part = values[..., :half_dim]
    back_part = values[..., half_dim:]
    return jnp.concatenate(
        [
            front_part * cosine_table - back_part * sine_table,
            back_part * cosine_table + front_part * sine_table,
        ],
        axis=-1,
    )


def place_rows(indices, quarter_rows, segment_rows, fs_count):
    source_device = indices // quarter_rows
    row_inside = indices % quarter_rows
    return (
        row_inside // segment_rows * fs_count + source_device
    ) * segment_rows + row_inside % segment_rows


def to_heads(stacked):
    return lax.all_to_all(stacked, "sp", split_axis=3, concat_axis=2, tiled=True)


def to_tokens(stacked):
    return lax.all_to_all(stacked, "sp", split_axis=2, concat_axis=3, tiled=True)


def to_experts(buffer):
    return lax.all_to_all(buffer, "fs", split_axis=1, concat_axis=0, tiled=True)


def from_experts(buffer):
    return lax.all_to_all(buffer, "fs", split_axis=0, concat_axis=1, tiled=True)


def score_grads(
    query_part,
    query_rows,
    key_part,
    value_part,
    key_rows,
    grad_part,
    lse_part,
    delta_part,
    score_scale,
):
    allowed = key_rows[None, None, None, :] <= query_rows[None, None, :, None]
    scores = (
        jnp.einsum("bqhd,bkhd->bhqk", query_part, key_part, preferred_element_type=jnp.float32)
        * score_scale
    )
    weights = jnp.where(allowed, jnp.exp(scores - lse_part[..., None]), 0.0)
    grad_value = jnp.einsum(
        "bhqk,bqhd->bkhd",
        weights.astype(jnp.bfloat16),
        grad_part,
        preferred_element_type=jnp.float32,
    )
    grad_weights = jnp.einsum(
        "bqhd,bkhd->bhqk", grad_part, value_part, preferred_element_type=jnp.float32
    )
    grad_scores = (weights * (grad_weights - delta_part[..., None]) * score_scale).astype(
        jnp.bfloat16
    )
    grad_query = jnp.einsum(
        "bhqk,bkhd->bqhd", grad_scores, key_part, preferred_element_type=jnp.float32
    )
    grad_key = jnp.einsum(
        "bhqk,bqhd->bkhd", grad_scores, query_part, preferred_element_type=jnp.float32
    )
    return (grad_query, grad_key, grad_value)


def per_device(
    tokens,
    expert_ids,
    fill_order,
    attention_gain,
    query_weight,
    key_weight,
    value_weight,
    output_weight,
    mixer_gain,
    router_weight,
    shared_gate,
    shared_up,
    shared_down,
    expert_gate,
    expert_up,
    expert_down,
    cotangent,
):
    seq_count, seg_rows, model_width = tokens.shape
    token_count = seq_count * seg_rows
    fs_count = lax.axis_size("fs")
    sp_count = lax.axis_size("sp")
    fs_place = lax.axis_index("fs")
    local_heads = HEADS // sp_count
    score_scale = HEAD_DIM ** (-0.5)
    (
        gain_full,
        query_full,
        key_full,
        value_full,
        output_full,
        mixer_full,
        router_full,
        shared_gate_full,
        shared_up_full,
        shared_down_full,
    ) = (
        lax.all_gather(attention_gain, ("sp", "fs"), axis=0, tiled=True),
        lax.all_gather(query_weight, ("sp", "fs"), axis=0, tiled=True),
        lax.all_gather(key_weight, ("sp", "fs"), axis=0, tiled=True),
        lax.all_gather(value_weight, ("sp", "fs"), axis=0, tiled=True),
        lax.all_gather(output_weight, ("sp", "fs"), axis=0, tiled=True),
        lax.all_gather(mixer_gain, ("sp", "fs"), axis=0, tiled=True),
        lax.all_gather(router_weight, ("sp", "fs"), axis=0, tiled=True),
        lax.all_gather(shared_gate, ("sp", "fs"), axis=0, tiled=True),
        lax.all_gather(shared_up, ("sp", "fs"), axis=0, tiled=True),
        lax.all_gather(shared_down, ("sp", "fs"), axis=0, tiled=True),
    )
    expert_gate_full, expert_up_full, expert_down_full = (
        lax.all_gather(expert_gate, "sp", axis=1, tiled=True),
        lax.all_gather(expert_up, "sp", axis=1, tiled=True),
        lax.all_gather(expert_down, "sp", axis=1, tiled=True),
    )
    residual = tokens.astype(jnp.float32)
    gain_one = gain_full.astype(jnp.float32)
    gain_two = mixer_full.astype(jnp.float32)
    normed = norm_apply(residual, gain_one).astype(jnp.bfloat16)
    query_raw = jnp.dot(normed, query_full, preferred_element_type=jnp.float32).astype(jnp.bfloat16)
    key_raw = jnp.dot(normed, key_full, preferred_element_type=jnp.float32).astype(jnp.bfloat16)
    value_raw = jnp.dot(normed, value_full, preferred_element_type=jnp.float32).astype(jnp.bfloat16)
    heads_view = to_heads(jnp.stack([query_raw, key_raw, value_raw]))
    quarter_rows = heads_view.shape[2]
    head_shape = (seq_count, quarter_rows, local_heads, HEAD_DIM)
    flat_width = local_heads * HEAD_DIM
    own_rows = place_rows(
        fs_place * quarter_rows + jnp.arange(quarter_rows, dtype=jnp.int32),
        quarter_rows,
        seg_rows,
        fs_count,
    )

    def rotate_own(values):
        return rotate(values, own_rows)

    query_rot = rotate_own(heads_view[0].reshape(head_shape).astype(jnp.float32)).astype(
        jnp.bfloat16
    )
    key_rot = rotate_own(heads_view[1].reshape(head_shape).astype(jnp.float32)).astype(jnp.bfloat16)
    key_flat = key_rot.reshape(seq_count, quarter_rows, flat_width)
    value_flat = heads_view[2]
    keys_all, values_all = (
        lax.all_gather(key_flat, "fs", axis=1, tiled=True),
        lax.all_gather(value_flat, "fs", axis=1, tiled=True),
    )
    total_rows = keys_all.shape[1]
    block_rows = math.gcd(quarter_rows, 512)
    part_shape = (seq_count, block_rows, local_heads, HEAD_DIM)
    offsets = jnp.arange(total_rows // block_rows, dtype=jnp.int32) * block_rows

    def key_slices(offset):
        key_part = lax.dynamic_slice_in_dim(keys_all, offset, block_rows, 1).reshape(part_shape)
        value_part = lax.dynamic_slice_in_dim(values_all, offset, block_rows, 1).reshape(part_shape)
        key_rows = place_rows(
            offset + jnp.arange(block_rows, dtype=jnp.int32), quarter_rows, seg_rows, fs_count
        )
        return (key_part, value_part, key_rows)

    def forward_block(carried, offset):
        running_max, running_sum, running_acc = carried
        key_part, value_part, key_rows = key_slices(offset)
        allowed = key_rows[None, None, None, :] <= own_rows[None, None, :, None]
        scores = (
            jnp.einsum("bqhd,bkhd->bhqk", query_rot, key_part, preferred_element_type=jnp.float32)
            * score_scale
        )
        scores = jnp.where(allowed, scores, MASKED)
        new_max = jnp.maximum(running_max, jnp.max(scores, axis=-1))
        weights = jnp.where(allowed, jnp.exp(scores - new_max[..., None]), 0.0)
        factor = jnp.exp(running_max - new_max)
        running_sum = running_sum * factor + jnp.sum(weights, axis=-1)
        running_acc = running_acc * factor[..., None] + jnp.einsum(
            "bhqk,bkhd->bhqd",
            weights.astype(jnp.bfloat16),
            value_part,
            preferred_element_type=jnp.float32,
        )
        return ((new_max, running_sum, running_acc), None)

    start_state = (
        jnp.full((seq_count, local_heads, quarter_rows), MASKED, jnp.float32),
        jnp.zeros((seq_count, local_heads, quarter_rows), jnp.float32),
        jnp.zeros((seq_count, local_heads, quarter_rows, HEAD_DIM), jnp.float32),
    )
    (final_max, final_sum, final_acc), _ = lax.scan(forward_block, start_state, offsets)
    attended_heads = (final_acc / final_sum[..., None]).astype(jnp.bfloat16)
    log_total = final_max + jnp.log(final_sum)
    attended_view = jnp.transpose(attended_heads, (0, 2, 1, 3))
    attended_flat = attended_view.reshape(seq_count, quarter_rows, flat_width)
    attended_tokens = to_tokens(attended_flat[None])[0]
    middle = residual + jnp.dot(attended_tokens, output_full, preferred_element_type=jnp.float32)
    mixed_in = norm_apply(middle, gain_two).astype(jnp.bfloat16)
    token_rows = mixed_in.reshape(token_count, model_width)
    logits = jnp.dot(token_rows, router_full, preferred_element_type=jnp.float32)
    choices = expert_ids.reshape(token_count, TOPK)
    expert_onehot = choices[:, :, None] == jnp.arange(EXPERTS, dtype=jnp.int32)[None, None, :]
    onehot_float = expert_onehot.astype(jnp.float32)

    def gate_values(raw_logits):
        shifted = jnp.exp(raw_logits - jnp.max(raw_logits, axis=-1, keepdims=True))
        router_probs = shifted / jnp.sum(shifted, axis=-1, keepdims=True)
        picked = jnp.sum(router_probs[:, None, :] * onehot_float, axis=2)
        return picked / jnp.sum(picked, axis=1, keepdims=True)

    gate_weights, gate_pull = jax.vjp(gate_values, logits)
    shared_gate_val = jnp.dot(mixed_in, shared_gate_full, preferred_element_type=jnp.float32)
    shared_up_val = jnp.dot(mixed_in, shared_up_full, preferred_element_type=jnp.float32)
    shared_hidden_full, shared_pull = jax.vjp(glu_product, shared_gate_val, shared_up_val)
    shared_hidden = shared_hidden_full.astype(jnp.bfloat16)
    shared_out = jnp.dot(shared_hidden, shared_down_full, preferred_element_type=jnp.float32)
    onehot_int = expert_onehot.astype(jnp.int32)
    per_token = jnp.sum(onehot_int, axis=1)
    fill_rank = fill_order.reshape(token_count)
    earlier = (fill_rank[None, :] < fill_rank[:, None]).astype(jnp.int32)
    counts = jnp.dot(earlier, per_token, preferred_element_type=jnp.int32)
    slot_ranks = jnp.sum(counts[:, None, :] * onehot_int, axis=2)
    slot_total = CAP * EXPERTS
    slots = jnp.where(slot_ranks < CAP, slot_ranks * EXPERTS + choices, slot_total).reshape(-1)
    outgoing = (
        jnp.zeros((slot_total, model_width), jnp.bfloat16)
        .at[slots]
        .set(jnp.repeat(token_rows, TOPK, axis=0), mode="drop")
    )
    incoming = to_experts(outgoing.reshape(CAP, EXPERTS, model_width))
    expert_gate_val = jnp.einsum(
        "red,edf->ref", incoming, expert_gate_full, preferred_element_type=jnp.float32
    )
    expert_up_val = jnp.einsum(
        "red,edf->ref", incoming, expert_up_full, preferred_element_type=jnp.float32
    )
    expert_hidden_full, expert_pull = jax.vjp(glu_product, expert_gate_val, expert_up_val)
    expert_hidden = expert_hidden_full.astype(jnp.bfloat16)
    expert_out = jnp.einsum(
        "ref,edf->red", expert_hidden, expert_down_full, preferred_element_type=jnp.float32
    ).astype(jnp.bfloat16)
    returned = from_experts(expert_out).reshape(slot_total, model_width)
    padded = jnp.concatenate([returned, jnp.zeros((1, model_width), jnp.bfloat16)], axis=0)
    picked_rows = padded[slots].reshape(token_count, TOPK, model_width).astype(jnp.float32)
    combined = jnp.sum(gate_weights[:, :, None] * picked_rows, axis=1)
    result = (
        middle.reshape(token_count, model_width)
        + shared_out.reshape(token_count, model_width)
        + combined
    )
    output = result.astype(jnp.bfloat16).reshape(seq_count, seg_rows, model_width)
    grad_result = cotangent.astype(jnp.float32).reshape(token_count, model_width)
    grad_gates = jnp.sum(grad_result[:, None, :] * picked_rows, axis=2)
    grad_slots = (
        (gate_weights[:, :, None] * grad_result[:, None, :])
        .astype(jnp.bfloat16)
        .reshape(token_count * TOPK, model_width)
    )
    grad_outgoing = (
        jnp.zeros((slot_total, model_width), jnp.bfloat16).at[slots].set(grad_slots, mode="drop")
    )
    grad_incoming = to_experts(grad_outgoing.reshape(CAP, EXPERTS, model_width))
    grad_expert_down = jnp.einsum(
        "red,ref->edf", grad_incoming, expert_hidden, preferred_element_type=jnp.float32
    )
    grad_expert_hidden = jnp.einsum(
        "red,edf->ref", grad_incoming, expert_down_full, preferred_element_type=jnp.float32
    )
    grad_gate_part, grad_up_part = expert_pull(grad_expert_hidden)
    grad_gate_part = grad_gate_part.astype(jnp.bfloat16)
    grad_up_part = grad_up_part.astype(jnp.bfloat16)
    grad_expert_gate = jnp.einsum(
        "red,ref->edf", incoming, grad_gate_part, preferred_element_type=jnp.float32
    )
    grad_expert_up = jnp.einsum(
        "red,ref->edf", incoming, grad_up_part, preferred_element_type=jnp.float32
    )
    grad_pair_rows = (
        jnp.einsum(
            "ref,edf->red", grad_gate_part, expert_gate_full, preferred_element_type=jnp.float32
        )
        + jnp.einsum(
            "ref,edf->red", grad_up_part, expert_up_full, preferred_element_type=jnp.float32
        )
    ).astype(jnp.bfloat16)
    grad_returned = from_experts(grad_pair_rows).reshape(slot_total, model_width)
    grad_padded = jnp.concatenate(
        [grad_returned, jnp.zeros((1, model_width), jnp.bfloat16)], axis=0
    )
    grad_mixed = jnp.sum(
        grad_padded[slots].reshape(token_count, TOPK, model_width).astype(jnp.float32), axis=1
    )
    (grad_logits,) = gate_pull(grad_gates)
    grad_logits = grad_logits.astype(jnp.bfloat16)
    grad_router = jnp.einsum(
        "td,te->de", token_rows, grad_logits, preferred_element_type=jnp.float32
    )
    grad_mixed = grad_mixed + jnp.einsum(
        "te,de->td", grad_logits, router_full, preferred_element_type=jnp.float32
    )
    grad_shared_out = grad_result.astype(jnp.bfloat16).reshape(seq_count, seg_rows, model_width)
    grad_shared_down = jnp.einsum(
        "blf,bld->fd", shared_hidden, grad_shared_out, preferred_element_type=jnp.float32
    )
    grad_shared_hidden = jnp.einsum(
        "bld,fd->blf", grad_shared_out, shared_down_full, preferred_element_type=jnp.float32
    )
    grad_shared_gate_part, grad_shared_up_part = shared_pull(grad_shared_hidden)
    grad_shared_gate_part = grad_shared_gate_part.astype(jnp.bfloat16)
    grad_shared_up_part = grad_shared_up_part.astype(jnp.bfloat16)
    grad_shared_gate = jnp.einsum(
        "bld,blf->df", mixed_in, grad_shared_gate_part, preferred_element_type=jnp.float32
    )
    grad_shared_up = jnp.einsum(
        "bld,blf->df", mixed_in, grad_shared_up_part, preferred_element_type=jnp.float32
    )
    grad_mixed = (
        grad_mixed.reshape(seq_count, seg_rows, model_width)
        + jnp.einsum(
            "blf,df->bld",
            grad_shared_gate_part,
            shared_gate_full,
            preferred_element_type=jnp.float32,
        )
        + jnp.einsum(
            "blf,df->bld", grad_shared_up_part, shared_up_full, preferred_element_type=jnp.float32
        )
    )
    _, norm_two_pull = jax.vjp(norm_apply, middle, gain_two)
    grad_middle_part, grad_gain_two = norm_two_pull(grad_mixed)
    grad_middle = grad_result.reshape(seq_count, seg_rows, model_width) + grad_middle_part
    grad_proj = grad_middle.astype(jnp.bfloat16)
    grad_output_matrix = jnp.einsum(
        "bld,ble->de", attended_tokens, grad_proj, preferred_element_type=jnp.float32
    )
    grad_attended = jnp.einsum(
        "ble,de->bld", grad_proj, output_full, preferred_element_type=jnp.float32
    ).astype(jnp.bfloat16)
    grad_attended_heads = to_heads(grad_attended[None])[0].reshape(head_shape)
    delta_rows = jnp.einsum(
        "bqhd,bqhd->bhq",
        grad_attended_heads,
        attended_flat.reshape(head_shape),
        preferred_element_type=jnp.float32,
    )

    def key_step(grad_query, offset):
        key_part, value_part, key_rows = key_slices(offset)
        part_query, part_key, part_value = score_grads(
            query_rot,
            own_rows,
            key_part,
            value_part,
            key_rows,
            grad_attended_heads,
            log_total,
            delta_rows,
            score_scale,
        )
        flat_shape = (seq_count, block_rows, flat_width)
        return (
            grad_query + part_query,
            (part_key.reshape(flat_shape), part_value.reshape(flat_shape)),
        )

    grad_query_rot, (key_terms, value_terms) = lax.scan(
        key_step, jnp.zeros(head_shape, jnp.float32), offsets
    )
    own_keys, own_values = (
        lax.psum_scatter(
            key_terms.astype(jnp.bfloat16), "fs", scatter_dimension=0, tiled=True
        ).astype(jnp.float32),
        lax.psum_scatter(
            value_terms.astype(jnp.bfloat16), "fs", scatter_dimension=0, tiled=True
        ).astype(jnp.float32),
    )
    grad_key_rot = jnp.moveaxis(own_keys, 0, 1).reshape(head_shape)
    grad_value = jnp.moveaxis(own_values, 0, 1).reshape(head_shape)
    _, rope_pull = jax.vjp(rotate_own, jnp.zeros(head_shape, jnp.float32))
    (grad_query_raw,) = rope_pull(grad_query_rot)
    (grad_key_raw,) = rope_pull(grad_key_rot)
    stacked_grads = (
        jnp.stack([grad_query_raw, grad_key_raw, grad_value])
        .astype(jnp.bfloat16)
        .reshape(3, seq_count, quarter_rows, flat_width)
    )
    token_grads = to_tokens(stacked_grads)
    grad_query_matrix = jnp.einsum(
        "bld,ble->de", normed, token_grads[0], preferred_element_type=jnp.float32
    )
    grad_key_matrix = jnp.einsum(
        "bld,ble->de", normed, token_grads[1], preferred_element_type=jnp.float32
    )
    grad_value_matrix = jnp.einsum(
        "bld,ble->de", normed, token_grads[2], preferred_element_type=jnp.float32
    )
    grad_normed = (
        jnp.einsum("ble,de->bld", token_grads[0], query_full, preferred_element_type=jnp.float32)
        + jnp.einsum("ble,de->bld", token_grads[1], key_full, preferred_element_type=jnp.float32)
        + jnp.einsum("ble,de->bld", token_grads[2], value_full, preferred_element_type=jnp.float32)
    )
    _, norm_one_pull = jax.vjp(norm_apply, residual, gain_one)
    grad_residual_part, grad_gain_one = norm_one_pull(grad_normed)
    grad_tokens = grad_middle + grad_residual_part
    (
        part_gain_one,
        part_query,
        part_key,
        part_value,
        part_output,
        part_gain_two,
        part_router,
        part_shared_gate,
        part_shared_up,
        part_shared_down,
    ) = (
        lax.psum_scatter(
            grad_gain_one.astype(jnp.bfloat16), ("sp", "fs"), scatter_dimension=0, tiled=True
        ).astype(jnp.float32),
        lax.psum_scatter(
            grad_query_matrix.astype(jnp.bfloat16), ("sp", "fs"), scatter_dimension=0, tiled=True
        ).astype(jnp.float32),
        lax.psum_scatter(
            grad_key_matrix.astype(jnp.bfloat16), ("sp", "fs"), scatter_dimension=0, tiled=True
        ).astype(jnp.float32),
        lax.psum_scatter(
            grad_value_matrix.astype(jnp.bfloat16), ("sp", "fs"), scatter_dimension=0, tiled=True
        ).astype(jnp.float32),
        lax.psum_scatter(
            grad_output_matrix.astype(jnp.bfloat16), ("sp", "fs"), scatter_dimension=0, tiled=True
        ).astype(jnp.float32),
        lax.psum_scatter(
            grad_gain_two.astype(jnp.bfloat16), ("sp", "fs"), scatter_dimension=0, tiled=True
        ).astype(jnp.float32),
        lax.psum_scatter(
            grad_router.astype(jnp.bfloat16), ("sp", "fs"), scatter_dimension=0, tiled=True
        ).astype(jnp.float32),
        lax.psum_scatter(
            grad_shared_gate.astype(jnp.bfloat16), ("sp", "fs"), scatter_dimension=0, tiled=True
        ).astype(jnp.float32),
        lax.psum_scatter(
            grad_shared_up.astype(jnp.bfloat16), ("sp", "fs"), scatter_dimension=0, tiled=True
        ).astype(jnp.float32),
        lax.psum_scatter(
            grad_shared_down.astype(jnp.bfloat16), ("sp", "fs"), scatter_dimension=0, tiled=True
        ).astype(jnp.float32),
    )
    own_gate, own_up, own_down = (
        lax.psum_scatter(
            grad_expert_gate.astype(jnp.bfloat16), "sp", scatter_dimension=1, tiled=True
        ).astype(jnp.float32),
        lax.psum_scatter(
            grad_expert_up.astype(jnp.bfloat16), "sp", scatter_dimension=1, tiled=True
        ).astype(jnp.float32),
        lax.psum_scatter(
            grad_expert_down.astype(jnp.bfloat16), "sp", scatter_dimension=1, tiled=True
        ).astype(jnp.float32),
    )
    (
        sum_gain_one,
        sum_query,
        sum_key,
        sum_value,
        sum_output,
        sum_gain_two,
        sum_router,
        sum_shared_gate,
        sum_shared_up,
        sum_shared_down,
        sum_gate,
        sum_up,
        sum_down,
    ) = (
        lax.psum(part_gain_one.astype(jnp.bfloat16), "dp").astype(jnp.float32),
        lax.psum(part_query.astype(jnp.bfloat16), "dp").astype(jnp.float32),
        lax.psum(part_key.astype(jnp.bfloat16), "dp").astype(jnp.float32),
        lax.psum(part_value.astype(jnp.bfloat16), "dp").astype(jnp.float32),
        lax.psum(part_output.astype(jnp.bfloat16), "dp").astype(jnp.float32),
        lax.psum(part_gain_two.astype(jnp.bfloat16), "dp").astype(jnp.float32),
        lax.psum(part_router.astype(jnp.bfloat16), "dp").astype(jnp.float32),
        lax.psum(part_shared_gate.astype(jnp.bfloat16), "dp").astype(jnp.float32),
        lax.psum(part_shared_up.astype(jnp.bfloat16), "dp").astype(jnp.float32),
        lax.psum(part_shared_down.astype(jnp.bfloat16), "dp").astype(jnp.float32),
        lax.psum(own_gate.astype(jnp.bfloat16), "dp").astype(jnp.float32),
        lax.psum(own_up.astype(jnp.bfloat16), "dp").astype(jnp.float32),
        lax.psum(own_down.astype(jnp.bfloat16), "dp").astype(jnp.float32),
    )
    return (
        output,
        grad_tokens,
        sum_gain_one,
        sum_query,
        sum_key,
        sum_value,
        sum_output,
        sum_gain_two,
        sum_router,
        sum_shared_gate,
        sum_shared_up,
        sum_shared_down,
        sum_gate,
        sum_up,
        sum_down,
    )


def solution(mesh):
    placed = (
        P("dp", ("sp", "fs"), None),
        P("dp", ("sp", "fs"), None),
        P("dp", ("sp", "fs")),
        P(("sp", "fs")),
        P(("sp", "fs"), None),
        P(("sp", "fs"), None),
        P(("sp", "fs"), None),
        P(("sp", "fs"), None),
        P(("sp", "fs")),
        P(("sp", "fs"), None),
        P(("sp", "fs"), None),
        P(("sp", "fs"), None),
        P(("sp", "fs"), None),
        P("fs", "sp", None),
        P("fs", "sp", None),
        P("fs", "sp", None),
        P("dp", ("sp", "fs"), None),
    )
    return jax.shard_map(
        per_device,
        mesh=mesh,
        in_specs=placed,
        out_specs=(
            P("dp", ("sp", "fs"), None),
            P("dp", ("sp", "fs"), None),
            P(("sp", "fs")),
            P(("sp", "fs"), None),
            P(("sp", "fs"), None),
            P(("sp", "fs"), None),
            P(("sp", "fs"), None),
            P(("sp", "fs")),
            P(("sp", "fs"), None),
            P(("sp", "fs"), None),
            P(("sp", "fs"), None),
            P(("sp", "fs"), None),
            P("fs", "sp", None),
            P("fs", "sp", None),
            P("fs", "sp", None),
        ),
        check_vma=False,
    )
```

profile of v0, /device:TPU:12, one launch (start us, length us, event | category | flops | bytes accessed | tf_op | source)
XLA Modules:
  0.0 2233.1 jit_solution(357948515237507348)
XLA Ops:
  13.1 30.5 %all-reduce.11 = (bf16[768]{0:T(1024)(128)(2,1)S(1)}, bf16[768]{0:T(1024)(128)(2,1)S(1)}) all-reduce(bf16[768]{0:T(1024)(128)(2,1)S(1)} %dynamic-update-slice, bf16[768]{0:T(1024)(128)(2,1)S(1)} %dynamic-update-slice.1), channel_id=1, replica_groups=mesh['dp'=2,'sp'=4,'fs'=4] {'sp','fs'}, use_global_device_ids=true, to_apply=%add.6 | all-reduce | flops 1536 | bytes 6144
  51.1 37.3 %all-gather.16.cloned.1.call-done = bf16[768,768]{1,0:T(8,128)(2,1)} async-done(((bf16[48,768]{1,0:T(8,128)(2,1)}), bf16[768,768]{1,0:T(8,128)(2,1)}) %all-gather.16.cloned.1.call-update) | async-done | bytes 1179664 | tf_op jit(solution)/shard_map/all_gather | solution.py:151
  90.5 37.5 %all-gather.18.cloned.1.call-done = bf16[768,768]{1,0:T(8,128)(2,1)} async-done(((bf16[48,768]{1,0:T(8,128)(2,1)}), bf16[768,768]{1,0:T(8,128)(2,1)}) %all-gather.18.cloned.1.call-update) | async-done | bytes 1179664 | tf_op jit(solution)/shard_map/all_gather | solution.py:152
  189.6 32.0 %all-gather = bf16[16,48,16]{1,2,0:T(8,128)(2,1)S(1)} all-gather(bf16[1,48,16]{1,2,0:T(8,128)(2,1)S(1)} %bitcast.371), channel_id=1, replica_groups=mesh['dp'=2,'sp'=4,'fs'=4] {'sp','fs'}, dimensions={0}, use_global_device_ids=true | all-gather | bytes 26112 | tf_op jit(solution)/shard_map/all_gather | solution.py:155
  246.8 64.2 %all-gather.22.cloned.1.call-done = bf16[4,2048,192]{1,2,0:T(8,128)(2,1)} async-done(((bf16[4,512,192]{1,2,0:T(8,128)(2,1)}), bf16[4,2048,192]{1,2,0:T(8,128)(2,1)}) %all-gather.22.cloned.1.call-update) | async-done | bytes 3145744 | tf_op jit(solution)/shard_map/all_gather | solution.py:194
  311.1 103.4 %while.36 = (s32[]{:T(128)}, f32[4,3,512]{2,1,0:T(4,128)S(1)}, f32[4,3,512]{2,1,0:T(4,128)S(1)}, f32[4,3,512,64]{2,3,1,0:T(8,128)}, s32[4]{0:T(128)S(1)}, /*inde...) while((s32[]{:T(128)}, f32[4,3,512]{2,1,0:T(4,128)S(1)}, ...), condition=%wide.region_4.5_spmd.clone, body=%wide.region_1.4_spmd.clone.sunk | while | flops 847717376 | bytes 98181328 | solution.py:235
  565.8 53.3 %all-gather.34.cloned.1.call-done = bf16[4,768,2048]{2,1,0:T(8,128)(2,1)} async-done(((bf16[4,192,2048]{2,1,0:T(8,128)(2,1)}), bf16[4,768,2048]{2,1,0:T(8,128)(2,1)}) %all-gather.34.cloned.1.call-update) | async-done | bytes 12582928 | tf_op jit(solution)/shard_map/all_gather | solution.py:162
  630.3 72.6 %all-gather.36.cloned.1.call-done = bf16[4,768,2048]{2,1,0:T(8,128)(2,1)} async-done(((bf16[4,192,2048]{2,1,0:T(8,128)(2,1)}), bf16[4,768,2048]{2,1,0:T(8,128)(2,1)}) %all-gather.36.cloned.1.call-update) | async-done | bytes 12582928 | tf_op jit(solution)/shard_map/all_gather | solution.py:163
  880.1 135.0 %while.37 = (s32[]{:T(128)}, f32[4,512,3,64]{1,3,2,0:T(8,128)}, bf16[4,4,512,192]{2,3,1,0:T(8,128)(2,1)}, bf16[4,4,512,192]{2,3,1,0:T(8,128)(2,1)}, s32[4]{0:T(1...) while((s32[]{:T(128)}, f32[4,512,3,64]{1,3,2,0:T(8,128)}, ...), condition=%wide.region_24.25_spmd.clone, body=%wide.region_23.24_spmd.clone.sunk | while | flops 2048961536 | bytes 124339096 | solution.py:410
  1030.9 45.4 %reduce-scatter.16.cloned.1.call-done = bf16[1,4,512,192]{2,3,1,0:T(8,128)(2,1)} async-done(((bf16[4,4,512,192]{2,3,1,0:T(8,128)(2,1)}), bf16[1,4,512,192]{2,3,1,0:T(8,128)(2,1)}) %reduce-scatter.16.cloned.1.call-update) | async-done | bytes 786448 | tf_op jit(solution)/shard_map/reduce_scatter | solution.py:414
  1079.3 59.5 %reduce-scatter.18.cloned.1.call-done = bf16[1,4,512,192]{2,3,1,0:T(8,128)(2,1)} async-done(((bf16[4,4,512,192]{2,3,1,0:T(8,128)(2,1)}), bf16[1,4,512,192]{2,3,1,0:T(8,128)(2,1)}) %reduce-scatter.18.cloned.1.call-update) | async-done | bytes 786448 | tf_op jit(solution)/shard_map/reduce_scatter | solution.py:417
  1151.2 41.9 %all-to-all-done.7 = bf16[3,4,512,192]{3,1,0,2:T(4,128)(2,1)} async-done(((bf16[3,4,512,192]{3,1,0,2:T(4,128)(2,1)}), bf16[3,4,512,192]{3,1,0,2:T(4,128)(2,1)}, u32[]{:S(2)}, u32[]{:S(2)}) %all-to-all-start.7) | async-done | bytes 2359328 | tf_op jit(solution)/shard_map/all_to_all | solution.py:62
  1253.1 33.8 %reduce-scatter.30.cloned.1.call-done = bf16[48,2048]{1,0:T(8,128)(2,1)} async-done(((bf16[768,2048]{1,0:T(8,128)(2,1)}), bf16[48,2048]{1,0:T(8,128)(2,1)}) %reduce-scatter.30.cloned.1.call-update) | async-done | bytes 196624 | tf_op jit(solution)/shard_map/reduce_scatter | solution.py:485
  1286.9 68.8 %reduce-scatter.32.cloned.1.call-done = bf16[128,768]{1,0:T(8,128)(2,1)} async-done(((bf16[2048,768]{1,0:T(8,128)(2,1)}), bf16[128,768]{1,0:T(8,128)(2,1)}) %reduce-scatter.32.cloned.1.call-update) | async-done | bytes 196624 | tf_op jit(solution)/shard_map/reduce_scatter | solution.py:488
  1355.7 60.7 %reduce-scatter.26.cloned.1.call-done = bf16[48,768]{1,0:T(8,128)(2,1)} async-done(((bf16[768,768]{1,0:T(8,128)(2,1)}), bf16[48,768]{1,0:T(8,128)(2,1)}) %reduce-scatter.26.cloned.1.call-update) | async-done | bytes 73744 | tf_op jit(solution)/shard_map/reduce_scatter | solution.py:473
  1416.4 61.3 %reduce-scatter.20.cloned.1.call-done = bf16[48,768]{1,0:T(8,128)(2,1)} async-done(((bf16[768,768]{1,0:T(8,128)(2,1)}), bf16[48,768]{1,0:T(8,128)(2,1)}) %reduce-scatter.20.cloned.1.call-update) | async-done | bytes 73744 | tf_op jit(solution)/shard_map/reduce_scatter | solution.py:464
  1477.7 61.2 %reduce-scatter.22.cloned.1.call-done = bf16[48,768]{1,0:T(8,128)(2,1)} async-done(((bf16[768,768]{1,0:T(8,128)(2,1)}), bf16[48,768]{1,0:T(8,128)(2,1)}) %reduce-scatter.22.cloned.1.call-update) | async-done | bytes 73744 | tf_op jit(solution)/shard_map/reduce_scatter | solution.py:467
  1538.8 60.7 %reduce-scatter.24.cloned.1.call-done = bf16[48,768]{1,0:T(8,128)(2,1)} async-done(((bf16[768,768]{1,0:T(8,128)(2,1)}), bf16[48,768]{1,0:T(8,128)(2,1)}) %reduce-scatter.24.cloned.1.call-update) | async-done | bytes 73744 | tf_op jit(solution)/shard_map/reduce_scatter | solution.py:470
  1599.6 99.8 %reduce-scatter.38.cloned.1.call-done = bf16[4,192,2048]{2,1,0:T(8,128)(2,1)} async-done(((bf16[4,768,2048]{2,1,0:T(8,128)(2,1)}), bf16[4,192,2048]{2,1,0:T(8,128)(2,1)}) %reduce-scatter.38.cloned.1.call-update) | async-done | bytes 3145744 | tf_op jit(solution)/shard_map/reduce_scatter | solution.py:499
  1699.4 101.7 %reduce-scatter.34.cloned.1.call-done = bf16[4,192,2048]{2,1,0:T(8,128)(2,1)} async-done(((bf16[4,768,2048]{2,1,0:T(8,128)(2,1)}), bf16[4,192,2048]{2,1,0:T(8,128)(2,1)}) %reduce-scatter.34.cloned.1.call-update) | async-done | bytes 3145744 | tf_op jit(solution)/shard_map/reduce_scatter | solution.py:493
  1801.1 101.6 %reduce-scatter.36.cloned.1.call-done = bf16[4,192,2048]{2,1,0:T(8,128)(2,1)} async-done(((bf16[4,768,2048]{2,1,0:T(8,128)(2,1)}), bf16[4,192,2048]{2,1,0:T(8,128)(2,1)}) %reduce-scatter.36.cloned.1.call-update) | async-done | bytes 3145744 | tf_op jit(solution)/shard_map/reduce_scatter | solution.py:496
  1909.7 51.6 %reduce-scatter.40.cloned.1.call-done = bf16[48,16]{1,0:T(8,128)(2,1)} async-done(((bf16[768,16]{1,0:T(8,128)(2,1)}), bf16[48,16]{1,0:T(8,128)(2,1)}) %reduce-scatter.40.cloned.1.call-update) | async-done | bytes 1552
  1969.4 30.5 %all-reduce.10 = (bf16[768]{0:T(1024)(128)(2,1)S(1)}, bf16[768]{0:T(1024)(128)(2,1)S(1)}) all-reduce(bf16[768]{0:T(1024)(128)(2,1)S(1)} %get-tuple-element.456, bf16[768]{0:T(1024)(128)(2,1)S(1)} %copy-done.64), channel_id=4, replica_groups=mesh['dp'=2,'sp'=4,'fs'=4] {'sp','fs'}, use_global_device_ids=true, to_apply=%region_29.30.clone | all-reduce | flops 1536 | bytes 6144
  2009.7 198.6 %all-reduce.16.cloned.1.call-done = (bf16[48,768]{1,0:T(8,128)(2,1)}, bf16[48,768]{1,0:T(8,128)(2,1)}, bf16[48,768]{1,0:T(8,128)(2,1)}, bf16[48,768]{1,0:T(8,128...) async-done(((bf16[48,768]{1,0:T(8,128)(2,1)}, ...) | async-done | bytes 10321936 | tf_op jit(solution)/shard_map/psum | solution.py:519
  (521 shorter events, 794.5 us)
Async XLA Ops:
  8.7 119.4 %all-gather.18.cloned.1.call-start = ((), (), s32[]{:S(2)}) async-start(), calls=%async_computation.23 | async-start | bytes 1253376 | tf_op jit(solution)/shard_map/all_gather | solution.py:152
  142.7 104.1 %all-gather.20.cloned.1.call-start = ((), (), s32[]{:S(2)}) async-start(), calls=%async_computation.24 | async-start | bytes 3932160 | tf_op jit(solution)/shard_map/all_gather | solution.py:193
  183.5 127.6 %all-gather.22.cloned.1.call-start = ((), (), s32[]{:S(2)}) async-start(), calls=%async_computation.25 | async-start | bytes 3932160 | tf_op jit(solution)/shard_map/all_gather | solution.py:194
  185.4 264.3 %all-gather.24.cloned.1.call-start = ((), (), s32[]{:S(2)}) async-start(), calls=%async_computation.26 | async-start | bytes 1253376 | tf_op jit(solution)/shard_map/all_gather | solution.py:153
  185.9 332.1 %all-gather.30.cloned.1.call-start = ((), (), s32[]{:S(2)}) async-start(), calls=%async_computation.29 | async-start | bytes 3342336 | tf_op jit(solution)/shard_map/all_gather | solution.py:158
  186.7 337.3 %all-gather.28.cloned.1.call-start = ((), (), s32[]{:S(2)}) async-start(), calls=%async_computation.28 | async-start | bytes 3342336 | tf_op jit(solution)/shard_map/all_gather | solution.py:157
  187.4 366.9 %all-gather.32.cloned.1.call-start = ((), (), s32[]{:S(2)}) async-start(), calls=%async_computation.30 | async-start | bytes 15728640 | tf_op jit(solution)/shard_map/all_gather | solution.py:161
  188.2 431.0 %all-gather.34.cloned.1.call-start = ((), (), s32[]{:S(2)}) async-start(), calls=%async_computation.31 | async-start | bytes 15728640 | tf_op jit(solution)/shard_map/all_gather | solution.py:162
  188.8 514.1 %all-gather.36.cloned.1.call-start = ((), (), s32[]{:S(2)}) async-start(), calls=%async_computation.32 | async-start | bytes 15728640 | tf_op jit(solution)/shard_map/all_gather | solution.py:163
  515.1 275.7 %all-gather.26.cloned.1.call-start = ((), (), s32[]{:S(2)}) async-start(), calls=%async_computation.27 | async-start | bytes 3342336 | tf_op jit(solution)/shard_map/all_gather | solution.py:156
  866.7 209.6 %reduce-scatter.16.cloned.1.call-start = ((), (), s32[]{:S(2)}) async-start(), calls=%async_computation.33 | async-start | bytes 3932160 | tf_op jit(solution)/shard_map/reduce_scatter | solution.py:414
  1015.1 123.7 %reduce-scatter.18.cloned.1.call-start = ((), (), s32[]{:S(2)}) async-start(), calls=%async_computation.34 | async-start | bytes 3932160 | tf_op jit(solution)/shard_map/reduce_scatter | solution.py:417
  1015.7 237.4 %reduce-scatter.28.cloned.1.call-start = ((), (), s32[]{:S(2)}) async-start(), calls=%async_computation.39 | async-start | bytes 3342336 | tf_op jit(solution)/shard_map/reduce_scatter | solution.py:482
  1020.5 266.4 %reduce-scatter.30.cloned.1.call-start = ((), (), s32[]{:S(2)}) async-start(), calls=%async_computation.40 | async-start | bytes 3342336 | tf_op jit(solution)/shard_map/reduce_scatter | solution.py:485
  1025.5 330.2 %reduce-scatter.32.cloned.1.call-start = ((), (), s32[]{:S(2)}) async-start(), calls=%async_computation.41 | async-start | bytes 3342336 | tf_op jit(solution)/shard_map/reduce_scatter | solution.py:488
  1149.3 267.1 %reduce-scatter.26.cloned.1.call-start = ((), (), s32[]{:S(2)}) async-start(), calls=%async_computation.38 | async-start | bytes 1253376 | tf_op jit(solution)/shard_map/reduce_scatter | solution.py:473
  1151.1 326.6 %reduce-scatter.20.cloned.1.call-start = ((), (), s32[]{:S(2)}) async-start(), calls=%async_computation.35 | async-start | bytes 1253376 | tf_op jit(solution)/shard_map/reduce_scatter | solution.py:464
  1205.7 333.1 %reduce-scatter.22.cloned.1.call-start = ((), (), s32[]{:S(2)}) async-start(), calls=%async_computation.36 | async-start | bytes 1253376 | tf_op jit(solution)/shard_map/reduce_scatter | solution.py:467
  1208.8 390.8 %reduce-scatter.24.cloned.1.call-start = ((), (), s32[]{:S(2)}) async-start(), calls=%async_computation.37 | async-start | bytes 1253376 | tf_op jit(solution)/shard_map/reduce_scatter | solution.py:470
  1212.2 487.2 %reduce-scatter.38.cloned.1.call-start = ((), (), s32[]{:S(2)}) async-start(), calls=%async_computation.44 | async-start | bytes 15728640 | tf_op jit(solution)/shard_map/reduce_scatter | solution.py:499
  1224.7 576.4 %reduce-scatter.34.cloned.1.call-start = ((), (), s32[]{:S(2)}) async-start(), calls=%async_computation.42 | async-start | bytes 15728640 | tf_op jit(solution)/shard_map/reduce_scatter | solution.py:493
  1238.3 664.3 %reduce-scatter.36.cloned.1.call-start = ((), (), s32[]{:S(2)}) async-start(), calls=%async_computation.43 | async-start | bytes 15728640 | tf_op jit(solution)/shard_map/reduce_scatter | solution.py:496
  1250.6 710.7 %reduce-scatter.40.cloned.1.call-start = ((), (), s32[]{:S(2)}) async-start(), calls=%async_computation.45 | async-start | bytes 208896
  1252.7 955.6 %all-reduce.16.cloned.1.call-start = ((), (), s32[]{:S(2)}) async-start(), calls=%async_computation.46 | async-start | bytes 20643840 | tf_op jit(solution)/shard_map/psum | solution.py:519
  (106 other events, 2118.9 us)
Sparse Core Ops, SparseCore 0:
  10.3 38.3 all-gather.13
  183.6 63.1 all-gather.19
  248.8 62.1 all-gather.21
  313.2 37.8 all-gather.23
  353.4 45.0 all-gather.29
  400.8 52.6 all-gather.27
  455.1 80.4 all-gather.31
  537.0 82.0 all-gather.33
  620.7 82.0 all-gather.35
  705.0 52.0 all-gather.25
  1015.2 61.0 reduce-scatter.15
  1078.5 60.2 reduce-scatter.17
  1142.5 75.4 reduce-scatter.27
  1221.6 65.1 reduce-scatter.29
  1290.5 65.1 reduce-scatter.31
  1359.2 57.2 reduce-scatter.25
  1420.6 57.0 reduce-scatter.19
  1481.7 57.0 reduce-scatter.21
  1542.5 57.0 reduce-scatter.23
  1602.2 97.1 reduce-scatter.37
  1702.0 99.0 reduce-scatter.33
  1803.6 99.0 reduce-scatter.35
  1906.7 54.5 reduce-scatter.39
  1964.6 243.7 all-reduce.15
  (2 shorter events, 74.5 us)
where the time goes:
time: 2250 us; the launch traced here: 2230 us
  waiting for transfers between devices  1450 us (64%)
  matrix products  316 us (14%)
  local copies, waits for them, and re-layouts  181 us (8%)
  other arithmetic  99.5 us (4%)
  blocking collectives  98.1 us (4%)
  starting transfers between devices  48.8 us (2%)
    psum x1, waiting for transfers between devices, per_device(): lax.psum(part_query.astype(jnp.bfloat16), 'dp').astype(jnp.float32)  199 us
    reduce_scatter x1, waiting for transfers between devices, per_device(): lax.psum_scatter(grad_expert_gate.astype(jnp.bfloat16), 'sp', scatter_dim...  102 us
    reduce_scatter x1, waiting for transfers between devices, per_device(): lax.psum_scatter(grad_expert_up.astype(jnp.bfloat16), 'sp', scatter_dimen...  102 us
    reduce_scatter x1, waiting for transfers between devices, per_device(): lax.psum_scatter(grad_expert_down.astype(jnp.bfloat16), 'sp', scatter_dim...  99.8 us
    all_gather x1, waiting for transfers between devices, per_device(): lax.all_gather(expert_down, 'sp', axis=1, tiled=True)  72.6 us
    reduce_scatter x1, waiting for transfers between devices, per_device(): lax.psum_scatter(grad_shared_down.astype(jnp.bfloat16), ('sp', 'fs'), sca...  68.8 us
    all_gather x1, waiting for transfers between devices, per_device(): lax.all_gather(value_flat, 'fs', axis=1, tiled=True)  64.2 us
    reduce_scatter x1, waiting for transfers between devices, per_device(): lax.psum_scatter(grad_query_matrix.astype(jnp.bfloat16), ('sp', 'fs'), sc...  61.3 us
  transfers between devices with their start and end apart: 34, of which 27 were waited for; matrix products, arithmetic and copies ran while one was open for 17% of the time, Pallas kernels for 0%

commit v1 on v0

--- a/solution.py
+++ b/solution.py
@@ -1,8 +1,11 @@
+import functools
 import math
 
 import jax
 import jax.numpy as jnp
 from jax import lax
+from jax.experimental import pallas as pl
+from jax.experimental.pallas import tpu as pltpu
 from jax.sharding import PartitionSpec as P
 
 HEADS = 12
@@ -548,6 +551,581 @@
     )
 
 
+BF16 = jnp.bfloat16
+F32 = jnp.float32
+
+
+def dot32(left, right):
+    return jnp.dot(left, right, preferred_element_type=F32)
+
+
+def dot_nt(left, right):
+    return lax.dot_general(left, right, (((1,), (1,)), ((), ())), preferred_element_type=F32)
+
+
+def turn(values, cosine, sine):
+    half = values.shape[0] // 2
+    front, back = values[:half], values[half:]
+    return jnp.concatenate([front * cosine - back * sine, back * cosine + front * sine], axis=0)
+
+
+def turn_back(values, cosine, sine):
+    half = values.shape[0] // 2
+    front, back = values[:half], values[half:]
+    return jnp.concatenate([front * cosine + back * sine, back * cosine - front * sine], axis=0)
+
+
+def causal(block):
+    keys = lax.broadcasted_iota(jnp.int32, (block, block), 0)
+    queries = lax.broadcasted_iota(jnp.int32, (block, block), 1)
+    return keys <= queries
+
+
+def attend_kernel(block, scale, q_ref, k_ref, v_ref, cos_ref, sin_ref, o_ref, lse_ref, k_rot):
+    place = pl.program_id(1)
+
+    @pl.when(place == 0)
+    def _():
+        rotated = turn(k_ref[...].astype(F32), cos_ref[...], sin_ref[...])
+        k_rot[...] = rotated.T.astype(BF16)
+
+    start = pl.multiple_of(place * block, block)
+    query = turn(
+        q_ref[...].astype(F32), cos_ref[:, pl.ds(start, block)], sin_ref[:, pl.ds(start, block)]
+    ).astype(BF16)
+
+    def scores_at(offset):
+        return dot32(k_rot[pl.ds(offset, block), :], query) * scale
+
+    def weighted(offset, weights):
+        return dot32(v_ref[:, pl.ds(offset, block)], weights.astype(BF16))
+
+    scores = jnp.where(causal(block), scores_at(start), MASKED)
+    first_max = jnp.max(scores, axis=0, keepdims=True)
+    weights = jnp.exp(scores - first_max)
+    first_sum = jnp.sum(weights, axis=0, keepdims=True)
+
+    def step(index, carried):
+        running_max, running_sum, running_acc = carried
+        offset = pl.multiple_of(index * block, block)
+        part = scores_at(offset)
+        new_max = jnp.maximum(running_max, jnp.max(part, axis=0, keepdims=True))
+        part = jnp.exp(part - new_max)
+        factor = jnp.exp(running_max - new_max)
+        return (
+            new_max,
+            running_sum * factor + jnp.sum(part, axis=0, keepdims=True),
+            running_acc * factor + weighted(offset, part),
+        )
+
+    final_max, final_sum, final_acc = lax.fori_loop(
+        0, place, step, (first_max, first_sum, weighted(start, weights))
+    )
+    o_ref[...] = (final_acc / final_sum).astype(BF16)
+    lse_ref[0] = final_max + jnp.log(final_sum)
+
+
+def attend_grad_kernel(
+    block,
+    scale,
+    q_ref,
+    k_ref,
+    v_ref,
+    cos_ref,
+    sin_ref,
+    o_ref,
+    lse_ref,
+    go_ref,
+    dq_ref,
+    dk_ref,
+    dv_ref,
+    q_feat,
+    q_rows,
+    k_feat,
+    go_rows,
+    delta,
+    dq_acc,
+):
+    place = pl.program_id(1)
+    count = pl.num_programs(1)
+
+    @pl.when(place == 0)
+    def _():
+        rotated = turn(q_ref[...].astype(F32), cos_ref[...], sin_ref[...])
+        q_feat[...] = rotated.astype(BF16)
+        q_rows[...] = rotated.T.astype(BF16)
+        k_feat[...] = turn(k_ref[...].astype(F32), cos_ref[...], sin_ref[...]).astype(BF16)
+        grad = go_ref[...].astype(F32)
+        go_rows[...] = grad.T.astype(BF16)
+        delta[...] = jnp.sum(grad * o_ref[...].astype(F32), axis=0, keepdims=True)
+        dq_acc[...] = jnp.zeros_like(dq_acc)
+
+    start = pl.multiple_of(place * block, block)
+    key_feat = k_feat[:, pl.ds(start, block)]
+    key_rows = key_feat.astype(F32).T.astype(BF16)
+    value_rows = v_ref[:, pl.ds(start, block)].astype(F32).T.astype(BF16)
+
+    def terms(offset, masked):
+        scores = dot32(key_rows, q_feat[:, pl.ds(offset, block)]) * scale
+        weights = jnp.exp(scores - lse_ref[0, :, pl.ds(offset, block)])
+        if masked:
+            weights = jnp.where(causal(block), weights, 0.0)
+        reach = dot32(value_rows, go_ref[:, pl.ds(offset, block)])
+        slopes = (weights * (reach - delta[:, pl.ds(offset, block)]) * scale).astype(BF16)
+        dq_acc[:, pl.ds(offset, block)] += dot32(key_feat, slopes)
+        part_key = dot32(slopes, q_rows[pl.ds(offset, block), :])
+        part_value = dot32(weights.astype(BF16), go_rows[pl.ds(offset, block), :])
+        return part_key, part_value
+
+    def step(index, carried):
+        part_key, part_value = terms(pl.multiple_of(index * block, block), False)
+        return carried[0] + part_key, carried[1] + part_value
+
+    grad_key, grad_value = lax.fori_loop(place + 1, count, step, terms(start, True))
+    own_cos, own_sin = cos_ref[:, pl.ds(start, block)], sin_ref[:, pl.ds(start, block)]
+    dk_ref[...] = turn_back(grad_key.T, own_cos, own_sin).astype(BF16)
+    dv_ref[...] = grad_value.T.astype(BF16)
+
+    @pl.when(place == count - 1)
+    def _():
+        dq_ref[...] = turn_back(dq_acc[...], cos_ref[...], sin_ref[...]).astype(BF16)
+
+
+def attention_block(length):
+    return math.gcd(length, 512)
+
+
+def attend(qkv, cosine, sine, heads, score_scale):
+    length = qkv.shape[1]
+    block = attention_block(length)
+    half = HEAD_DIM // 2
+    table = pl.BlockSpec((half, length), lambda h, i: (0, 0))
+    return pl.pallas_call(
+        functools.partial(attend_kernel, block, score_scale),
+        grid=(heads, length // block),
+        in_specs=[
+            pl.BlockSpec((HEAD_DIM, block), lambda h, i: (h, i)),
+            pl.BlockSpec((HEAD_DIM, length), lambda h, i: (heads + h, 0)),
+            pl.BlockSpec((HEAD_DIM, length), lambda h, i: (2 * heads + h, 0)),
+            table,
+            table,
+        ],
+        out_specs=[
+            pl.BlockSpec((HEAD_DIM, block), lambda h, i: (h, i)),
+            pl.BlockSpec((1, 1, block), lambda h, i: (h, 0, i)),
+        ],
+        out_shape=[
+            jax.ShapeDtypeStruct((heads * HEAD_DIM, length), BF16),
+            jax.ShapeDtypeStruct((heads, 1, length), F32),
+        ],
+        scratch_shapes=[pltpu.VMEM((length, HEAD_DIM), BF16)],
+        name="attend",
+    )(qkv, qkv, qkv, cosine, sine)
+
+
+def attend_grad(qkv, cosine, sine, out, lse, grad_out, heads, score_scale):
+    length = qkv.shape[1]
+    block = attention_block(length)
+    half = HEAD_DIM // 2
+    table = pl.BlockSpec((half, length), lambda h, i: (0, 0))
+
+    def whole(base):
+        return pl.BlockSpec((HEAD_DIM, length), lambda h, i: (base + h, 0))
+
+    shape = jax.ShapeDtypeStruct((heads * HEAD_DIM, length), BF16)
+    return pl.pallas_call(
+        functools.partial(attend_grad_kernel, block, score_scale),
+        grid=(heads, length // block),
+        in_specs=[
+            whole(0),
+            whole(heads),
+            whole(2 * heads),
+            table,
+            table,
+            whole(0),
+            pl.BlockSpec((1, 1, length), lambda h, i: (h, 0, 0)),
+            whole(0),
+        ],
+        out_specs=[
+            whole(0),
+            pl.BlockSpec((HEAD_DIM, block), lambda h, i: (h, i)),
+            pl.BlockSpec((HEAD_DIM, block), lambda h, i: (h, i)),
+        ],
+        out_shape=[shape, shape, shape],
+        scratch_shapes=[
+            pltpu.VMEM((HEAD_DIM, length), BF16),
+            pltpu.VMEM((length, HEAD_DIM), BF16),
+            pltpu.VMEM((HEAD_DIM, length), BF16),
+            pltpu.VMEM((length, HEAD_DIM), BF16),
+            pltpu.VMEM((1, length), F32),
+            pltpu.VMEM((HEAD_DIM, length), F32),
+        ],
+        name="attend_grad",
+    )(qkv, qkv, qkv, cosine, sine, out, lse, grad_out)
+
+
+def expert_kernel(
+    x_ref,
+    g_ref,
+    gate_ref,
+    up_ref,
+    down_ref,
+    y_ref,
+    gx_ref,
+    dgate_ref,
+    dup_ref,
+    ddown_ref,
+    x_feat,
+    g_feat,
+    y_acc,
+    gx_acc,
+):
+    place = pl.program_id(0)
+
+    @pl.when(place == 0)
+    def _():
+        x_feat[...] = x_ref[...].T
+        g_feat[...] = g_ref[...].T
+        y_acc[...] = jnp.zeros_like(y_acc)
+        gx_acc[...] = jnp.zeros_like(gx_acc)
+
+    gate_val = dot32(x_ref[...], gate_ref[...])
+    up_val = dot32(x_ref[...], up_ref[...])
+    sigmoid = jax.nn.sigmoid(gate_val)
+    swished = gate_val * sigmoid
+    hidden = (swished * up_val).astype(BF16)
+    grad_hidden = dot32(g_ref[...], down_ref[...])
+    slope = sigmoid * (1.0 + gate_val * (1.0 - sigmoid))
+    gate_part = (grad_hidden * up_val * slope).astype(BF16)
+    up_part = (grad_hidden * swished).astype(BF16)
+    y_acc[...] += dot_nt(hidden, down_ref[...])
+    gx_acc[...] += dot_nt(gate_part, gate_ref[...]) + dot_nt(up_part, up_ref[...])
+    ddown_ref[...] = dot32(g_feat[...], hidden).astype(BF16)
+    dgate_ref[...] = dot32(x_feat[...], gate_part).astype(BF16)
+    dup_ref[...] = dot32(x_feat[...], up_part).astype(BF16)
+
+    @pl.when(place == pl.num_programs(0) - 1)
+    def _():
+        y_ref[...] = y_acc[...].astype(BF16)
+        gx_ref[...] = gx_acc[...].astype(BF16)
+
+
+def expert_pass(rows, grads, gate, up, down):
+    count, width = rows.shape
+    hidden = gate.shape[1]
+    tile = 256
+    whole = pl.BlockSpec((count, width), lambda i: (0, 0), pipeline_mode=pl.Buffered(1))
+    part = pl.BlockSpec((width, tile), lambda i: (0, i))
+    return pl.pallas_call(
+        expert_kernel,
+        grid=(hidden // tile,),
+        in_specs=[whole, whole, part, part, part],
+        out_specs=[whole, whole, part, part, part],
+        out_shape=[jax.ShapeDtypeStruct((count, width), BF16)] * 2
+        + [jax.ShapeDtypeStruct((width, hidden), BF16)] * 3,
+        scratch_shapes=[
+            pltpu.VMEM((width, count), BF16),
+            pltpu.VMEM((width, count), BF16),
+            pltpu.VMEM((count, width), F32),
+            pltpu.VMEM((count, width), F32),
+        ],
+        name="expert_pass",
+    )(rows, grads, gate, up, down)
+
+
+def swap_sum(value, axis):
+    if lax.axis_size(axis) == 2:
+        other = lax.ppermute(value, axis, [(0, 1), (1, 0)])
+        return value.astype(F32) + other.astype(F32)
+    return lax.psum(value, axis).astype(F32)
+
+
+def exchange(chunks):
+    return lax.all_to_all(chunks, ("sp", "fs"), split_axis=0, concat_axis=0, tiled=True)
+
+
+def per_device_split(
+    tokens,
+    expert_ids,
+    fill_order,
+    attention_gain,
+    query_weight,
+    key_weight,
+    value_weight,
+    output_weight,
+    mixer_gain,
+    router_weight,
+    shared_gate,
+    shared_up,
+    shared_down,
+    expert_gate,
+    expert_up,
+    expert_down,
+    cotangent,
+):
+    seq_count, seg_rows, width = tokens.shape
+    token_count = seq_count * seg_rows
+    fs_count = lax.axis_size("fs")
+    sp_count = lax.axis_size("sp")
+    place_count = fs_count * sp_count
+    sp_place = lax.axis_index("sp")
+    local_heads = HEADS // sp_count
+    flat_width = local_heads * HEAD_DIM
+    score_scale = HEAD_DIM ** (-0.5)
+    length = place_count * seg_rows
+    shard_rows = query_weight.shape[0]
+    qkv_width = 3 * flat_width
+    all_qkv = sp_count * qkv_width
+    shared_width = shared_gate.shape[1]
+
+    gathered = lax.all_to_all(tokens, "fs", split_axis=0, concat_axis=0, tiled=True)
+    seq_tokens = lax.all_gather(
+        gathered.reshape(fs_count * seg_rows, width), "sp", axis=0, tiled=True
+    )
+
+    grouped = jnp.stack([query_weight, key_weight, value_weight], axis=1)
+    grouped = grouped.reshape(shard_rows, 3, sp_count, flat_width)
+    grouped = jnp.transpose(grouped, (0, 2, 1, 3)).reshape(shard_rows, all_qkv)
+    small = jnp.concatenate(
+        [
+            attention_gain[:, None],
+            mixer_gain[:, None],
+            router_weight,
+            jnp.zeros((shard_rows, 128 - 2 - EXPERTS), BF16),
+        ],
+        axis=1,
+    )
+    first_pack = lax.all_gather(
+        jnp.concatenate([grouped, small], axis=1), ("sp", "fs"), axis=0, tiled=True
+    )
+    second_pack = lax.all_gather(
+        jnp.concatenate([output_weight, shared_gate, shared_up], axis=1),
+        ("sp", "fs"),
+        axis=0,
+        tiled=True,
+    )
+    shared_down_full = lax.all_gather(shared_down, ("sp", "fs"), axis=0, tiled=True)
+    gain_one = first_pack[:, all_qkv].astype(F32)
+    gain_two = first_pack[:, all_qkv + 1].astype(F32)
+    router_full = first_pack[:, all_qkv + 2 : all_qkv + 2 + EXPERTS]
+    qkv_full = first_pack[:, :all_qkv]
+    output_full = second_pack[:, :width]
+    shared_gate_full = second_pack[:, width : width + shared_width]
+    shared_up_full = second_pack[:, width + shared_width :]
+
+    def own_expert(shard):
+        moved = lax.all_to_all(shard, "sp", split_axis=0, concat_axis=0, tiled=True)
+        return moved.reshape(width, shard.shape[2])
+
+    gate_own, up_own, down_own = (
+        own_expert(expert_gate),
+        own_expert(expert_up),
+        own_expert(expert_down),
+    )
+
+    half = HEAD_DIM // 2
+    frequency = 10000.0 ** (-jnp.arange(half, dtype=F32) / half)
+    angles = frequency[:, None] * jnp.arange(length, dtype=jnp.int32).astype(F32)[None, :]
+    cosine, sine = jnp.cos(angles), jnp.sin(angles)
+
+    normed_seq = norm_apply(seq_tokens.astype(F32), gain_one).astype(BF16)
+    qkv_own = lax.dynamic_slice(first_pack, (0, sp_place * qkv_width), (width, qkv_width))
+    qkv = jnp.einsum("de,ld->el", qkv_own, normed_seq, preferred_element_type=F32).astype(BF16)
+    out_heads, lse = attend(qkv, cosine, sine, local_heads, score_scale)
+
+    def to_places(feature_rows):
+        return exchange(feature_rows.T.reshape(place_count, seg_rows, feature_rows.shape[0]))
+
+    def to_token_rows(chunks):
+        features = chunks.shape[-1]
+        chunks = chunks.reshape(sp_count, token_count, features)
+        return jnp.transpose(chunks, (1, 0, 2)).reshape(token_count, sp_count * features)
+
+    attended = to_token_rows(to_places(out_heads))
+    residual = tokens.astype(F32).reshape(token_count, width)
+    middle = residual + dot32(attended, output_full)
+    mixed_in = norm_apply(middle, gain_two).astype(BF16)
+
+    logits = dot32(mixed_in, router_full)
+    choices = expert_ids.reshape(token_count, TOPK)
+    expert_onehot = choices[:, :, None] == jnp.arange(EXPERTS, dtype=jnp.int32)[None, None, :]
+    onehot_float = expert_onehot.astype(F32)
+
+    def gate_values(raw_logits):
+        shifted = jnp.exp(raw_logits - jnp.max(raw_logits, axis=-1, keepdims=True))
+        router_probs = shifted / jnp.sum(shifted, axis=-1, keepdims=True)
+        picked = jnp.sum(router_probs[:, None, :] * onehot_float, axis=2)
+        return picked / jnp.sum(picked, axis=1, keepdims=True)
+
+    gate_weights, gate_pull = jax.vjp(gate_values, logits)
+
+    fill_rank = fill_order.reshape(token_count)
+    earlier = (fill_rank[None, :] < fill_rank[:, None]).astype(BF16)
+    per_token = jnp.sum(onehot_float, axis=1).astype(BF16)
+    counts = dot32(earlier, per_token)
+    slot_ranks = jnp.sum(counts[:, None, :] * onehot_float, axis=2).astype(jnp.int32)
+    group = EXPERTS // fs_count
+    holder = (choices % group) * fs_count + choices // group
+    slots = jnp.where(slot_ranks < CAP, holder * CAP + slot_ranks, -1)
+    slot_total = CAP * EXPERTS
+    slot_ids = jnp.arange(slot_total, dtype=jnp.int32)
+    takes_a = slot_ids[:, None] == slots[None, :, 0]
+    takes_b = slot_ids[:, None] == slots[None, :, 1]
+    taking = (takes_a | takes_b).astype(BF16)
+    gate_of_slot = jnp.sum(
+        jnp.where(takes_a, gate_weights[None, :, 0], 0.0)
+        + jnp.where(takes_b, gate_weights[None, :, 1], 0.0),
+        axis=1,
+    )
+    cot_rows = cotangent.reshape(token_count, width)
+    outgoing = dot32(taking, mixed_in).astype(BF16)
+    grad_outgoing = (gate_of_slot[:, None] * dot32(taking, cot_rows)).astype(BF16)
+    sent = jnp.concatenate(
+        [
+            outgoing.reshape(place_count, CAP, width),
+            grad_outgoing.reshape(place_count, CAP, width),
+        ],
+        axis=1,
+    )
+    arrived = exchange(sent)
+    incoming = arrived[:, :CAP].reshape(slot_total, width)
+    grad_incoming = arrived[:, CAP:].reshape(slot_total, width)
+    expert_out, grad_pair_rows, dgate, dup, ddown = expert_pass(
+        incoming, grad_incoming, gate_own, up_own, down_own
+    )
+
+    def to_owner(grad):
+        parts = grad.reshape(sp_count, width // sp_count, grad.shape[1])
+        return lax.all_to_all(parts, "sp", split_axis=0, concat_axis=0, tiled=True)
+
+    own_gate, own_up, own_down = (to_owner(dgate), to_owner(dup), to_owner(ddown))
+
+    back = exchange(
+        jnp.concatenate(
+            [
+                expert_out.reshape(place_count, CAP, width),
+                grad_pair_rows.reshape(place_count, CAP, width),
+            ],
+            axis=1,
+        )
+    )
+    returned = back[:, :CAP].reshape(slot_total, width)
+    grad_returned = back[:, CAP:].reshape(slot_total, width)
+
+    shared_gate_val = dot32(mixed_in, shared_gate_full)
+    shared_up_val = dot32(mixed_in, shared_up_full)
+    shared_hidden_full, shared_pull = jax.vjp(glu_product, shared_gate_val, shared_up_val)
+    shared_hidden = shared_hidden_full.astype(BF16)
+    shared_out = dot32(shared_hidden, shared_down_full)
+    grad_shared_hidden = dot_nt(cot_rows, shared_down_full)
+    grad_shared_gate_part, grad_shared_up_part = (
+        part.astype(BF16) for part in shared_pull(grad_shared_hidden)
+    )
+
+    def outer(left, right):
+        return lax.dot_general(left, right, (((0,), (0,)), ((), ())), preferred_element_type=F32)
+
+    grad_shared_down = outer(shared_hidden, cot_rows)
+    grad_shared_gate = outer(mixed_in, grad_shared_gate_part)
+    grad_shared_up = outer(mixed_in, grad_shared_up_part)
+    grad_mixed_shared = dot_nt(grad_shared_gate_part, shared_gate_full) + dot_nt(
+        grad_shared_up_part, shared_up_full
+    )
+
+    grad_result = cot_rows.astype(F32)
+    picked_a = dot32((slots[:, 0:1] == slot_ids[None, :]).astype(BF16), returned)
+    picked_b = dot32((slots[:, 1:2] == slot_ids[None, :]).astype(BF16), returned)
+    combined = gate_weights[:, 0:1] * picked_a + gate_weights[:, 1:2] * picked_b
+    output = (middle + shared_out + combined).astype(BF16)
+    grad_gates = jnp.stack(
+        [jnp.sum(grad_result * picked_a, axis=1), jnp.sum(grad_result * picked_b, axis=1)], axis=1
+    )
+    (grad_logits,) = gate_pull(grad_gates)
+    grad_logits = grad_logits.astype(BF16)
+    grad_router = outer(mixed_in, grad_logits)
+    grad_mixed = (
+        outer(taking, grad_returned) + dot_nt(grad_logits, router_full) + grad_mixed_shared
+    )
+    _, norm_two_pull = jax.vjp(norm_apply, middle, gain_two)
+    grad_middle_part, grad_gain_two = norm_two_pull(grad_mixed)
+    grad_middle = grad_result + grad_middle_part
+    grad_proj = grad_middle.astype(BF16)
+    grad_output_matrix = outer(attended, grad_proj)
+    grad_attended = dot_nt(grad_proj, output_full).astype(BF16)
+
+    parts = grad_attended.reshape(fs_count, seg_rows, sp_count, flat_width)
+    parts = jnp.transpose(parts, (2, 0, 1, 3)).reshape(place_count, seg_rows, flat_width)
+    grad_heads = exchange(parts).reshape(length, flat_width).T
+    dq, dk, dv = attend_grad(
+        qkv, cosine, sine, out_heads, lse, grad_heads, local_heads, score_scale
+    )
+    dqkv = jnp.concatenate([dq, dk, dv], axis=0)
+    token_grads = to_token_rows(to_places(dqkv))
+    grad_qkv_matrix = jnp.einsum("ld,el->de", normed_seq, dqkv, preferred_element_type=F32)
+    grad_normed = dot_nt(token_grads, qkv_full)
+    _, norm_one_pull = jax.vjp(norm_apply, residual, gain_one)
+    grad_residual_part, grad_gain_one = norm_one_pull(grad_normed)
+    grad_tokens = grad_middle + grad_residual_part
+
+    def column(vector, columns):
+        return jnp.pad(vector[:, None], ((0, 0), (0, columns - 1)))
+
+    dense = jnp.concatenate(
+        [
+            grad_output_matrix,
+            grad_shared_gate,
+            grad_shared_up,
+            grad_router,
+            column(grad_gain_two, 128 - EXPERTS),
+        ],
+        axis=1,
+    ).astype(BF16)
+    dense = lax.psum_scatter(dense, ("sp", "fs"), scatter_dimension=0, tiled=True)
+    own_shared_down = lax.psum_scatter(
+        grad_shared_down.astype(BF16), ("sp", "fs"), scatter_dimension=0, tiled=True
+    )
+    tail = jnp.concatenate([grad_qkv_matrix, column(grad_gain_one, 128)], axis=1).astype(BF16)
+    tail = exchange(tail.reshape(place_count, shard_rows, tail.shape[1]))
+    tail = tail.reshape(sp_count, fs_count, shard_rows, tail.shape[2]).astype(F32)
+    tail = jnp.sum(tail, axis=1).astype(BF16)
+    sum_gate, sum_up, sum_down = (
+        swap_sum(own_gate, "dp"),
+        swap_sum(own_up, "dp"),
+        swap_sum(own_down, "dp"),
+    )
+    sum_dense = swap_sum(dense, "dp")
+    sum_shared_down = swap_sum(own_shared_down, "dp")
+    sum_tail = swap_sum(tail, "dp")
+    sum_qkv = sum_tail[:, :, :qkv_width].reshape(sp_count, shard_rows, 3, flat_width)
+    sum_qkv = jnp.transpose(sum_qkv, (2, 1, 0, 3)).reshape(3, shard_rows, width)
+    sum_gain_one = jnp.sum(sum_tail[:, :, qkv_width], axis=0)
+    edge = width + 2 * shared_width
+    return (
+        output.reshape(tokens.shape),
+        grad_tokens.reshape(tokens.shape),
+        sum_gain_one,
+        sum_qkv[0],
+        sum_qkv[1],
+        sum_qkv[2],
+        sum_dense[:, :width],
+        sum_dense[:, edge + EXPERTS],
+        sum_dense[:, edge : edge + EXPERTS],
+        sum_dense[:, width : width + shared_width],
+        sum_dense[:, width + shared_width : edge],
+        sum_shared_down,
+        sum_gate,
+        sum_up,
+        sum_down,
+    )
+
+
+def per_device_any(*shards):
+    fs_count, sp_count = lax.axis_size("fs"), lax.axis_size("sp")
+    if shards[0].shape[0] == fs_count and EXPERTS == sp_count * fs_count:
+        return per_device_split(*shards)
+    return per_device(*shards)
+
+
 def solution(mesh):
     placed = (
         P("dp", ("sp", "fs"), None),
@@ -569,7 +1147,7 @@
         P("dp", ("sp", "fs"), None),
     )
     return jax.shard_map(
-        per_device,
+        per_device_any,
         mesh=mesh,
         in_specs=placed,
         out_specs=(

time: 2250 us -> 932 us (0.41)
  waiting for transfers between devices: 1450 us -> 371 us
  matrix products: 316 us -> 81.9 us
  local copies, waits for them, and re-layouts: 181 us -> 72.5 us
  Pallas kernels: 0 us -> 104 us
  blocking collectives: 98.1 us -> 154 us
  other arithmetic: 99.5 us -> 48 us
  starting transfers between devices: 48.8 us -> 71.5 us
    reduce_scatter x12 -> x2, waiting for transfers between devices: 755 us -> 0.02 us  [the longest x1 0.02 us: per_device_split(): lax.psum_scatter(grad_shared_down.astype(BF16), ('sp', 'fs'), scatter_dim...]
    dot_general x62 -> x24, matrix products: 316 us -> 81.9 us  [the longest x6 28.9 us: dot_nt(): lax.dot_general(left, right, (((1,), (1,)), ((), ())), preferred_element_...]
    all_gather x12 -> x4, waiting for transfers between devices: 293 us -> 71 us  [the longest x1 48.5 us: per_device_split(): lax.all_gather(jnp.concatenate([grouped, small], axis=1), ('sp', 'fs'), a...]
    psum x1 -> x0, waiting for transfers between devices: 199 us -> none  [per_device(): lax.psum(part_query.astype(jnp.bfloat16), 'dp').astype(jnp.float32)]
    all_to_all x0 -> x3, blocking collectives: none -> 154 us  [the longest x2 130 us: exchange(): lax.all_to_all(chunks, ('sp', 'fs'), split_axis=0, concat_axis=0, tiled=T...]
    ppermute x0 -> x6, waiting for transfers between devices: none -> 116 us  [swap_sum(): other = lax.ppermute(value, axis, [(0, 1), (1, 0)])]
    pallas_call x0 -> x3, Pallas kernels: none -> 104 us  [the longest x1 45.4 us: expert_pass(): pl.pallas_call(expert_kernel, grid=(hidden // tile,), in_specs=[whole, wh...]
    unnamed x2 -> x0, blocking collectives: 61 us -> none
  transfers between devices with their start and end apart: 34 -> 22, of which waited for: 27 -> 12; matrix products, arithmetic and copies ran while one was open for 17% -> 21% of each run, Pallas kernels for 0% -> 11%
where the time goes in v1:
time: 932 us; the launch traced here: 918 us
  waiting for transfers between devices  371 us (40%)
  blocking collectives  154 us (17%)
  Pallas kernels  104 us (11%)
  matrix products  81.9 us (9%)
  local copies, waits for them, and re-layouts  72.5 us (8%)
  starting transfers between devices  71.5 us (8%)
  other arithmetic  48 us (5%)
  between operations  15.6 us (2%)
    all_to_all x2, blocking collectives, exchange(): lax.all_to_all(chunks, ('sp', 'fs'), split_axis=0, concat_axis=0, tiled=T...  130 us
    ppermute x6, waiting for transfers between devices, swap_sum(): other = lax.ppermute(value, axis, [(0, 1), (1, 0)])  116 us
    all_to_all x3, waiting for transfers between devices, own_expert(): moved = lax.all_to_all(shard, 'sp', split_axis=0, concat_axis=0, tiled=True)  89.8 us
    all_to_all x4, waiting for transfers between devices, exchange(): lax.all_to_all(chunks, ('sp', 'fs'), split_axis=0, concat_axis=0, tiled=T...  58.2 us
    all_gather x1, waiting for transfers between devices, per_device_split(): lax.all_gather(jnp.concatenate([grouped, small], axis=1), ('sp', 'fs'), a...  48.5 us
    pallas_call x1, Pallas kernels, expert_pass(): pl.pallas_call(expert_kernel, grid=(hidden // tile,), in_specs=[whole, wh...  45.4 us
    pallas_call x1, Pallas kernels, attend_grad(): pl.pallas_call(functools.partial(attend_grad_kernel, block, score_scale),...  36.7 us
    all_to_all x3, waiting for transfers between devices, to_owner(): return lax.all_to_all(parts, 'sp', split_axis=0, concat_axis=0, tiled=True)  35.6 us
  transfers between devices with their start and end apart: 22, of which 12 were waited for; matrix products, arithmetic and copies ran while one was open for 21% of the time, Pallas kernels for 11%

profile of v1, /device:TPU:12, one launch (start us, length us, event | category | flops | bytes accessed | tf_op | source)
XLA Modules:
  0.0 917.7 jit_solution(12358225632900139537)
XLA Ops:
  7.3 23.9 %all_to_all.65 = bf16[4,128,768]{2,1,0:T(8,128)(2,1)} all-to-all(bf16[4,128,768]{2,1,0:T(8,128)(2,1)} %param.17), channel_id=1, replica_groups=mesh['dp'=2,'sp'=4,'fs'=4] {'fs'}, dimensions={0} | all-to-all | bytes 1572864 | tf_op jit(solution)/shard_map/all_to_all | solution.py:881
  36.8 22.5 %all-gather.7.cloned.1.call-done = bf16[2048,768]{1,0:T(8,128)(2,1)} async-done(((bf16[512,768]{1,0:T(8,128)(2,1)}), bf16[2048,768]{1,0:T(8,128)(2,1)}) %all-gather.7.cloned.1.call-update) | async-done | bytes 3145744 | tf_op jit(solution)/shard_map/all_gather | solution.py:882
  62.1 48.5 %all-gather.5.cloned.1.call-done = bf16[768,2432]{1,0:T(8,128)(2,1)} async-done(((bf16[48,2432]{1,0:T(8,128)(2,1)}), bf16[768,2432]{1,0:T(8,128)(2,1)}) %all-gather.5.cloned.1.call-update) | async-done | bytes 3735568 | tf_op jit(solution)/shard_map/all_gather | solution.py:898
  117.4 21.6 %attend.1 = (bf16[192,2048]{1,0:T(8,128)(2,1)}, f32[3,1,2048]{2,1,0:T(1,128)}) custom-call(bf16[576,2048]{1,0:T(8,128)(2,1)} %convolution_convert_fusion.4.q_ref.k_ref.v_ref, bf16[576,2048]{1,0:T(8,128)(2,1)} %convolution_convert_fusion.4.q_ref.k_ref.v_ref, bf16[576,2048]{1,0:T(8,128)(2,1)} %convolution_convert_fusion.4.q_ref.k_ref.v_ref, ...), custom_call_target="tpu_custom_call" | custom-call | tf_op jit(solution)/shard_map/attend/pallas_call | solution.py:703
  140.3 44.1 %all_to_all.66 = bf16[16,128,192]{1,2,0:T(8,128)(2,1)} all-to-all(bf16[16,128,192]{1,2,0:T(8,128)(2,1)S(1)} %copy_bitcast_fusion.1), channel_id=1, replica_groups=mesh['dp'=2,'sp'=4,'fs'=4] {'sp','fs'}, dimensions={0} | all-to-all | bytes 1572864 | tf_op jit(solution)/shard_map/all_to_all | solution.py:844
  202.6 21.5 %all-to-all-done.3 = bf16[4,192,2048]{2,1,0:T(8,128)(2,1)S(1)} async-done(((bf16[4,192,2048]{2,1,0:T(8,128)(2,1)}), bf16[4,192,2048]{2,1,0:T(8,128)(2,1)S(1)}, u32[]{:S(2)}, u32[]{:S(2)}) %all-to-all-start.3) | async-done | bytes 3145760 | tf_op jit(solution)/shard_map/all_to_all | solution.py:917
  225.8 6.6 all-to-all-start.4
  240.1 27.6 %all-to-all-done.4 = bf16[4,192,2048]{2,1,0:T(8,128)(2,1)} async-done(((bf16[4,192,2048]{2,1,0:T(8,128)(2,1)}), bf16[4,192,2048]{2,1,0:T(8,128)(2,1)}, u32[]{:S(2)}, u32[]{:S(2)}) %all-to-all-start.4) | async-done | bytes 3145760 | tf_op jit(solution)/shard_map/all_to_all | solution.py:917
  267.7 85.6 %all_to_all.67 = bf16[16,144,768]{2,1,0:T(8,128)(2,1)S(1)} all-to-all(bf16[16,144,768]{2,1,0:T(8,128)(2,1)} %pad_maximum_fusion), channel_id=1, replica_groups=mesh['dp'=2,'sp'=4,'fs'=4] {'sp','fs'}, dimensions={0} | all-to-all | bytes 7077888 | tf_op jit(solution)/shard_map/all_to_all | solution.py:844
  361.1 40.7 %all-to-all-done.5 = bf16[4,192,2048]{2,1,0:T(8,128)(2,1)} async-done(((bf16[4,192,2048]{2,1,0:T(8,128)(2,1)}), bf16[4,192,2048]{2,1,0:T(8,128)(2,1)}, u32[]{:S(2)}, u32[]{:S(2)}) %all-to-all-start.5) | async-done | bytes 3145760 | tf_op jit(solution)/shard_map/all_to_all | solution.py:917
  401.8 45.4 %expert_pass.1 = (bf16[1152,768]{1,0:T(8,128)(2,1)}, bf16[1152,768]{1,0:T(8,128)(2,1)}, bf16[768,2048]{1,0:T(8,128)(2,1)}, bf16[768,2048]{1,0:T(8,128)(2,1)}, bf16[768,2048]{1,0:T(8,128)(2,1)}) custom-call(bf16[1152,768]{1,0:T(8,128)(2,1)} %bitcast.119, bf16[1152,768]{1,0:T(8,128)(2,1)} %bitcast.118, bf16[768,2048]{1,0:T(8,128)(2,1)} %bitcast.116, ...), custom_call_target="tpu_custom_call" | custom-call | tf_op jit(solution)/shard_map/expert_pass/pallas_call | solution.py:819
  451.2 8.9 all-to-all-start.6
  472.4 9.8 %multiply_convert_fusion = (bf16[512,2048]{1,0:T(8,128)(2,1)}, bf16[512,2048]{1,0:T(8,128)(2,1)}, bf16[512,2048]{1,0:T(8,128)(2,1)S(1)}) fusion(f32[512,2048]{1,0:T(8,128)} %fusion.16, f32[512,2048]{1,0:T(8,128)} %fusion.12, bf16[512,768]{1,0:T(8,128)(2,1)} %bitcast.140, bf16[2048,768]{1,0:T(8,128)(2,1)} %all-gather.11.cloned.1.call-done), kind=kOutput, calls=%fused_computation.12 | convolution fusion | flops 1627389952 | bytes 18612224 | tf_op jit(solution)/shard_map/dot_general | solution.py:563
  493.6 58.2 %all-to-all-done.6 = bf16[16,144,768]{2,1,0:T(8,128)(2,1)S(1)} async-done(((bf16[16,144,768]{2,1,0:T(8,128)(2,1)}), bf16[16,144,768]{2,1,0:T(8,128)(2,1)S(1)}, u32[]{:S(2)}, u32[]{:S(2)}) %all-to-all-start.6) | async-done | bytes 3538976 | tf_op jit(solution)/shard_map/all_to_all | solution.py:844
  577.1 15.2 %all-to-all-done.10 = bf16[4,192,2048]{2,1,0:T(8,128)(2,1)} async-done(((bf16[4,192,2048]{2,1,0:T(8,128)(2,1)}), bf16[4,192,2048]{2,1,0:T(8,128)(2,1)}, u32[]{:S(2)}, u32[]{:S(2)}) %all-to-all-start.10) | async-done | bytes 3145760 | tf_op jit(solution)/shard_map/all_to_all | solution.py:999
  613.8 20.4 %all-to-all-done.11 = bf16[4,192,2048]{2,1,0:T(8,128)(2,1)} async-done(((bf16[4,192,2048]{2,1,0:T(8,128)(2,1)}), bf16[4,192,2048]{2,1,0:T(8,128)(2,1)}, u32[]{:S(2)}, u32[]{:S(2)}) %all-to-all-start.11) | async-done | bytes 3145760 | tf_op jit(solution)/shard_map/all_to_all | solution.py:999
  634.2 9.5 %all-to-all-start.7 = ((bf16[16,128,192]{1,2,0:T(8,128)(2,1)}), bf16[16,128,192]{1,2,0:T(8,128)(2,1)}, u32[]{:S(2)}, u32[]{:S(2)}) async-start(bf16[16,128,192]{1,2,0:T(8,128)(2,1)} %bitcast.126), calls=%async_computation.7 | async-start | bytes 1572864 | tf_op jit(solution)/shard_map/all_to_all | solution.py:844
  650.8 12.2 %concatenate.37 = bf16[768,4992]{1,0:T(8,128)(2,1)} concatenate(bf16[768,768]{1,0:T(8,128)(2,1)} %copy.159, bf16[768,2048]{1,0:T(8,128)(2,1)} %convolution_convert_fusion.2, bf16[768,2048]{1,0:T(8,128)(2,1)} %convolution_convert_fusion.1, bf16[768,16]{1,0:T(8,128)(2,1)S(1)} %copy.160, bf16[768,112]{1,0:T(8,128)(2,1)S(1)} %pad.11), dimensions={1} | concatenate | bytes 15335424 | tf_op jit(solution)/shard_map/concatenate | solution.py:1073
  671.7 36.7 %attend_grad.1 = (bf16[192,2048]{1,0:T(8,128)(2,1)}, bf16[192,2048]{1,0:T(8,128)(2,1)}, bf16[192,2048]{1,0:T(8,128)(2,1)}) custom-call(bf16[576,2048]{1,0:T(8,128)(2,1)} %convolution_convert_fusion.4.q_ref.k_ref.v_ref, bf16[576,2048]{1,0:T(8,128)(2,1)} %convolution_convert_fusion.4.q_ref.k_ref.v_ref, ...), custom_call_target="tpu_custom_call" | custom-call | tf_op jit(solution)/shard_map/attend_grad/pallas_call | solution.py:736
  725.4 85.5 %collective-permute-done.2 = bf16[128,768]{1,0:T(8,128)(2,1)S(1)} collective-permute-done((bf16[128,768]{1,0:T(8,128)(2,1)}, bf16[128,768]{1,0:T(8,128)(2,1)S(1)}, u32[]{:S(2)}, u32[]{:S(2)}) %collective-permute-start.2) | collective-permute-done | bytes 196640 | tf_op jit(solution)/shard_map/ppermute | solution.py:838
  812.6 7.0 convert_add_fusion.2
  849.3 6.9 convert_add_fusion.1
  856.2 21.4 %collective-permute-done.5 = bf16[4,192,2048]{2,1,0:T(8,128)(2,1)} collective-permute-done((bf16[4,192,2048]{2,1,0:T(8,128)(2,1)}, bf16[4,192,2048]{2,1,0:T(8,128)(2,1)}, u32[]{:S(2)}, u32[]{:S(2)}) %collective-permute-start.5) | collective-permute-done | bytes 3145760 | tf_op jit(solution)/shard_map/ppermute | solution.py:838
  877.6 6.9 convert_add_fusion
  (292 shorter events, 215.7 us)
Async XLA Ops:
  7.2 52.1 %all-gather.7.cloned.1.call-start = ((), (), s32[]{:S(2)}) async-start(), calls=%async_computation.16 | async-start | bytes 3932160 | tf_op jit(solution)/shard_map/all_gather | solution.py:882
  31.2 79.3 %all-gather.5.cloned.1.call-start = ((), (), s32[]{:S(2)}) async-start(), calls=%async_computation.15 | async-start | bytes 3969024 | tf_op jit(solution)/shard_map/all_gather | solution.py:898
  34.0 162.3 %all-gather.9.cloned.1.call-start = ((), (), s32[]{:S(2)}) async-start(), calls=%async_computation.17 | async-start | bytes 7938048 | tf_op jit(solution)/shard_map/all_gather | solution.py:901
  59.3 52.5 %copy-start.10 = (bf16[2048,768]{1,0:T(8,128)(2,1)S(1)}, bf16[2048,768]{1,0:T(8,128)(2,1)}, u32[]{:S(2)}) copy-start(bf16[2048,768]{1,0:T(8,128)(2,1)} %all-gather.7.cloned.1.call-done) | copy-start | bytes 9437188
  62.0 55.3 %copy-start.48 = (f32[2048]{0:T(1024)}, f32[2048]{0:T(1024)S(1)}, u32[]{:S(2)}) copy-start(f32[2048]{0:T(1024)S(1)} %add_rsqrt_fusion) | copy-start | bytes 24580
  184.5 39.6 %all-to-all-start.3 = ((bf16[4,192,2048]{2,1,0:T(8,128)(2,1)}), bf16[4,192,2048]{2,1,0:T(8,128)(2,1)S(1)}, u32[]{:S(2)}, u32[]{:S(2)}) async-start(bf16[4,192,2048]{2,1,0:T(8,128)(2,1)} %param.30), calls=%async_computation.3 | async-start | bytes 6291456 | tf_op jit(solution)/shard_map/all_to_all | solution.py:917
  225.8 41.9 %all-to-all-start.4 = ((bf16[4,192,2048]{2,1,0:T(8,128)(2,1)}), bf16[4,192,2048]{2,1,0:T(8,128)(2,1)}, u32[]{:S(2)}, u32[]{:S(2)}) async-start(bf16[4,192,2048]{2,1,0:T(8,128)(2,1)} %param.31), calls=%async_computation.4 | async-start | bytes 6291456 | tf_op jit(solution)/shard_map/all_to_all | solution.py:917
  353.3 48.5 %all-to-all-start.5 = ((bf16[4,192,2048]{2,1,0:T(8,128)(2,1)}), bf16[4,192,2048]{2,1,0:T(8,128)(2,1)}, u32[]{:S(2)}, u32[]{:S(2)}) async-start(bf16[4,192,2048]{2,1,0:T(8,128)(2,1)} %param.32), calls=%async_computation.5 | async-start | bytes 6291456 | tf_op jit(solution)/shard_map/all_to_all | solution.py:917
  358.5 113.8 %all-gather.11.cloned.1.call-start = ((), (), s32[]{:S(2)}) async-start(), calls=%async_computation.18 | async-start | bytes 3342336 | tf_op jit(solution)/shard_map/all_gather | solution.py:907
  451.2 100.6 %all-to-all-start.6 = ((bf16[16,144,768]{2,1,0:T(8,128)(2,1)}), bf16[16,144,768]{2,1,0:T(8,128)(2,1)S(1)}, u32[]{:S(2)}, u32[]{:S(2)}) async-start(bf16[16,144,768]{2,1,0:T(8,128)(2,1)} %pad_maximum_fusion.1), calls=%async_computation.6 | async-start | bytes 7077888 | tf_op jit(solution)/shard_map/all_to_all | solution.py:844
  460.1 263.2 %reduce-scatter.5.cloned.1.call-start = ((), (), s32[]{:S(2)}) async-start(), calls=%async_computation.20 | async-start | bytes 3342336 | tf_op jit(solution)/shard_map/reduce_scatter | solution.py:1084
  551.8 40.5 %all-to-all-start.10 = ((bf16[4,192,2048]{2,1,0:T(8,128)(2,1)}), bf16[4,192,2048]{2,1,0:T(8,128)(2,1)}, u32[]{:S(2)}, u32[]{:S(2)}) async-start(bf16[4,192,2048]{2,1,0:T(8,128)(2,1)} %bitcast.124), calls=%async_computation.12 | async-start | bytes 6291456 | tf_op jit(solution)/shard_map/all_to_all | solution.py:999
  592.4 41.8 %all-to-all-start.11 = ((bf16[4,192,2048]{2,1,0:T(8,128)(2,1)}), bf16[4,192,2048]{2,1,0:T(8,128)(2,1)}, u32[]{:S(2)}, u32[]{:S(2)}) async-start(bf16[4,192,2048]{2,1,0:T(8,128)(2,1)} %bitcast.42), calls=%async_computation.13 | async-start | bytes 6291456 | tf_op jit(solution)/shard_map/all_to_all | solution.py:999
  634.2 28.8 %all-to-all-start.7 = ((bf16[16,128,192]{1,2,0:T(8,128)(2,1)}), bf16[16,128,192]{1,2,0:T(8,128)(2,1)}, u32[]{:S(2)}, u32[]{:S(2)}) async-start(bf16[16,128,192]{1,2,0:T(8,128)(2,1)} %bitcast.126), calls=%async_computation.7 | async-start | bytes 1572864 | tf_op jit(solution)/shard_map/all_to_all | solution.py:844
  643.6 249.8 %reduce-scatter.3.cloned.1.call-start = ((), (), s32[]{:S(2)}) async-start(), calls=%async_computation.19 | async-start | bytes 8146944 | tf_op jit(solution)/shard_map/reduce_scatter | solution.py:1083
  663.0 51.4 %all-to-all-start.12 = ((bf16[4,192,2048]{2,1,0:T(8,128)(2,1)}), bf16[4,192,2048]{2,1,0:T(8,128)(2,1)}, u32[]{:S(2)}, u32[]{:S(2)}) async-start(bf16[4,192,2048]{2,1,0:T(8,128)(2,1)} %bitcast.123), calls=%async_computation.14 | async-start | bytes 6291456 | tf_op jit(solution)/shard_map/all_to_all | solution.py:999
  668.1 144.5 %collective-permute-start.3 = (bf16[4,192,2048]{2,1,0:T(8,128)(2,1)}, bf16[4,192,2048]{2,1,0:T(8,128)(2,1)}, u32[]{:S(2)}, u32[]{:S(2)}) collective-permute-start(bf16[4,192,2048]{2,1,0:T(8,128)(2,1)} %all-to-all-done.10), channel_id=1, source_target_pairs={{0,16},{16,0},{1,17},{17,1},{2,18},{18,2},{3,19},{19,3},{4,20},{20... | collective-permute-start | bytes 9437192 | tf_op jit(solution)/shard_map/ppermute | solution.py:838
  714.4 110.7 %all-to-all-start.8 = ((bf16[16,128,576]{1,2,0:T(8,128)(2,1)}), bf16[16,128,576]{1,2,0:T(8,128)(2,1)}, u32[]{:S(2)}, u32[]{:S(2)}) async-start(bf16[16,128,576]{1,2,0:T(8,128)(2,1)} %copy_bitcast_fusion), calls=%async_computation.8 | async-start | bytes 4718592 | tf_op jit(solution)/shard_map/all_to_all | solution.py:844
  720.5 128.8 %collective-permute-start.4 = (bf16[4,192,2048]{2,1,0:T(8,128)(2,1)}, bf16[4,192,2048]{2,1,0:T(8,128)(2,1)}, u32[]{:S(2)}, u32[]{:S(2)}) collective-permute-start(bf16[4,192,2048]{2,1,0:T(8,128)(2,1)} %all-to-all-done.11), channel_id=1, source_target_pairs={{0,16},{16,0},{1,17},{17,1},{2,18},{18,2},{3,19},{19,3},{4,20},{20... | collective-permute-start | bytes 9437192 | tf_op jit(solution)/shard_map/ppermute | solution.py:838
  723.3 87.6 %collective-permute-start.2 = (bf16[128,768]{1,0:T(8,128)(2,1)}, bf16[128,768]{1,0:T(8,128)(2,1)S(1)}, u32[]{:S(2)}, u32[]{:S(2)}) collective-permute-start(bf16[128,768]{1,0:T(8,128)(2,1)} %reduce-scatter.5.cloned.1.call-done), channel_id=1, source_target_pairs={{0,16},{16,0},{1,17},{17,1},{2,18},{18,2},{3,19},{19,3},{4,20},{20... | collective-permute-start | bytes 589832 | tf_op jit(solution)/shard_map/ppermute | solution.py:838
  724.0 153.7 %collective-permute-start.5 = (bf16[4,192,2048]{2,1,0:T(8,128)(2,1)}, bf16[4,192,2048]{2,1,0:T(8,128)(2,1)}, u32[]{:S(2)}, u32[]{:S(2)}) collective-permute-start(bf16[4,192,2048]{2,1,0:T(8,128)(2,1)} %all-to-all-done.12), channel_id=1, source_target_pairs={{0,16},{16,0},{1,17},{17,1},{2,18},{18,2},{3,19},{19,3},{4,20},{20... | collective-permute-start | bytes 9437192 | tf_op jit(solution)/shard_map/ppermute | solution.py:838
  842.9 44.4 %all-to-all-start.9 = ((bf16[16,48,704]{2,1,0:T(8,128)(2,1)}), bf16[16,48,704]{2,1,0:T(8,128)(2,1)}, u32[]{:S(2)}, u32[]{:S(2)}) async-start(bf16[16,48,704]{2,1,0:T(8,128)(2,1)} %pad_maximum_fusion.2), calls=%async_computation.9 | async-start | bytes 2359296 | tf_op jit(solution)/shard_map/all_to_all | solution.py:844
  888.7 9.9 %collective-permute-start = (bf16[4,48,704]{2,1,0:T(8,128)(2,1)S(1)}, bf16[4,48,704]{2,1,0:T(8,128)(2,1)S(1)}, u32[]{:S(2)}, u32[]{:S(2)}) collective-permute-start(bf16[4,48,704]{2,1,0:T(8,128)(2,1)S(1)} %bitcast_reduce_fusion), channel_id=1, source_target_pairs={{0,16},{16,0},{1,17},{17,1},{2,18},{18,2},{3,19},{19,3},{4,20},{20... | collective-permute-start | bytes 811016 | tf_op jit(solution)/shard_map/ppermute | solution.py:838
  893.5 13.8 %collective-permute-start.1 = (bf16[48,4992]{1,0:T(8,128)(2,1)}, bf16[48,4992]{1,0:T(8,128)(2,1)S(1)}, u32[]{:S(2)}, u32[]{:S(2)}) collective-permute-start(bf16[48,4992]{1,0:T(8,128)(2,1)} %reduce-scatter.3.cloned.1.call-done), channel_id=1, source_target_pairs={{0,16},{16,0},{1,17},{17,1},{2,18},{18,2},{3,19},{19,3},{4,20},{20... | collective-permute-start | bytes 1437704 | tf_op jit(solution)/shard_map/ppermute | solution.py:838
  (69 other events, 589.5 us)
Sparse Core Ops, SparseCore 0:
  31.3 27.9 all-gather.6
  62.1 48.4 all-gather.4
  113.4 80.2 all-gather.8
  361.3 52.3 all-gather.10
  487.2 73.2 reduce-scatter.4
  663.1 138.8 reduce-scatter.2

commit v2 on v0

--- a/solution.py
+++ b/solution.py
@@ -1,8 +1,11 @@
+import functools
 import math
 
 import jax
 import jax.numpy as jnp
 from jax import lax
+from jax.experimental import pallas as pl
+from jax.experimental.pallas import tpu as pltpu
 from jax.sharding import PartitionSpec as P
 
 HEADS = 12
@@ -548,6 +551,1409 @@
     )
 
 
+BF16 = jnp.bfloat16
+F32 = jnp.float32
+LANES = 128
+NOTE_ROWS = 8
+VMEM_WHOLE = pl.BlockSpec(memory_space=pltpu.VMEM)
+IN_PLACE = pl.BlockSpec(memory_space=pl.ANY)
+ROOM = 60 * 1024 * 1024
+
+
+def dot32(left, right):
+    return jnp.dot(left, right, preferred_element_type=F32)
+
+
+def dot_nt(left, right):
+    return lax.dot_general(left, right, (((1,), (1,)), ((), ())), preferred_element_type=F32)
+
+
+def turn(values, cosine, sine):
+    half = values.shape[0] // 2
+    front, back = values[:half], values[half:]
+    return jnp.concatenate([front * cosine - back * sine, back * cosine + front * sine], axis=0)
+
+
+def turn_back(values, cosine, sine):
+    half = values.shape[0] // 2
+    front, back = values[:half], values[half:]
+    return jnp.concatenate([front * cosine + back * sine, back * cosine - front * sine], axis=0)
+
+
+def causal(block):
+    keys = lax.broadcasted_iota(jnp.int32, (block, block), 0)
+    queries = lax.broadcasted_iota(jnp.int32, (block, block), 1)
+    return keys <= queries
+
+
+def remote_params(number):
+    return pltpu.CompilerParams(
+        collective_id=number, has_side_effects=True, vmem_limit_bytes=ROOM
+    )
+
+
+def places():
+    sp_count, fs_count = lax.axis_size("sp"), lax.axis_size("fs")
+    own = lax.axis_index("sp") * fs_count + lax.axis_index("fs")
+    return sp_count * fs_count, own
+
+
+def at_place(place):
+    fs_count = lax.axis_size("fs")
+    return {"sp": place // fs_count, "fs": lax.rem(place, fs_count)}
+
+
+def greet_places():
+    total, own = places()
+    barrier = pltpu.get_barrier_semaphore()
+
+    def greet(step, _):
+        pl.semaphore_signal(
+            barrier,
+            inc=1,
+            device_id=at_place(lax.rem(own + step, total)),
+            device_id_type=pl.DeviceIdType.MESH,
+        )
+        return 0
+
+    lax.fori_loop(1, total, greet, 0)
+
+
+def await_places(others=0):
+    pl.semaphore_wait(pltpu.get_barrier_semaphore(), places()[0] - 1 + others)
+
+
+def columns(index, size):
+    return pl.ds(pl.multiple_of(index * size, size), size)
+
+
+class Swap:
+    def __init__(self, source, target, send, recv, local):
+        self.source, self.target = source, target
+        self.send, self.recv, self.local = send, recv, local
+
+    def remote(self, place, landing, mark):
+        return pltpu.make_async_remote_copy(
+            src_ref=self.source(place),
+            dst_ref=self.target(landing),
+            send_sem=self.send.at[place],
+            recv_sem=self.recv.at[mark],
+            device_id=at_place(place),
+            device_id_type=pl.DeviceIdType.MESH,
+        )
+
+    def own(self):
+        own = places()[1]
+        return pltpu.make_async_copy(self.source(own), self.target(own), self.local)
+
+    def start(self, place):
+        own = places()[1]
+
+        @pl.when(place != own)
+        def _():
+            self.remote(place, own, own).start()
+
+        @pl.when(place == own)
+        def _():
+            self.own().start()
+
+    def start_all(self):
+        total, own = places()
+
+        def begin(step, _):
+            self.remote(lax.rem(own + step, total), own, own).start()
+            return 0
+
+        lax.fori_loop(1, total, begin, 0)
+        self.own().start()
+
+    def finish(self):
+        total, own = places()
+
+        def end(step, _):
+            place = lax.rem(own + step, total)
+            copy = self.remote(place, place, place)
+            copy.wait_send()
+            copy.wait_recv()
+            return 0
+
+        lax.fori_loop(1, total, end, 0)
+        self.own().wait()
+
+
+def swap_semaphores(total):
+    return [
+        pltpu.SemaphoreType.DMA((total,)),
+        pltpu.SemaphoreType.DMA((total,)),
+        pltpu.SemaphoreType.DMA,
+    ]
+
+
+class Spread:
+    def __init__(self, shard, full, stage, near, far_send, far_recv, dp_send, dp_recv, local):
+        self.shard, self.full, self.stage = shard, full, stage
+        self.near, self.far_send, self.far_recv = near, far_send, far_recv
+        self.dp_send, self.dp_recv, self.local = dp_send, dp_recv, local
+        self.sp, self.dp = lax.axis_index("sp"), lax.axis_index("dp")
+        self.core = self.sp + 1 - 2 * lax.rem(self.sp, 2)
+        self.other = 2 - 2 * (self.sp // 2)
+        self.half = shard.shape[1] // 2
+        self.rows = pl.ds(pl.multiple_of(self.dp * self.half, self.half), self.half)
+        self.dp_rows = pl.ds(pl.multiple_of((1 - self.dp) * self.half, self.half), self.half)
+
+    def to_core(self):
+        return pltpu.make_async_remote_copy(
+            src_ref=self.shard.at[self.core],
+            dst_ref=self.full.at[self.sp],
+            send_sem=self.near.at[0],
+            recv_sem=self.near.at[1],
+            device_id={"sp": self.core},
+            device_id_type=pl.DeviceIdType.MESH,
+        )
+
+    def to_far(self, turn):
+        return pltpu.make_async_remote_copy(
+            src_ref=self.shard.at[self.other + turn, self.rows],
+            dst_ref=self.full.at[self.sp, self.rows],
+            send_sem=self.far_send.at[turn],
+            recv_sem=self.far_recv.at[lax.rem(self.sp, 2)],
+            device_id={"sp": self.other + turn},
+            device_id_type=pl.DeviceIdType.MESH,
+        )
+
+    def from_far(self, turn):
+        return pltpu.make_async_remote_copy(
+            src_ref=self.shard.at[self.other + turn, self.rows],
+            dst_ref=self.full.at[self.other + turn, self.rows],
+            send_sem=self.far_send.at[turn],
+            recv_sem=self.far_recv.at[turn],
+            device_id={"sp": self.other + turn},
+            device_id_type=pl.DeviceIdType.MESH,
+        )
+
+    def to_dp(self, turn):
+        block = self.full.at[self.other + turn, self.rows]
+        return pltpu.make_async_remote_copy(
+            src_ref=block,
+            dst_ref=block,
+            send_sem=self.dp_send.at[turn],
+            recv_sem=self.dp_recv.at[turn],
+            device_id={"dp": 1 - self.dp},
+            device_id_type=pl.DeviceIdType.MESH,
+        )
+
+    def from_dp(self, turn):
+        block = self.full.at[self.other + turn, self.dp_rows]
+        return pltpu.make_async_remote_copy(
+            src_ref=block,
+            dst_ref=block,
+            send_sem=self.dp_send.at[turn],
+            recv_sem=self.dp_recv.at[turn],
+            device_id={"dp": 1 - self.dp},
+            device_id_type=pl.DeviceIdType.MESH,
+        )
+
+    def own_in(self):
+        return pltpu.make_async_copy(self.shard.at[self.sp], self.stage, self.local.at[0])
+
+    def own_out(self):
+        return pltpu.make_async_copy(self.stage, self.full.at[self.sp], self.local.at[1])
+
+    def start_cross(self):
+        self.own_in().start()
+        self.to_far(0).start()
+        self.to_far(1).start()
+        self.to_core().start()
+
+    def finish_cross(self):
+        self.own_in().wait()
+        self.own_out().start()
+        for turn in range(2):
+            self.from_far(turn).wait_recv()
+            self.to_far(turn).wait_send()
+        self.to_core().wait_send()
+        self.to_core().wait_recv()
+        self.own_out().wait()
+
+    def start_share(self):
+        self.to_dp(0).start()
+        self.to_dp(1).start()
+
+    def finish_share(self):
+        for turn in range(2):
+            self.from_dp(turn).wait_recv()
+            self.to_dp(turn).wait_send()
+
+
+def pair_semaphores():
+    return pltpu.SemaphoreType.DMA((2,))
+
+
+def cross_scratch(shard):
+    return [pltpu.VMEM(shard.shape[1:], shard.dtype)] + [pair_semaphores()] * 4
+
+
+def share_scratch():
+    return [pair_semaphores()] * 2
+
+
+def crossing(shard, full, stage, near, far_send, far_recv, local):
+    return Spread(shard, full, stage, near, far_send, far_recv, None, None, local)
+
+
+def sharing(full, dp_send, dp_recv):
+    return Spread(full, full, None, None, None, None, dp_send, dp_recv, None)
+
+
+def greet_dp():
+    pl.semaphore_signal(
+        pltpu.get_barrier_semaphore(),
+        inc=1,
+        device_id={"dp": 1 - lax.axis_index("dp")},
+        device_id_type=pl.DeviceIdType.MESH,
+    )
+
+
+def gather_kernel(
+    tokens_ref,
+    pack_ref,
+    shard_ref,
+    seq_ref,
+    got_ref,
+    full_ref,
+    z_send,
+    z_recv,
+    core_send,
+    core_recv,
+    y_send,
+    y_recv,
+    late_send,
+    late_recv,
+    pack_send,
+    pack_recv,
+    up_send,
+    up_recv,
+    down_send,
+    down_recv,
+    local,
+    *cross,
+):
+    fs_count, sp_count = lax.axis_size("fs"), lax.axis_size("sp")
+    fs_place, sp_place = lax.axis_index("fs"), lax.axis_index("sp")
+    core = sp_place + 1 - 2 * lax.rem(sp_place, 2)
+    across = lax.rem(sp_place + 2, sp_count)
+    barrier = pltpu.get_barrier_semaphore()
+
+    def fs_peer(step):
+        return lax.rem(fs_place + step, fs_count)
+
+    def sp_peer(step):
+        return lax.rem(sp_place + step, sp_count)
+
+    def greet(where):
+        pl.semaphore_signal(barrier, inc=1, device_id=where, device_id_type=pl.DeviceIdType.MESH)
+
+    def move(source, target, send, recv, where):
+        return pltpu.make_async_remote_copy(
+            src_ref=source,
+            dst_ref=target,
+            send_sem=send,
+            recv_sem=recv,
+            device_id=where,
+            device_id_type=pl.DeviceIdType.MESH,
+        )
+
+    def each(count, body):
+        def run(index, _):
+            body(index)
+            return 0
+
+        lax.fori_loop(1, count, run, 0)
+
+    each(fs_count, lambda step: greet({"fs": fs_peer(step)}))
+    each(sp_count, lambda step: greet({"sp": sp_peer(step)}))
+    pl.semaphore_wait(barrier, fs_count + sp_count - 2)
+
+    def pack_move(place, mark):
+        return move(
+            pack_ref.at[place],
+            got_ref.at[sp_place, fs_place],
+            pack_send.at[place],
+            pack_recv.at[mark],
+            {"sp": place},
+        )
+
+    def pack_landed(mark):
+        return move(
+            pack_ref.at[mark],
+            got_ref.at[mark, fs_place],
+            pack_send.at[mark],
+            pack_recv.at[mark],
+            {"sp": mark},
+        )
+
+    def z_move(place):
+        return move(
+            tokens_ref.at[place],
+            seq_ref.at[sp_place, fs_place],
+            z_send.at[place],
+            z_recv.at[fs_place],
+            {"fs": place},
+        )
+
+    def z_landed(mark):
+        return move(
+            tokens_ref.at[mark],
+            seq_ref.at[sp_place, mark],
+            z_send.at[mark],
+            z_recv.at[mark],
+            {"fs": mark},
+        )
+
+    def to_core(source, mark):
+        return move(
+            source, seq_ref.at[sp_place, mark], core_send.at[mark], core_recv.at[mark], {"sp": core}
+        )
+
+    def to_across(source, mark):
+        return move(
+            source, seq_ref.at[sp_place, mark], y_send.at[mark], y_recv.at[mark], {"sp": across}
+        )
+
+    def late(mark):
+        block = seq_ref.at[across, mark]
+        return move(block, block, late_send.at[mark], late_recv.at[mark], {"sp": core})
+
+    def upward(mark):
+        block = got_ref.at[:, mark]
+        return move(block, block, up_send.at[mark], up_recv.at[mark], {"fs": fs_peer(1)})
+
+    def downward(mark):
+        block = got_ref.at[:, mark]
+        return move(
+            block, block, down_send.at[mark], down_recv.at[mark], {"fs": fs_peer(fs_count - 1)}
+        )
+
+    each(sp_count, lambda step: pack_move(sp_peer(step), sp_place).start())
+    each(fs_count, lambda step: z_move(fs_peer(step)).start())
+    own_tokens = tokens_ref.at[fs_place]
+    to_across(own_tokens, fs_place).start()
+    to_core(own_tokens, fs_place).start()
+    own_seq = pltpu.make_async_copy(own_tokens, seq_ref.at[sp_place, fs_place], local.at[0])
+    own_pack = pltpu.make_async_copy(
+        pack_ref.at[sp_place], got_ref.at[sp_place, fs_place], local.at[1]
+    )
+    own_seq.start()
+    own_pack.start()
+    weights = crossing(shard_ref, full_ref, *cross)
+    weights.start_cross()
+    own_pack.wait()
+    each(sp_count, lambda step: pack_landed(sp_peer(step)).wait_recv())
+
+    has_up = fs_place < fs_count - 1
+    has_down = fs_place > 0
+
+    @pl.when(has_up)
+    def _():
+        upward(fs_place).start()
+
+    @pl.when(has_down)
+    def _():
+        downward(fs_place).start()
+
+    def relay(step):
+        below, above = fs_place - step, fs_place + step
+
+        @pl.when(below >= 0)
+        def _():
+            upward(below).wait_recv()
+
+        @pl.when((below >= 0) & has_up)
+        def _():
+            upward(below).start()
+
+        @pl.when(above < fs_count)
+        def _():
+            downward(above).wait_recv()
+
+        @pl.when((above < fs_count) & has_down)
+        def _():
+            downward(above).start()
+
+        mark = fs_peer(step)
+        z_landed(mark).wait_recv()
+        block = seq_ref.at[sp_place, mark]
+        to_across(block, mark).start()
+        to_core(block, mark).start()
+
+    each(fs_count, relay)
+
+    def pass_on(mark, _):
+        to_across(own_tokens, mark).wait_recv()
+        late(mark).start()
+        return 0
+
+    lax.fori_loop(0, fs_count, pass_on, 0)
+
+    def end(mark, _):
+        to_core(own_tokens, mark).wait_recv()
+        late(mark).wait_recv()
+        to_core(own_tokens, mark).wait_send()
+        to_across(own_tokens, mark).wait_send()
+        late(mark).wait_send()
+
+        @pl.when(has_up & (mark <= fs_place))
+        def _():
+            upward(mark).wait_send()
+
+        @pl.when(has_down & (mark >= fs_place))
+        def _():
+            downward(mark).wait_send()
+
+        return 0
+
+    lax.fori_loop(0, fs_count, end, 0)
+    each(sp_count, lambda step: pack_move(sp_peer(step), sp_place).wait_send())
+    each(fs_count, lambda step: z_move(fs_peer(step)).wait_send())
+    own_seq.wait()
+    weights.finish_cross()
+
+
+def gather_start(tokens, pack, shard):
+    sp_count, fs_count = lax.axis_size("sp"), lax.axis_size("fs")
+    fs_sems = pltpu.SemaphoreType.DMA((fs_count,))
+    sp_sems = pltpu.SemaphoreType.DMA((sp_count,))
+    return pl.pallas_call(
+        gather_kernel,
+        in_specs=[IN_PLACE] * 3,
+        out_specs=[IN_PLACE] * 3,
+        out_shape=[
+            jax.ShapeDtypeStruct((sp_count, fs_count) + tokens.shape[1:], tokens.dtype),
+            jax.ShapeDtypeStruct((sp_count, fs_count) + pack.shape[1:], pack.dtype),
+            jax.ShapeDtypeStruct(shard.shape, shard.dtype),
+        ],
+        scratch_shapes=[fs_sems] * 8
+        + [sp_sems] * 2
+        + [fs_sems] * 4
+        + [pltpu.SemaphoreType.DMA((2,))]
+        + cross_scratch(shard),
+        compiler_params=remote_params(5),
+        cost_estimate=pl.CostEstimate(
+            flops=40_000_000_000, bytes_accessed=4_000_000, transcendentals=0
+        ),
+        name="gather_start",
+    )(tokens, pack, shard)
+
+
+def attend_kernel(
+    block,
+    scale,
+    qkv_ref,
+    cos_ref,
+    sin_ref,
+    crossed_ref,
+    shard_ref,
+    o_ref,
+    lse_ref,
+    got_ref,
+    shared_ref,
+    full_ref,
+    k_rot,
+    send,
+    recv,
+    local,
+    dp_send,
+    dp_recv,
+    *cross,
+):
+    heads, length, _ = k_rot.shape
+    wide = heads * HEAD_DIM
+    total, own = places()
+    seg = length // total
+    greet_places()
+    greet_dp()
+
+    def head_rows(kind, head):
+        return columns(kind * heads + head, HEAD_DIM)
+
+    def turn_keys(head, _):
+        rotated = turn(qkv_ref[head_rows(1, head), :].astype(F32), cos_ref[...], sin_ref[...])
+        k_rot[head] = rotated.T.astype(BF16)
+        return 0
+
+    lax.fori_loop(0, heads, turn_keys, 0)
+    await_places(1)
+    share = sharing(shared_ref, dp_send, dp_recv)
+    share.start_share()
+    weights = crossing(shard_ref, full_ref, *cross)
+    weights.start_cross()
+    exchange = Swap(
+        lambda place: o_ref.at[:, columns(place, seg)],
+        lambda place: got_ref.at[
+            columns(place // lax.axis_size("fs"), wide),
+            columns(lax.rem(place, lax.axis_size("fs")), seg),
+        ],
+        send,
+        recv,
+        local,
+    )
+
+    def attend_block(place):
+        own_columns = columns(place, block)
+
+        def attend_head(head, _):
+            query = turn(
+                qkv_ref[head_rows(0, head), own_columns].astype(F32),
+                cos_ref[:, own_columns],
+                sin_ref[:, own_columns],
+            ).astype(BF16)
+
+            def scores_at(index):
+                return dot32(k_rot[head, columns(index, block), :], query) * scale
+
+            def weighted(index, weights):
+                values = qkv_ref[head_rows(2, head), columns(index, block)]
+                return dot32(values, weights.astype(BF16))
+
+            scores = jnp.where(causal(block), scores_at(place), MASKED)
+            first_max = jnp.max(scores, axis=0, keepdims=True)
+            weights = jnp.exp(scores - first_max)
+            first_sum = jnp.sum(weights, axis=0, keepdims=True)
+
+            def step(index, carried):
+                running_max, running_sum, running_acc = carried
+                part = scores_at(index)
+                new_max = jnp.maximum(running_max, jnp.max(part, axis=0, keepdims=True))
+                part = jnp.exp(part - new_max)
+                factor = jnp.exp(running_max - new_max)
+                return (
+                    new_max,
+                    running_sum * factor + jnp.sum(part, axis=0, keepdims=True),
+                    running_acc * factor + weighted(index, part),
+                )
+
+            final_max, final_sum, final_acc = lax.fori_loop(
+                0, place, step, (first_max, first_sum, weighted(place, weights))
+            )
+            o_ref[columns(head, HEAD_DIM), own_columns] = (final_acc / final_sum).astype(BF16)
+            lse_ref[head, :, own_columns] = final_max + jnp.log(final_sum)
+            return 0
+
+        lax.fori_loop(0, heads, attend_head, 0)
+
+    def step(index, _):
+        place = length // block - 1 - index
+        attend_block(place)
+
+        def begin(part, _):
+            exchange.start(place * (block // seg) + part)
+            return 0
+
+        lax.fori_loop(0, block // seg, begin, 0)
+        return 0
+
+    lax.fori_loop(0, length // block, step, 0)
+    exchange.finish()
+    share.finish_share()
+    weights.finish_cross()
+
+
+def attend_grad_kernel(
+    block,
+    scale,
+    qkv_ref,
+    cos_ref,
+    sin_ref,
+    o_ref,
+    lse_ref,
+    ga_ref,
+    grad_ref,
+    got_ref,
+    go_feat,
+    q_feat,
+    q_rows,
+    k_feat,
+    go_rows,
+    delta,
+    dq_acc,
+    dk_acc,
+    dv_acc,
+    send_in,
+    recv_in,
+    local_in,
+    send,
+    recv,
+    local,
+):
+    heads, length, _ = q_rows.shape
+    wide = heads * HEAD_DIM
+    total, own = places()
+    seg = length // total
+    fs_count = lax.axis_size("fs")
+    greet_places()
+
+    def head_rows(kind, head):
+        return columns(kind * heads + head, HEAD_DIM)
+
+    def prepare(head, _):
+        rotated = turn(qkv_ref[head_rows(0, head), :].astype(F32), cos_ref[...], sin_ref[...])
+        q_feat[columns(head, HEAD_DIM), :] = rotated.astype(BF16)
+        q_rows[head] = rotated.T.astype(BF16)
+        rotated = turn(qkv_ref[head_rows(1, head), :].astype(F32), cos_ref[...], sin_ref[...])
+        k_feat[columns(head, HEAD_DIM), :] = rotated.astype(BF16)
+        return 0
+
+    arrival = Swap(
+        lambda place: ga_ref.at[
+            columns(place // fs_count, wide), columns(lax.rem(place, fs_count), seg)
+        ],
+        lambda place: go_feat.at[:, columns(place, seg)],
+        send_in,
+        recv_in,
+        local_in,
+    )
+    await_places()
+    arrival.start_all()
+    lax.fori_loop(0, heads, prepare, 0)
+    dq_acc[...] = jnp.zeros_like(dq_acc)
+    arrival.finish()
+
+    def prepare_grad(head, _):
+        grad = go_feat[columns(head, HEAD_DIM), :].astype(F32)
+        go_rows[head] = grad.T.astype(BF16)
+        delta[head] = jnp.sum(
+            grad * o_ref[columns(head, HEAD_DIM), :].astype(F32), axis=0, keepdims=True
+        )
+        return 0
+
+    lax.fori_loop(0, heads, prepare_grad, 0)
+    exchange = Swap(
+        lambda place: grad_ref.at[:, columns(place, seg)],
+        lambda place: got_ref.at[
+            columns(place // fs_count, 3 * wide), columns(lax.rem(place, fs_count), seg)
+        ],
+        send,
+        recv,
+        local,
+    )
+    count = length // block
+
+    def key_block(place, _):
+        own_columns = columns(place, block)
+        own_cos, own_sin = cos_ref[:, own_columns], sin_ref[:, own_columns]
+
+        def key_head(head, _):
+            rows = columns(head, HEAD_DIM)
+            key_feat = k_feat[rows, own_columns]
+            key_rows = key_feat.astype(F32).T.astype(BF16)
+            value_rows = qkv_ref[head_rows(2, head), own_columns].astype(F32).T.astype(BF16)
+
+            def terms(index, masked):
+                here = columns(index, block)
+                scores = dot32(key_rows, q_feat[rows, here]) * scale
+                weights = jnp.exp(scores - lse_ref[head, :, here])
+                if masked:
+                    weights = jnp.where(causal(block), weights, 0.0)
+                reach = dot32(value_rows, go_feat[rows, here])
+                slopes = (weights * (reach - delta[head, :, here]) * scale).astype(BF16)
+                dq_acc[rows, here] += dot32(key_feat, slopes)
+                part_key = dot32(slopes, q_rows[head, here, :])
+                part_value = dot32(weights.astype(BF16), go_rows[head, here, :])
+                return part_key, part_value
+
+            dk_acc[...], dv_acc[...] = terms(place, True)
+
+            def step(index, _):
+                part_key, part_value = terms(index, False)
+                dk_acc[...] += part_key
+                dv_acc[...] += part_value
+                return 0
+
+            lax.fori_loop(place + 1, count, step, 0)
+            grad_ref[head_rows(0, head), own_columns] = turn_back(
+                dq_acc[rows, own_columns], own_cos, own_sin
+            ).astype(BF16)
+            grad_ref[head_rows(1, head), own_columns] = turn_back(
+                dk_acc[...].T, own_cos, own_sin
+            ).astype(BF16)
+            grad_ref[head_rows(2, head), own_columns] = dv_acc[...].T.astype(BF16)
+            return 0
+
+        lax.fori_loop(0, heads, key_head, 0)
+
+        def begin(part, _):
+            exchange.start(place * (block // seg) + part)
+            return 0
+
+        lax.fori_loop(0, block // seg, begin, 0)
+        return 0
+
+    lax.fori_loop(0, count, key_block, 0)
+    exchange.finish()
+
+
+def attention_block(length, seg):
+    return math.gcd(length, 4 * seg)
+
+
+def attend(qkv, cosine, sine, crossed, shard, heads, score_scale):
+    length = qkv.shape[1]
+    total = lax.axis_size("sp") * lax.axis_size("fs")
+    seg = length // total
+    wide = heads * HEAD_DIM
+    tokens_here = lax.axis_size("fs") * seg
+    return pl.pallas_call(
+        functools.partial(attend_kernel, attention_block(length, seg), score_scale),
+        in_specs=[VMEM_WHOLE] * 3 + [IN_PLACE] * 2,
+        out_specs=[VMEM_WHOLE] * 2 + [IN_PLACE] * 3,
+        out_shape=[
+            jax.ShapeDtypeStruct((wide, length), BF16),
+            jax.ShapeDtypeStruct((heads, 1, length), F32),
+            jax.ShapeDtypeStruct((lax.axis_size("sp") * wide, tokens_here), BF16),
+            jax.ShapeDtypeStruct(crossed.shape, crossed.dtype),
+            jax.ShapeDtypeStruct(shard.shape, shard.dtype),
+        ],
+        input_output_aliases={3: 3},
+        scratch_shapes=[pltpu.VMEM((heads, length, HEAD_DIM), BF16)]
+        + swap_semaphores(total)
+        + share_scratch()
+        + cross_scratch(shard),
+        compiler_params=remote_params(1),
+        cost_estimate=pl.CostEstimate(
+            flops=30_000_000_000, bytes_accessed=4_000_000, transcendentals=0
+        ),
+        name="attend",
+    )(qkv, cosine, sine, crossed, shard)
+
+
+def attend_grad(qkv, cosine, sine, out, lse, grad_attended, heads, score_scale):
+    length = qkv.shape[1]
+    total = lax.axis_size("sp") * lax.axis_size("fs")
+    seg = length // total
+    block = attention_block(length, seg)
+    wide = heads * HEAD_DIM
+    tokens_here = lax.axis_size("fs") * seg
+    return pl.pallas_call(
+        functools.partial(attend_grad_kernel, block, score_scale),
+        in_specs=[VMEM_WHOLE] * 6,
+        out_specs=[VMEM_WHOLE, IN_PLACE],
+        out_shape=[
+            jax.ShapeDtypeStruct((3 * wide, length), BF16),
+            jax.ShapeDtypeStruct((lax.axis_size("sp") * 3 * wide, tokens_here), BF16),
+        ],
+        scratch_shapes=[
+            pltpu.VMEM((wide, length), BF16),
+            pltpu.VMEM((wide, length), BF16),
+            pltpu.VMEM((heads, length, HEAD_DIM), BF16),
+            pltpu.VMEM((wide, length), BF16),
+            pltpu.VMEM((heads, length, HEAD_DIM), BF16),
+            pltpu.VMEM((heads, 1, length), F32),
+            pltpu.VMEM((wide, length), F32),
+            pltpu.VMEM((block, HEAD_DIM), F32),
+            pltpu.VMEM((block, HEAD_DIM), F32),
+        ]
+        + swap_semaphores(total)
+        + swap_semaphores(total),
+        compiler_params=remote_params(2),
+        cost_estimate=pl.CostEstimate(
+            flops=60_000_000_000, bytes_accessed=8_000_000, transcendentals=0
+        ),
+        name="attend_grad",
+    )(qkv, cosine, sine, out, lse, grad_attended)
+
+
+def slope_of(gate_val, sigmoid):
+    return sigmoid * (1.0 + gate_val * (1.0 - sigmoid))
+
+
+def dispatch_kernel(
+    rows_ref,
+    note_ref,
+    crossed_ref,
+    shard_ref,
+    got_ref,
+    got_note_ref,
+    shared_ref,
+    full_ref,
+    send,
+    recv,
+    local,
+    send_note,
+    recv_note,
+    local_note,
+    dp_send,
+    dp_recv,
+    last_dp_send,
+    last_dp_recv,
+    *cross,
+):
+    greet_places()
+    greet_dp()
+    rows = Swap(
+        lambda place: rows_ref.at[place], lambda place: got_ref.at[place], send, recv, local
+    )
+    notes = Swap(
+        lambda place: note_ref.at[place],
+        lambda place: got_note_ref.at[place],
+        send_note,
+        recv_note,
+        local_note,
+    )
+    await_places(1)
+    weights = crossing(shard_ref, full_ref, *cross)
+    weights.start_cross()
+    share = sharing(shared_ref, dp_send, dp_recv)
+    share.start_share()
+    notes.start_all()
+    rows.start_all()
+    weights.finish_cross()
+    last = sharing(full_ref, last_dp_send, last_dp_recv)
+    last.start_share()
+    notes.finish()
+    share.finish_share()
+    rows.finish()
+    last.finish_share()
+
+
+def dispatch(sent, note, crossed, shard):
+    total = sent.shape[0]
+    return pl.pallas_call(
+        dispatch_kernel,
+        in_specs=[IN_PLACE] * 4,
+        out_specs=[IN_PLACE] * 4,
+        out_shape=[
+            jax.ShapeDtypeStruct(array.shape, array.dtype)
+            for array in (sent, note, crossed, shard)
+        ],
+        input_output_aliases={2: 2},
+        scratch_shapes=swap_semaphores(total)
+        + swap_semaphores(total)
+        + share_scratch()
+        + share_scratch()
+        + cross_scratch(shard),
+        compiler_params=remote_params(3),
+        cost_estimate=pl.CostEstimate(
+            flops=40_000_000_000, bytes_accessed=20_000_000, transcendentals=0
+        ),
+        name="dispatch",
+    )(sent, note, crossed, shard)
+
+
+def expert_kernel(
+    x_ref,
+    c_ref,
+    note_ref,
+    gate_ref,
+    up_ref,
+    down_ref,
+    own_x_ref,
+    own_g_ref,
+    own_gate_ref,
+    own_up_ref,
+    own_down_ref,
+    y_ref,
+    dgate_ref,
+    dup_ref,
+    ddown_ref,
+    own_y_ref,
+    own_gx_ref,
+    own_dgate_ref,
+    own_dup_ref,
+    own_ddown_ref,
+    got_ref,
+    got_note_ref,
+    x_feat,
+    g_feat,
+    gate_of_row,
+    acc,
+    dots,
+    hidden_all,
+    gate_all,
+    up_all,
+    gx_send,
+    dots_send,
+    own_x_feat,
+    send,
+    recv,
+    local,
+    send_note,
+    recv_note,
+    local_note,
+):
+    step = pl.program_id(0)
+    tiles = pl.num_programs(0) // 3
+    total, cap, width = gx_send.shape
+    tile = hidden_all.shape[2]
+    lanes = dots.shape[1]
+    rows = Swap(
+        lambda place: gx_send.at[place], lambda place: got_ref.at[place], send, recv, local
+    )
+    notes = Swap(
+        lambda place: dots_send.at[place],
+        lambda place: got_note_ref.at[place],
+        send_note,
+        recv_note,
+        local_note,
+    )
+
+    def block(place):
+        return slice(place * cap, (place + 1) * cap)
+
+    @pl.when(step == 0)
+    def _():
+        greet_places()
+        x_feat[...] = x_ref[...].T
+        for place in range(total):
+            gate_of_row[block(place), :] = jnp.broadcast_to(
+                note_ref[place].T[:cap, 0:1], (cap, lanes)
+            )
+        grads = gate_of_row[:, 0:1] * c_ref[...].astype(F32)
+        g_feat[...] = grads.astype(BF16).T
+        acc[...] = jnp.zeros_like(acc)
+        dots[...] = jnp.zeros_like(dots)
+        await_places()
+
+    @pl.when(step < tiles)
+    def _():
+        gate_val = dot32(x_ref[...], gate_ref[...])
+        up_val = dot32(x_ref[...], up_ref[...])
+        sigmoid = jax.nn.sigmoid(gate_val)
+        swished = gate_val * sigmoid
+        hidden = (swished * up_val).astype(BF16)
+        reach = dot32(c_ref[...], down_ref[...])
+        product = hidden.astype(F32) * reach
+        for part in range(tile // lanes):
+            dots[...] += product[:, part * lanes : (part + 1) * lanes]
+        grad_hidden = gate_of_row[:, 0:1] * reach
+        gate_part = (grad_hidden * up_val * slope_of(gate_val, sigmoid)).astype(BF16)
+        up_part = (grad_hidden * swished).astype(BF16)
+        acc[...] += dot_nt(gate_part, gate_ref[...]) + dot_nt(up_part, up_ref[...])
+        hidden_all[step] = hidden
+        gate_all[step] = gate_part
+        up_all[step] = up_part
+
+    @pl.when(step == tiles - 1)
+    def _():
+        for place in range(total):
+            gx_send[place] = acc[block(place), :].astype(BF16)
+            dots_send[place, 0:1, :cap] = jnp.sum(dots[block(place), :].T, axis=0, keepdims=True)
+        acc[...] = jnp.zeros_like(acc)
+        rows.start_all()
+        notes.start_all()
+
+    @pl.when((step >= tiles) & (step < 2 * tiles))
+    def _():
+        here = step - tiles
+        hidden = hidden_all[here]
+        acc[...] += dot_nt(hidden, down_ref[...])
+        ddown_ref[...] = dot32(g_feat[...], hidden).astype(BF16)
+        dgate_ref[...] = dot32(x_feat[...], gate_all[here]).astype(BF16)
+        dup_ref[...] = dot32(x_feat[...], up_all[here]).astype(BF16)
+
+    @pl.when(step == 2 * tiles - 1)
+    def _():
+        for place in range(total):
+            y_ref[place] = (gate_of_row[block(place), 0:1] * acc[block(place), :]).astype(BF16)
+        own_x_feat[...] = own_x_ref[...].T
+        own_y_ref[...] = jnp.zeros_like(own_y_ref)
+        own_gx_ref[...] = jnp.zeros_like(own_gx_ref)
+
+    @pl.when(step >= 2 * tiles)
+    def _():
+        gate_val = dot32(own_x_ref[...], own_gate_ref[...])
+        up_val = dot32(own_x_ref[...], own_up_ref[...])
+        sigmoid = jax.nn.sigmoid(gate_val)
+        swished = gate_val * sigmoid
+        hidden = swished * up_val
+        hidden_low = hidden.astype(BF16)
+        grad_hidden = dot_nt(own_g_ref[...], own_down_ref[...])
+        gate_part = (grad_hidden * up_val * slope_of(gate_val, sigmoid)).astype(BF16)
+        up_part = (grad_hidden * swished).astype(BF16)
+        own_y_ref[...] += dot32(hidden_low, own_down_ref[...])
+        own_gx_ref[...] += dot_nt(gate_part, own_gate_ref[...]) + dot_nt(up_part, own_up_ref[...])
+        own_ddown_ref[...] = dot32(hidden.T.astype(BF16), own_g_ref[...]).astype(BF16)
+        own_dgate_ref[...] = dot32(own_x_feat[...], gate_part).astype(BF16)
+        own_dup_ref[...] = dot32(own_x_feat[...], up_part).astype(BF16)
+
+    @pl.when(step == 3 * tiles - 1)
+    def _():
+        rows.finish()
+        notes.finish()
+
+
+def expert_pass(rows, cots, note, gate, up, down, own_x, own_g, own_gate, own_up, own_down):
+    total, cap, width = rows.shape
+    count = total * cap
+    hidden = gate.shape[1]
+    tile = 256
+    tiles = hidden // tile
+    own_tile = own_gate.shape[1] // tiles
+    own_count = own_x.shape[0]
+    lanes = note.shape[2]
+    once = pl.Buffered(1)
+    whole = pl.BlockSpec((count, width), lambda i: (0, 0), pipeline_mode=once)
+    whole_note = pl.BlockSpec(note.shape, lambda i: (0, 0, 0), pipeline_mode=once)
+    whole_own = pl.BlockSpec((own_count, width), lambda i: (0, 0), pipeline_mode=once)
+    early = pl.BlockSpec((width, tile), lambda i: (0, jnp.minimum(i, tiles - 1)))
+    both = pl.BlockSpec(
+        (width, tile), lambda i: (0, jnp.where(i < 2 * tiles, lax.rem(i, tiles), tiles - 1))
+    )
+    late = pl.BlockSpec((width, tile), lambda i: (0, jnp.clip(i - tiles, 0, tiles - 1)))
+    last = pl.BlockSpec((width, own_tile), lambda i: (0, jnp.maximum(i - 2 * tiles, 0)))
+    last_flat = pl.BlockSpec((own_tile, width), lambda i: (jnp.maximum(i - 2 * tiles, 0), 0))
+    return pl.pallas_call(
+        expert_kernel,
+        grid=(3 * tiles,),
+        in_specs=[whole, whole, whole_note, early, early, both]
+        + [whole_own, whole_own, last, last, last_flat],
+        out_specs=[pl.BlockSpec(rows.shape, lambda i: (0, 0, 0), pipeline_mode=once)]
+        + [late] * 3
+        + [whole_own, whole_own, last, last, last_flat]
+        + [IN_PLACE] * 2,
+        out_shape=[jax.ShapeDtypeStruct(rows.shape, BF16)]
+        + [jax.ShapeDtypeStruct((width, hidden), BF16)] * 3
+        + [jax.ShapeDtypeStruct((own_count, width), F32)] * 2
+        + [jax.ShapeDtypeStruct(own_gate.shape, BF16)] * 2
+        + [
+            jax.ShapeDtypeStruct(own_down.shape, BF16),
+            jax.ShapeDtypeStruct(rows.shape, BF16),
+            jax.ShapeDtypeStruct(note.shape, F32),
+        ],
+        scratch_shapes=[
+            pltpu.VMEM((width, count), BF16),
+            pltpu.VMEM((width, count), BF16),
+            pltpu.VMEM((count, lanes), F32),
+            pltpu.VMEM((count, width), F32),
+            pltpu.VMEM((count, lanes), F32),
+            pltpu.VMEM((tiles, count, tile), BF16),
+            pltpu.VMEM((tiles, count, tile), BF16),
+            pltpu.VMEM((tiles, count, tile), BF16),
+            pltpu.VMEM(rows.shape, BF16),
+            pltpu.VMEM(note.shape, F32),
+            pltpu.VMEM((width, own_count), BF16),
+        ]
+        + swap_semaphores(total)
+        + swap_semaphores(total),
+        compiler_params=remote_params(4),
+        cost_estimate=pl.CostEstimate(
+            flops=80_000_000_000, bytes_accessed=30_000_000, transcendentals=0
+        ),
+        name="expert_pass",
+    )(
+        rows.reshape(count, width),
+        cots.reshape(count, width),
+        note,
+        gate,
+        up,
+        down,
+        own_x,
+        own_g,
+        own_gate,
+        own_up,
+        own_down,
+    )
+
+
+def swap_sum(value, axis):
+    if lax.axis_size(axis) == 2:
+        other = lax.ppermute(value, axis, [(0, 1), (1, 0)])
+        return value.astype(F32) + other.astype(F32)
+    return lax.psum(value, axis).astype(F32)
+
+
+def exchange(chunks):
+    return lax.all_to_all(chunks, ("sp", "fs"), split_axis=0, concat_axis=0, tiled=True)
+
+
+def per_device_split(
+    tokens,
+    expert_ids,
+    fill_order,
+    attention_gain,
+    query_weight,
+    key_weight,
+    value_weight,
+    output_weight,
+    mixer_gain,
+    router_weight,
+    shared_gate,
+    shared_up,
+    shared_down,
+    expert_gate,
+    expert_up,
+    expert_down,
+    cotangent,
+):
+    seq_count, seg_rows, width = tokens.shape
+    token_count = seq_count * seg_rows
+    fs_count = lax.axis_size("fs")
+    sp_count = lax.axis_size("sp")
+    place_count = fs_count * sp_count
+    local_heads = HEADS // sp_count
+    flat_width = local_heads * HEAD_DIM
+    score_scale = HEAD_DIM ** (-0.5)
+    length = place_count * seg_rows
+    shard_rows = query_weight.shape[0]
+    qkv_width = 3 * flat_width
+    shared_width = shared_gate.shape[1]
+
+    choices = expert_ids.reshape(token_count, TOPK)
+    expert_onehot = choices[:, :, None] == jnp.arange(EXPERTS, dtype=jnp.int32)[None, None, :]
+    onehot_float = expert_onehot.astype(F32)
+
+    fill_rank = fill_order.reshape(token_count)
+    earlier = (fill_rank[None, :] < fill_rank[:, None]).astype(BF16)
+    per_token = jnp.sum(onehot_float, axis=1).astype(BF16)
+    counts = dot32(earlier, per_token)
+    slot_ranks = jnp.sum(counts[:, None, :] * onehot_float, axis=2).astype(jnp.int32)
+    group = EXPERTS // fs_count
+    holder = (choices % group) * fs_count + choices // group
+    slots = jnp.where(slot_ranks < CAP, holder * CAP + slot_ranks, -1)
+    slot_total = CAP * EXPERTS
+    slot_ids = jnp.arange(slot_total, dtype=jnp.int32)
+    takes_a = slot_ids[:, None] == slots[None, :, 0]
+    takes_b = slot_ids[:, None] == slots[None, :, 1]
+    taking = (takes_a | takes_b).astype(BF16)
+    cot_rows = cotangent.reshape(token_count, width)
+    cot_outgoing = dot32(taking, cot_rows).astype(BF16).reshape(place_count, CAP, width)
+    grouped = jnp.stack([query_weight, key_weight, value_weight], axis=1)
+    grouped = grouped.reshape(shard_rows, 3, sp_count, flat_width)
+    small = jnp.concatenate([attention_gain[:, None], mixer_gain[:, None], router_weight], axis=1)
+    grouped = jnp.transpose(grouped, (2, 0, 1, 3)).reshape(sp_count, shard_rows, qkv_width)
+    pack_width = -(-(qkv_width + small.shape[1]) // LANES) * LANES
+    pack = jnp.concatenate(
+        [
+            grouped,
+            jnp.broadcast_to(small[None], (sp_count,) + small.shape),
+            jnp.zeros((sp_count, shard_rows, pack_width - qkv_width - small.shape[1]), BF16),
+        ],
+        axis=2,
+    )
+    seq_tokens, own_pack, gate_crossed = gather_start(tokens, pack, expert_gate)
+    seq_tokens = seq_tokens.reshape(length, width)
+    own_pack = own_pack.reshape(width, pack_width)
+    qkv_own = own_pack[:, :qkv_width]
+    gain_one = own_pack[:, qkv_width].astype(F32)
+    gain_two = own_pack[:, qkv_width + 1].astype(F32)
+    router_full = own_pack[:, qkv_width + 2 : qkv_width + 2 + EXPERTS]
+
+    def gather_all(shard):
+        return lax.all_gather(shard, ("sp", "fs"), axis=0, tiled=True)
+
+    output_full = gather_all(output_weight)
+    shared_pack, shared_down_sent, cot_sent, seq_tokens = lax.optimization_barrier(
+        (
+            jnp.concatenate([shared_gate, shared_up], axis=1),
+            shared_down,
+            cot_outgoing,
+            seq_tokens,
+        )
+    )
+    arrived_cots = exchange(cot_sent)
+    shared_pack = gather_all(shared_pack)
+    shared_down_full = gather_all(shared_down_sent)
+    shared_gate_full = shared_pack[:, :shared_width]
+    shared_up_full = shared_pack[:, shared_width:]
+
+    half = HEAD_DIM // 2
+    frequency = 10000.0 ** (-jnp.arange(half, dtype=F32) / half)
+    angles = frequency[:, None] * jnp.arange(length, dtype=jnp.int32).astype(F32)[None, :]
+    cosine, sine = jnp.cos(angles), jnp.sin(angles)
+
+    normed_seq = norm_apply(seq_tokens.astype(F32), gain_one).astype(BF16)
+    qkv = jnp.einsum("de,ld->el", qkv_own, normed_seq, preferred_element_type=F32).astype(BF16)
+    out_heads, lse, attended, gate_own, up_crossed = attend(
+        qkv, cosine, sine, gate_crossed, expert_up, local_heads, score_scale
+    )
+    residual = tokens.astype(F32).reshape(token_count, width)
+
+    def outer(left, right):
+        return lax.dot_general(left, right, (((0,), (0,)), ((), ())), preferred_element_type=F32)
+
+    middle = residual + outer(attended, output_full)
+    mixed_in = norm_apply(middle, gain_two).astype(BF16)
+
+    logits = dot32(mixed_in, router_full)
+    def gate_values(raw_logits):
+        shifted = jnp.exp(raw_logits - jnp.max(raw_logits, axis=-1, keepdims=True))
+        router_probs = shifted / jnp.sum(shifted, axis=-1, keepdims=True)
+        picked = jnp.sum(router_probs[:, None, :] * onehot_float, axis=2)
+        return picked / jnp.sum(picked, axis=1, keepdims=True)
+
+    gate_weights, gate_pull = jax.vjp(gate_values, logits)
+
+    gate_of_slot = jnp.sum(
+        jnp.where(takes_a, gate_weights[None, :, 0], 0.0)
+        + jnp.where(takes_b, gate_weights[None, :, 1], 0.0),
+        axis=1,
+    )
+    outgoing = dot32(taking, mixed_in).astype(BF16)
+    note = jnp.pad(
+        gate_of_slot.reshape(place_count, 1, CAP), ((0, 0), (0, NOTE_ROWS - 1), (0, LANES - CAP))
+    )
+    rows, notes, up_own, down_own = dispatch(
+        outgoing.reshape(place_count, CAP, width), note, up_crossed, expert_down
+    )
+    qkv_pack, rows = lax.optimization_barrier(
+        (jnp.transpose(grouped, (1, 0, 2)).reshape(shard_rows, sp_count * qkv_width), rows)
+    )
+    qkv_full = gather_all(qkv_pack)
+    (
+        expert_out,
+        dgate,
+        dup,
+        ddown,
+        shared_out,
+        grad_mixed_shared,
+        grad_shared_gate,
+        grad_shared_up,
+        grad_shared_down,
+        grad_returned,
+        dots,
+    ) = expert_pass(
+        rows,
+        arrived_cots,
+        notes,
+        gate_own.reshape(width, -1),
+        up_own.reshape(width, -1),
+        down_own.reshape(width, -1),
+        mixed_in,
+        cot_rows,
+        shared_gate_full,
+        shared_up_full,
+        shared_down_full,
+    )
+    returned = exchange(expert_out).reshape(slot_total, width)
+    grad_returned = grad_returned.reshape(slot_total, width)
+    dots = dots[:, 0, :CAP].reshape(slot_total)
+
+    sp_place = lax.axis_index("sp")
+    part_rows = width // sp_count
+
+    def partner(step):
+        return lax.bitwise_xor(sp_place, step)
+
+    def rows_of(grad, step):
+        return lax.dynamic_slice_in_dim(grad, partner(step) * part_rows, part_rows, 0)
+
+    def to_sp(value, step):
+        return lax.ppermute(value, "sp", [(i, i ^ step) for i in range(sp_count)])
+
+    def to_dp(value):
+        return lax.ppermute(value, "dp", [(0, 1), (1, 0)])
+
+    def placed(parts):
+        whole = jnp.zeros((sp_count,) + parts[0].shape, F32)
+        for step, part in enumerate(parts):
+            whole = lax.dynamic_update_slice(whole, part[None], (partner(step), 0, 0))
+        return whole
+
+    def sum_then_spread(grad):
+        other = to_dp(grad)
+        sums = [
+            rows_of(grad, step).astype(F32) + rows_of(other, step).astype(F32)
+            for step in range(sp_count)
+        ]
+        moved = [to_sp(sums[step].astype(BF16), step).astype(F32) for step in range(1, sp_count)]
+        return placed([sums[0]] + moved)
+
+    def spread_then_sum(grad):
+        parts = [rows_of(grad, 0)] + [
+            to_sp(rows_of(grad, step), step) for step in range(1, sp_count)
+        ]
+        return placed([part.astype(F32) + to_dp(part).astype(F32) for part in parts])
+
+    sum_gate, sum_up, sum_down = (
+        spread_then_sum(dgate),
+        spread_then_sum(dup),
+        sum_then_spread(ddown),
+    )
+
+    grad_result = cot_rows.astype(F32)
+    output = (middle + shared_out + outer(taking, returned)).astype(BF16)
+    grad_gates = jnp.stack(
+        [
+            jnp.sum(jnp.where(slots[:, j : j + 1] == slot_ids[None, :], dots[None, :], 0.0), axis=1)
+            for j in range(TOPK)
+        ],
+        axis=1,
+    )
+    (grad_logits,) = gate_pull(grad_gates)
+    grad_logits = grad_logits.astype(BF16)
+    grad_router = outer(mixed_in, grad_logits)
+    grad_mixed = (
+        outer(taking, grad_returned) + dot_nt(grad_logits, router_full) + grad_mixed_shared
+    )
+    _, norm_two_pull = jax.vjp(norm_apply, middle, gain_two)
+    grad_middle_part, grad_gain_two = norm_two_pull(grad_mixed)
+    grad_middle = grad_result + grad_middle_part
+    grad_proj = grad_middle.astype(BF16)
+    grad_output_matrix = dot32(attended, grad_proj)
+    grad_attended = dot_nt(output_full, grad_proj).astype(BF16)
+    dqkv, token_grads = attend_grad(
+        qkv, cosine, sine, out_heads, lse, grad_attended, local_heads, score_scale
+    )
+    grad_qkv_matrix = jnp.einsum("ld,el->de", normed_seq, dqkv, preferred_element_type=F32)
+    grad_normed = jnp.einsum("et,de->td", token_grads, qkv_full, preferred_element_type=F32)
+    _, norm_one_pull = jax.vjp(norm_apply, residual, gain_one)
+    grad_residual_part, grad_gain_one = norm_one_pull(grad_normed)
+    grad_tokens = grad_middle + grad_residual_part
+
+    def column(vector, columns):
+        return jnp.pad(vector[:, None], ((0, 0), (0, columns - 1)))
+
+    dense = jnp.concatenate(
+        [
+            grad_output_matrix.astype(BF16),
+            grad_shared_gate,
+            grad_shared_up,
+            grad_router.astype(BF16),
+            column(grad_gain_two, 128 - EXPERTS).astype(BF16),
+        ],
+        axis=1,
+    )
+    dense = lax.psum_scatter(dense, ("sp", "fs"), scatter_dimension=0, tiled=True)
+    own_shared_down = lax.psum_scatter(
+        grad_shared_down, ("sp", "fs"), scatter_dimension=0, tiled=True
+    )
+    tail = jnp.concatenate([grad_qkv_matrix, column(grad_gain_one, 128)], axis=1).astype(BF16)
+    tail = exchange(tail.reshape(place_count, shard_rows, tail.shape[1]))
+    tail = tail.reshape(sp_count, fs_count, shard_rows, tail.shape[2]).astype(F32)
+    tail = jnp.sum(tail, axis=1).astype(BF16)
+    sum_dense = swap_sum(dense, "dp")
+    sum_shared_down = swap_sum(own_shared_down, "dp")
+    sum_tail = swap_sum(tail, "dp")
+    sum_qkv = sum_tail[:, :, :qkv_width].reshape(sp_count, shard_rows, 3, flat_width)
+    sum_qkv = jnp.transpose(sum_qkv, (2, 1, 0, 3)).reshape(3, shard_rows, width)
+    sum_gain_one = jnp.sum(sum_tail[:, :, qkv_width], axis=0)
+    edge = width + 2 * shared_width
+    return (
+        output.reshape(tokens.shape),
+        grad_tokens.reshape(tokens.shape),
+        sum_gain_one,
+        sum_qkv[0],
+        sum_qkv[1],
+        sum_qkv[2],
+        sum_dense[:, :width],
+        sum_dense[:, edge + EXPERTS],
+        sum_dense[:, edge : edge + EXPERTS],
+        sum_dense[:, width : width + shared_width],
+        sum_dense[:, width + shared_width : edge],
+        sum_shared_down,
+        sum_gate,
+        sum_up,
+        sum_down,
+    )
+
+
+def per_device_any(*shards):
+    fs_count, sp_count = lax.axis_size("fs"), lax.axis_size("sp")
+    same = shards[0].shape[0] == fs_count and EXPERTS == 4 * fs_count
+    if same and sp_count == 4 and lax.axis_size("dp") == 2:
+        return per_device_split(*shards)
+    return per_device(*shards)
+
+
 def solution(mesh):
     placed = (
         P("dp", ("sp", "fs"), None),
@@ -569,7 +1975,7 @@
         P("dp", ("sp", "fs"), None),
     )
     return jax.shard_map(
-        per_device,
+        per_device_any,
         mesh=mesh,
         in_specs=placed,
         out_specs=(

time: 2250 us -> 769 us (0.34)
  waiting for transfers between devices: 1450 us -> 156 us
  Pallas kernels: 0 us -> 408 us
  matrix products: 316 us -> 39.3 us
  local copies, waits for them, and re-layouts: 181 us -> 52.3 us
  blocking collectives: 98.1 us -> 0 us
  other arithmetic: 99.5 us -> 54.2 us
    reduce_scatter x12 -> x2, waiting for transfers between devices: 755 us -> 0.01 us  [the longest x1 0.01 us: per_device_split(): lax.psum_scatter(grad_shared_down, ('sp', 'fs'), scatter_dimension=0, til...]
    pallas_call x0 -> x5, Pallas kernels: none -> 408 us  [the longest x1 123 us: attend_grad(): pl.pallas_call(functools.partial(attend_grad_kernel, block, score_scale),...]
    all_gather x12 -> x4, waiting for transfers between devices: 293 us -> 0.06 us  [gather_all(): return lax.all_gather(shard, ('sp', 'fs'), axis=0, tiled=True)]
    dot_general x62 -> x14, matrix products: 316 us -> 39.3 us  [the longest x4 9.73 us: outer(): lax.dot_general(left, right, (((0,), (0,)), ((), ())), preferred_element_...]
    psum x1 -> x0, waiting for transfers between devices: 199 us -> none  [per_device(): lax.psum(part_query.astype(jnp.bfloat16), 'dp').astype(jnp.float32)]
    ppermute x0 -> x21, waiting for transfers between devices: none -> 155 us  [the longest x9 94.7 us: to_dp(): return lax.ppermute(value, 'dp', [(0, 1), (1, 0)])]
    all_to_all x8 -> x3, waiting for transfers between devices: 150 us -> 0.01 us  [exchange(): lax.all_to_all(chunks, ('sp', 'fs'), split_axis=0, concat_axis=0, tiled=T...]
    unnamed x2 -> x0, blocking collectives: 61 us -> none
  transfers between devices with their start and end apart: 34 -> 30, of which waited for: 27 -> 9; matrix products, arithmetic and copies ran while one was open for 17% -> 19% of each run, Pallas kernels for 0% -> 54%
where the time goes in v2:
time: 769 us; the launch traced here: 762 us
  Pallas kernels  408 us (53%)
  waiting for transfers between devices  156 us (20%)
  other arithmetic  54.2 us (7%)
  local copies, waits for them, and re-layouts  52.3 us (7%)
  matrix products  39.3 us (5%)
  starting transfers between devices  37.1 us (5%)
  between operations  15.1 us (2%)
    pallas_call x1, Pallas kernels, attend_grad(): pl.pallas_call(functools.partial(attend_grad_kernel, block, score_scale),...  123 us
    ppermute x9, waiting for transfers between devices, to_dp(): return lax.ppermute(value, 'dp', [(0, 1), (1, 0)])  94.7 us
    pallas_call x1, Pallas kernels, expert_pass(): pl.pallas_call(expert_kernel, grid=(3 * tiles,), in_specs=[whole, whole,...  87.6 us
    pallas_call x1, Pallas kernels, attend(): pl.pallas_call(functools.partial(attend_kernel, attention_block(length, s...  82.7 us
    pallas_call x1, Pallas kernels, dispatch(): pl.pallas_call(dispatch_kernel, in_specs=[IN_PLACE] * 4, out_specs=[IN_PL...  64.1 us
    ppermute x9, waiting for transfers between devices, to_sp(): return lax.ppermute(value, 'sp', [(i, i ^ step) for i in range(sp_count)])  56.8 us
    pallas_call x1, Pallas kernels, gather_start(): pl.pallas_call(gather_kernel, in_specs=[IN_PLACE] * 3, out_specs=[IN_PLAC...  50 us
    dynamic_update_slice x12, other arithmetic, placed(): whole = lax.dynamic_update_slice(whole, part[None], (partner(step), 0, 0))  28.9 us
  transfers between devices with their start and end apart: 30, of which 9 were waited for; matrix products, arithmetic and copies ran while one was open for 19% of the time, Pallas kernels for 54%

profile of v2, /device:TPU:12, one launch (start us, length us, event | category | flops | bytes accessed | tf_op | source)
XLA Modules:
  0.0 761.7 jit_solution(8949906224035170168)
XLA Ops:
  20.2 50.0 %gather_start.1 = (bf16[4,4,128,768]{3,2,1,0:T(8,128)(2,1)}, bf16[4,4,48,640]{3,2,1,0:T(8,128)(2,1)}, bf16[4,192,2048]{2,1,0:T(8,128)(2,1)}) custom-call(bf16[4,128,768]{2,1,0:T(8,128)(2,1)} %tokens_ref.1, bf16[4,48,640]{2,1,0:T(8,128)(2,1)} %maximum_maximum_fusion.pack_ref, bf16[4,192,2048]{2,1,0:T(8,128)(2,1)} %shard_ref.3), custom_call_target="tpu_custom_call" | custom-call | flops 40000000000 | bytes 4000000 | tf_op jit(solution)/shard_map/gather_start/pallas_call | solution.py:1026
  70.2 8.0 %all-to-all-start = ((bf16[16,72,768]{2,1,0:T(8,128)(2,1)}), bf16[16,72,768]{2,1,0:T(8,128)(2,1)}, u32[]{:S(2)}, u32[]{:S(2)}) async-start(bf16[16,72,768]{2,1,0:T(8,128)(2,1)} %bitcast.10), calls=%async_computation | async-start | bytes 3538944 | tf_op jit(solution)/shard_map/all_to_all | solution.py:1665
  83.6 5.9 convolution_convert_fusion.2.qkv_ref
  91.3 82.7 %attend.1 = (bf16[192,2048]{1,0:T(8,128)(2,1)}, f32[3,1,2048]{2,1,0:T(1,128)}, bf16[768,512]{1,0:T(8,128)(2,1)}, bf16[4,192,2048]{2,1,0:T(8,128)(2,1)}, bf16[4,192,2048]{2,1,0:T(8,128)(2,1)}) custom-call(bf16[576,2048]{1,0:T(8,128)(2,1)} %convolution_convert_fusion.2.qkv_ref, ...), custom_call_target="tpu_custom_call", output_to_operand_aliasing={{3}: (3, {})} | custom-call | flops 30000001024 | bytes 4000000 | tf_op jit(solution)/shard_map/attend/pallas_call | solution.py:1305
  182.1 64.1 %dispatch.1 = (bf16[16,72,768]{2,1,0:T(8,128)(2,1)}, f32[16,8,128]{2,1,0:T(8,128)}, bf16[4,192,2048]{2,1,0:T(8,128)(2,1)}, bf16[4,192,2048]{2,1,0:T(8,128)(2,1)}) custom-call(bf16[16,72,768]{2,1,0:T(8,128)(2,1)} %bitcast.141, f32[16,8,128]{2,1,0:T(8,128)} %pad.14.note_ref, ...), custom_call_target="tpu_custom_call", output_to_operand_aliasing={{2}: (2, {})} | custom-call | flops 40000000000 | bytes 20000000 | tf_op jit(solution)/shard_map/dispatch/pallas_call | solution.py:1420
  246.8 6.7 fusion.35
  253.4 87.6 %expert_pass.1 = (bf16[16,72,768]{2,1,0:T(8,128)(2,1)}, bf16[768,2048]{1,0:T(8,128)(2,1)}, bf16[768,2048]{1,0:T(8,128)(2,1)}, bf16[768,2048]{1,0:T(8,128)(2,1)},...) custom-call(bf16[1152,768]{1,0:T(8,128)(2,1)} %bitcast.140, ...), custom_call_target="tpu_custom_call" | custom-call | flops 80000000000 | bytes 30000000 | tf_op jit(solution)/shard_map/expert_pass/pallas_call | solution.py:1604
  342.0 3.8 constant_dynamic-slice_fusion
  360.7 12.4 %concatenate.28 = bf16[768,4992]{1,0:T(8,128)(2,1)} concatenate(bf16[768,768]{1,0:T(8,128)(2,1)} %convolution_convert_fusion.3, bf16[768,2048]{1,0:T(8,128)(2,1)} %get-tuple-element.71, bf16[768,2048]{1,0:T(8,128)(2,1)} %get-tuple-element.72, bf16[768,16]{1,0:T(8,128)(2,1)S(1)} %copy.118, bf16[768,112]{1,0:T(8,128)(2,1)S(1)} %pad.16), dimensions={1} | concatenate | bytes 15335424 | tf_op jit(solution)/shard_map/concatenate | solution.py:1905
  376.0 123.2 %attend_grad.1 = (bf16[576,2048]{1,0:T(8,128)(2,1)}, bf16[2304,512]{1,0:T(8,128)(2,1)}) custom-call(bf16[576,2048]{1,0:T(8,128)(2,1)} %convolution_convert_fusion.2.qkv_ref, f32[32,2048]{1,0:T(8,128)} %get-tuple-element.186.cos_ref, f32[32,2048]{1,0:T(8,128)} %get-tuple-element.185.sin_ref, bf16[192,2048]{1,0:T(8,128)(2,1)} %get-tuple-element.66.o_ref, ...), custom_call_target="tpu_custom_call" | custom-call | flops 60000002048 | bytes 8000000 | tf_op jit(solution)/shard_map/attend_grad/pallas_call | solution.py:1336
  499.3 6.4 fusion.9
  513.7 8.6 %all-to-all-start.2 = ((bf16[16,48,704]{2,1,0:T(8,128)(2,1)}), bf16[16,48,704]{2,1,0:T(8,128)(2,1)}, u32[]{:S(2)}, u32[]{:S(2)}) async-start(bf16[16,48,704]{2,1,0:T(8,128)(2,1)} %pad_maximum_fusion), calls=%async_computation.2 | async-start | bytes 2359296 | tf_op jit(solution)/shard_map/all_to_all | solution.py:1665
  526.0 3.5 broadcast.144.clone.1
  542.1 4.4 collective-permute-done.12
  549.0 4.5 collective-permute-done.15
  553.5 17.1 %collective-permute-done.6 = bf16[192,2048]{1,0:T(8,128)(2,1)} collective-permute-done((bf16[192,2048]{1,0:T(8,128)(2,1)S(1)}, bf16[192,2048]{1,0:T(8,128)(2,1)}, u32[]{:S(2)}, u32[]{:S(2)}) %collective-permute-start.6) | collective-permute-done | bytes 786464 | tf_op jit(solution)/shard_map/ppermute | solution.py:1840
  570.6 16.6 %collective-permute-done.8 = bf16[192,2048]{1,0:T(8,128)(2,1)S(1)} collective-permute-done((bf16[192,2048]{1,0:T(8,128)(2,1)S(1)}, bf16[192,2048]{1,0:T(8,128)(2,1)S(1)}, u32[]{:S(2)}, u32[]{:S(2)}) %collective-permute-start.8) | collective-permute-done | bytes 786464 | tf_op jit(solution)/shard_map/ppermute | solution.py:1840
  591.7 6.8 all-to-all-start.1
  601.3 80.2 %collective-permute-done.7 = bf16[192,2048]{1,0:T(8,128)(2,1)} collective-permute-done((bf16[192,2048]{1,0:T(8,128)(2,1)}, bf16[192,2048]{1,0:T(8,128)(2,1)}, u32[]{:S(2)}, u32[]{:S(2)}) %collective-permute-start.7) | collective-permute-done | bytes 786464 | tf_op jit(solution)/shard_map/ppermute | solution.py:1843
  688.2 10.1 %collective-permute-done.9 = bf16[192,2048]{1,0:T(8,128)(2,1)} collective-permute-done((bf16[192,2048]{1,0:T(8,128)(2,1)S(1)}, bf16[192,2048]{1,0:T(8,128)(2,1)}, u32[]{:S(2)}, u32[]{:S(2)}) %collective-permute-start.9) | collective-permute-done | bytes 786464 | tf_op jit(solution)/shard_map/ppermute | solution.py:1843
  707.6 4.5 add_convert_fusion
  720.9 4.1 add_convert_fusion.3
  727.5 5.9 collective-permute-done.19
  736.7 12.7 %collective-permute-done.20 = bf16[192,2048]{1,0:T(8,128)(2,1)S(1)} collective-permute-done((bf16[192,2048]{1,0:T(8,128)(2,1)}, bf16[192,2048]{1,0:T(8,128)(2,1)S(1)}, u32[]{:S(2)}, u32[]{:S(2)}) %collective-permute-start.20) | collective-permute-done | bytes 786464 | tf_op jit(solution)/shard_map/ppermute | solution.py:1840
  (229 shorter events, 117.0 us)
Async XLA Ops:
  7.2 166.7 %all-gather.5.cloned.1.call-start = ((), (), s32[]{:S(2)}) async-start(), calls=%async_computation.5 | async-start | bytes 1253376 | tf_op jit(solution)/shard_map/all_gather | solution.py:1741
  8.0 238.8 %all-gather.7.cloned.1.call-start = ((), (), s32[]{:S(2)}) async-start(), calls=%async_computation.6 | async-start | bytes 6684672 | tf_op jit(solution)/shard_map/all_gather | solution.py:1741
  70.2 183.2 %all-to-all-start = ((bf16[16,72,768]{2,1,0:T(8,128)(2,1)}), bf16[16,72,768]{2,1,0:T(8,128)(2,1)}, u32[]{:S(2)}, u32[]{:S(2)}) async-start(bf16[16,72,768]{2,1,0:T(8,128)(2,1)} %bitcast.10), calls=%async_computation | async-start | bytes 3538944 | tf_op jit(solution)/shard_map/all_to_all | solution.py:1665
  78.2 175.2 %all-gather.9.cloned.1.call-start = ((), (), s32[]{:S(2)}) async-start(), calls=%async_computation.7 | async-start | bytes 3342336 | tf_op jit(solution)/shard_map/all_gather | solution.py:1741
  79.0 420.3 %all-gather.11.cloned.1.call-start = ((), (), s32[]{:S(2)}) async-start(), calls=%async_computation.8 | async-start | bytes 3760128 | tf_op jit(solution)/shard_map/all_gather | solution.py:1741
  246.2 488.5 %reduce-scatter.5.cloned.1.call-start = ((), (), s32[]{:S(2)}) async-start(), calls=%async_computation.10 | async-start | bytes 3342336 | tf_op jit(solution)/shard_map/reduce_scatter | solution.py:1916
  341.0 393.9 %reduce-scatter.3.cloned.1.call-start = ((), (), s32[]{:S(2)}) async-start(), calls=%async_computation.9 | async-start | bytes 8146944 | tf_op jit(solution)/shard_map/reduce_scatter | solution.py:1915
  345.7 179.9 %collective-permute-start.10 = (bf16[192,2048]{1,0:T(8,128)(2,1)}, bf16[192,2048]{1,0:T(8,128)(2,1)}, u32[]{:S(2)}, u32[]{:S(2)}) collective-permute-start(bf16[192,2048]{1,0:T(8,128)(2,1)} %get-tuple-element.172), channel_id=1, source_target_pairs={{0,16},{16,0},{1,17},{17,1},{2,18},{18,2},{3,19},{19,3},{4,20},{20... | collective-permute-start | bytes 2359304 | tf_op jit(solution)/shard_map/ppermute | solution.py:1843
  346.1 179.8 %collective-permute-start.11 = (bf16[192,2048]{1,0:T(8,128)(2,1)}, bf16[192,2048]{1,0:T(8,128)(2,1)}, u32[]{:S(2)}, u32[]{:S(2)}) collective-permute-start(bf16[192,2048]{1,0:T(8,128)(2,1)} %get-tuple-element.171), channel_id=1, source_target_pairs={{0,4},{4,0},{8,12},{12,8},{1,5},{5,1},{9,13},{13,9},{2,6},{6,2},{1... | collective-permute-start | bytes 2359304 | tf_op jit(solution)/shard_map/ppermute | solution.py:1840
  346.1 186.2 %collective-permute-start.13 = (bf16[192,2048]{1,0:T(8,128)(2,1)}, bf16[192,2048]{1,0:T(8,128)(2,1)}, u32[]{:S(2)}, u32[]{:S(2)}) collective-permute-start(bf16[192,2048]{1,0:T(8,128)(2,1)} %get-tuple-element.170), channel_id=1, source_target_pairs={{0,8},{4,12},{8,0},{12,4},{1,9},{5,13},{9,1},{13,5},{2,10},{6,14},... | collective-permute-start | bytes 2359304 | tf_op jit(solution)/shard_map/ppermute | solution.py:1840
  348.7 185.1 %collective-permute-start.3 = (bf16[192,2048]{1,0:T(8,128)(2,1)}, bf16[192,2048]{1,0:T(8,128)(2,1)}, u32[]{:S(2)}, u32[]{:S(2)}) collective-permute-start(bf16[192,2048]{1,0:T(8,128)(2,1)} %get-tuple-element.176), channel_id=1, source_target_pairs={{0,16},{16,0},{1,17},{17,1},{2,18},{18,2},{3,19},{19,3},{4,20},{20... | collective-permute-start | bytes 2359304 | tf_op jit(solution)/shard_map/ppermute | solution.py:1843
  350.3 183.7 %collective-permute-start.4 = (bf16[192,2048]{1,0:T(8,128)(2,1)}, bf16[192,2048]{1,0:T(8,128)(2,1)}, u32[]{:S(2)}, u32[]{:S(2)}) collective-permute-start(bf16[192,2048]{1,0:T(8,128)(2,1)} %get-tuple-element.175), channel_id=1, source_target_pairs={{0,4},{4,0},{8,12},{12,8},{1,5},{5,1},{9,13},{13,9},{2,6},{6,2},{1... | collective-permute-start | bytes 2359304 | tf_op jit(solution)/shard_map/ppermute | solution.py:1840
  513.7 78.0 %all-to-all-start.2 = ((bf16[16,48,704]{2,1,0:T(8,128)(2,1)}), bf16[16,48,704]{2,1,0:T(8,128)(2,1)}, u32[]{:S(2)}, u32[]{:S(2)}) async-start(bf16[16,48,704]{2,1,0:T(8,128)(2,1)} %pad_maximum_fusion), calls=%async_computation.2 | async-start | bytes 2359296 | tf_op jit(solution)/shard_map/all_to_all | solution.py:1665
  525.6 27.9 %collective-permute-start.15 = (bf16[192,2048]{1,0:T(8,128)(2,1)S(1)}, bf16[192,2048]{1,0:T(8,128)(2,1)S(1)}, u32[]{:S(2)}, u32[]{:S(2)}) collective-permute-start(bf16[192,2048]{1,0:T(8,128)(2,1)S(1)} %copy-done.9), channel_id=1, source_target_pairs={{0,12},{4,8},{8,4},{12,0},{1,13},{5,9},{9,5},{13,1},{2,14},{6,10},... | collective-permute-start | bytes 2359304 | tf_op jit(solution)/shard_map/ppermute | solution.py:1840
  532.3 38.3 %collective-permute-start.6 = (bf16[192,2048]{1,0:T(8,128)(2,1)S(1)}, bf16[192,2048]{1,0:T(8,128)(2,1)}, u32[]{:S(2)}, u32[]{:S(2)}) collective-permute-start(bf16[192,2048]{1,0:T(8,128)(2,1)S(1)} %copy-done.11), channel_id=1, source_target_pairs={{0,8},{4,12},{8,0},{12,4},{1,9},{5,13},{9,1},{13,5},{2,10},{6,14},... | collective-permute-start | bytes 2359304 | tf_op jit(solution)/shard_map/ppermute | solution.py:1840
  533.8 53.4 %collective-permute-start.8 = (bf16[192,2048]{1,0:T(8,128)(2,1)S(1)}, bf16[192,2048]{1,0:T(8,128)(2,1)S(1)}, u32[]{:S(2)}, u32[]{:S(2)}) collective-permute-start(bf16[192,2048]{1,0:T(8,128)(2,1)S(1)} %copy-done.10), channel_id=1, source_target_pairs={{0,12},{4,8},{8,4},{12,0},{1,13},{5,9},{9,5},{13,1},{2,14},{6,10},... | collective-permute-start | bytes 2359304 | tf_op jit(solution)/shard_map/ppermute | solution.py:1840
  534.0 53.2 %collective-permute-start.5 = (bf16[192,2048]{1,0:T(8,128)(2,1)}, bf16[192,2048]{1,0:T(8,128)(2,1)S(1)}, u32[]{:S(2)}, u32[]{:S(2)}) collective-permute-start(bf16[192,2048]{1,0:T(8,128)(2,1)} %collective-permute-done.4), channel_id=1, source_target_pairs={{0,16},{16,0},{1,17},{17,1},{2,18},{18,2},{3,19},{19,3},{4,20},{20... | collective-permute-start | bytes 2359304 | tf_op jit(solution)/shard_map/ppermute | solution.py:1843
  546.5 52.0 %collective-permute-start.14 = (bf16[192,2048]{1,0:T(8,128)(2,1)}, bf16[192,2048]{1,0:T(8,128)(2,1)}, u32[]{:S(2)}, u32[]{:S(2)}) collective-permute-start(bf16[192,2048]{1,0:T(8,128)(2,1)} %collective-permute-done.13), channel_id=1, source_target_pairs={{0,16},{16,0},{1,17},{17,1},{2,18},{18,2},{3,19},{19,3},{4,20},{20... | collective-permute-start | bytes 2359304 | tf_op jit(solution)/shard_map/ppermute | solution.py:1843
  553.5 154.1 %collective-permute-start.17 = (bf16[768,2048]{1,0:T(8,128)(2,1)}, bf16[768,2048]{1,0:T(8,128)(2,1)}, u32[]{:S(2)}, u32[]{:S(2)}) collective-permute-start(bf16[768,2048]{1,0:T(8,128)(2,1)} %get-tuple-element.76), channel_id=1, source_target_pairs={{0,16},{16,0},{1,17},{17,1},{2,18},{18,2},{3,19},{19,3},{4,20},{20... | collective-permute-start | bytes 9437192 | tf_op jit(solution)/shard_map/ppermute | solution.py:1843
  570.6 113.6 %collective-permute-start.16 = (bf16[192,2048]{1,0:T(8,128)(2,1)S(1)}, bf16[192,2048]{1,0:T(8,128)(2,1)}, u32[]{:S(2)}, u32[]{:S(2)}) collective-permute-start(bf16[192,2048]{1,0:T(8,128)(2,1)S(1)} %collective-permute-done.15), channel_id=1, source_target_pairs={{0,16},{16,0},{1,17},{17,1},{2,18},{18,2},{3,19},{19,3},{4,20},{20... | collective-permute-start | bytes 2359304 | tf_op jit(solution)/shard_map/ppermute | solution.py:1843
  587.2 94.3 %collective-permute-start.7 = (bf16[192,2048]{1,0:T(8,128)(2,1)}, bf16[192,2048]{1,0:T(8,128)(2,1)}, u32[]{:S(2)}, u32[]{:S(2)}) collective-permute-start(bf16[192,2048]{1,0:T(8,128)(2,1)} %collective-permute-done.6), channel_id=1, source_target_pairs={{0,16},{16,0},{1,17},{17,1},{2,18},{18,2},{3,19},{19,3},{4,20},{20... | collective-permute-start | bytes 2359304 | tf_op jit(solution)/shard_map/ppermute | solution.py:1843
  587.2 111.1 %collective-permute-start.9 = (bf16[192,2048]{1,0:T(8,128)(2,1)S(1)}, bf16[192,2048]{1,0:T(8,128)(2,1)}, u32[]{:S(2)}, u32[]{:S(2)}) collective-permute-start(bf16[192,2048]{1,0:T(8,128)(2,1)S(1)} %collective-permute-done.8), channel_id=1, source_target_pairs={{0,16},{16,0},{1,17},{17,1},{2,18},{18,2},{3,19},{19,3},{4,20},{20... | collective-permute-start | bytes 2359304 | tf_op jit(solution)/shard_map/ppermute | solution.py:1843
  591.7 129.2 %all-to-all-start.1 = ((bf16[16,72,768]{2,1,0:T(8,128)(2,1)}), bf16[16,72,768]{2,1,0:T(8,128)(2,1)}, u32[]{:S(2)}, u32[]{:S(2)}) async-start(bf16[16,72,768]{2,1,0:T(8,128)(2,1)} %get-tuple-element.62), calls=%async_computation.1 | async-start | bytes 3538944 | tf_op jit(solution)/shard_map/all_to_all | solution.py:1665
  714.3 35.2 %collective-permute-start.20 = (bf16[192,2048]{1,0:T(8,128)(2,1)}, bf16[192,2048]{1,0:T(8,128)(2,1)S(1)}, u32[]{:S(2)}, u32[]{:S(2)}) collective-permute-start(bf16[192,2048]{1,0:T(8,128)(2,1)} %get-tuple-element.164), channel_id=1, source_target_pairs={{0,12},{4,8},{8,4},{12,0},{1,13},{5,9},{9,5},{13,1},{2,14},{6,10},... | collective-permute-start | bytes 2359304 | tf_op jit(solution)/shard_map/ppermute | solution.py:1840
  (37 other events, 942.2 us)
Sparse Core Ops, SparseCore 0:
  10.4 46.9 all-gather.4
  70.4 98.8 all-gather.6
  171.5 66.7 all-gather.8
  246.3 47.4 all-gather.10
  341.2 74.8 reduce-scatter.4
  420.0 108.2 reduce-scatter.2

commit v3 on v2

--- a/solution.py
+++ b/solution.py
@@ -814,13 +814,64 @@
     )
 
 
+def route(ids_ref, fill_ref, slots_ref, taking_ref):
+    count = fill_ref.shape[1]
+    group = EXPERTS // lax.axis_size("fs")
+    fill_row = fill_ref[...].astype(F32)
+    fill_column = jnp.broadcast_to(fill_row, (8, count)).T[:, 0:1]
+    earlier = (fill_column < fill_row).astype(BF16)
+    experts = lax.broadcasted_iota(jnp.int32, (EXPERTS, count), 0)
+    named = [(experts == ids_ref[j : j + 1, :]).astype(F32) for j in range(TOPK)]
+    counts = dot32((named[0] + named[1]).astype(BF16), earlier)
+    slots = []
+    for j in range(TOPK):
+        rank = jnp.sum(counts * named[j], axis=0, keepdims=True).astype(jnp.int32)
+        choice = ids_ref[j : j + 1, :]
+        holder = lax.rem(choice, group) * lax.axis_size("fs") + choice // group
+        slots.append(jnp.where(rank < CAP, holder * CAP + rank, -1))
+        slots_ref[j : j + 1, :] = slots[j]
+    total = taking_ref.shape[0]
+    half = total // 2
+    for start in (0, half):
+        slot_ids = start + lax.broadcasted_iota(jnp.int32, (half, count), 0)
+        taken = (slot_ids == slots[0]) | (slot_ids == slots[1])
+        taking_ref[start : start + half, :] = taken.astype(F32).astype(BF16)
+
+
+def spread_rows(taking_ref, rows_ref, out_ref):
+    total, cap, _ = out_ref.shape
+    half = total // 2
+    for first in (0, half):
+        rows = dot32(taking_ref[first * cap : (first + half) * cap, :], rows_ref[...])
+        for place in range(half):
+            out_ref[first + place] = rows[place * cap : (place + 1) * cap].astype(BF16)
+
+
+def cot_swap(source, target, rows, send, recv, local):
+    return Swap(
+        lambda place: source.at[place, rows], lambda place: target.at[place, rows], send, recv, local
+    )
+
+
 def gather_kernel(
+    first_rows,
     tokens_ref,
-    pack_ref,
+    query_ref,
+    key_ref,
+    value_ref,
+    small_ref,
+    ids_ref,
+    fill_ref,
+    cot_ref,
     shard_ref,
     seq_ref,
     got_ref,
     full_ref,
+    slots_ref,
+    taking_ref,
+    cot_out_ref,
+    cots_ref,
+    pack_ref,
     z_send,
     z_recv,
     core_send,
@@ -836,22 +887,21 @@
     down_send,
     down_recv,
     local,
+    cot_send,
+    cot_recv,
+    cot_local,
     *cross,
 ):
     fs_count, sp_count = lax.axis_size("fs"), lax.axis_size("sp")
     fs_place, sp_place = lax.axis_index("fs"), lax.axis_index("sp")
     core = sp_place + 1 - 2 * lax.rem(sp_place, 2)
     across = lax.rem(sp_place + 2, sp_count)
-    barrier = pltpu.get_barrier_semaphore()
 
     def fs_peer(step):
         return lax.rem(fs_place + step, fs_count)
 
     def sp_peer(step):
         return lax.rem(sp_place + step, sp_count)
-
-    def greet(where):
-        pl.semaphore_signal(barrier, inc=1, device_id=where, device_id_type=pl.DeviceIdType.MESH)
 
     def move(source, target, send, recv, where):
         return pltpu.make_async_remote_copy(
@@ -870,9 +920,15 @@
 
         lax.fori_loop(1, count, run, 0)
 
-    each(fs_count, lambda step: greet({"fs": fs_peer(step)}))
-    each(sp_count, lambda step: greet({"sp": sp_peer(step)}))
-    pl.semaphore_wait(barrier, fs_count + sp_count - 2)
+    greet_places()
+    part = query_ref.shape[1] // sp_count
+    for place in range(sp_count):
+        for kind, source in enumerate((query_ref, key_ref, value_ref)):
+            pack_ref[place, :, kind * part : (kind + 1) * part] = source[
+                :, place * part : (place + 1) * part
+            ]
+        pack_ref[place, :, 3 * part :] = small_ref[:, : pack_ref.shape[2] - 3 * part]
+    await_places()
 
     def pack_move(place, mark):
         return move(
@@ -945,8 +1001,6 @@
     )
     own_seq.start()
     own_pack.start()
-    weights = crossing(shard_ref, full_ref, *cross)
-    weights.start_cross()
     own_pack.wait()
     each(sp_count, lambda step: pack_landed(sp_peer(step)).wait_recv())
 
@@ -960,6 +1014,9 @@
     @pl.when(has_down)
     def _():
         downward(fs_place).start()
+
+    route(ids_ref, fill_ref, slots_ref, taking_ref)
+    spread_rows(taking_ref, cot_ref, cot_out_ref)
 
     def relay(step):
         below, above = fs_place - step, fs_place + step
@@ -993,6 +1050,10 @@
         late(mark).start()
         return 0
 
+    cots = cot_swap(cot_out_ref, cots_ref, pl.ds(0, first_rows), cot_send, cot_recv, cot_local)
+    cots.start_all()
+    weights = crossing(shard_ref, full_ref, *cross)
+    weights.start_cross()
     lax.fori_loop(0, fs_count, pass_on, 0)
 
     def end(mark, _):
@@ -1016,33 +1077,48 @@
     each(sp_count, lambda step: pack_move(sp_peer(step), sp_place).wait_send())
     each(fs_count, lambda step: z_move(fs_peer(step)).wait_send())
     own_seq.wait()
+    cots.finish()
     weights.finish_cross()
 
 
-def gather_start(tokens, pack, shard):
+FIRST_ROWS = 32
+
+
+def gather_start(tokens, query, key, value, small, ids, fill, cots, shard):
     sp_count, fs_count = lax.axis_size("sp"), lax.axis_size("fs")
+    total = sp_count * fs_count
     fs_sems = pltpu.SemaphoreType.DMA((fs_count,))
     sp_sems = pltpu.SemaphoreType.DMA((sp_count,))
+    rows, width = query.shape
+    pack = (rows, -(-(3 * width // sp_count + 2 + EXPERTS) // LANES) * LANES)
+    count = ids.shape[1]
+    slot_rows = (total, CAP, width)
     return pl.pallas_call(
-        gather_kernel,
-        in_specs=[IN_PLACE] * 3,
-        out_specs=[IN_PLACE] * 3,
+        functools.partial(gather_kernel, FIRST_ROWS),
+        in_specs=[IN_PLACE] + [VMEM_WHOLE] * 7 + [IN_PLACE],
+        out_specs=[IN_PLACE] * 3 + [VMEM_WHOLE] * 3 + [IN_PLACE],
         out_shape=[
             jax.ShapeDtypeStruct((sp_count, fs_count) + tokens.shape[1:], tokens.dtype),
-            jax.ShapeDtypeStruct((sp_count, fs_count) + pack.shape[1:], pack.dtype),
+            jax.ShapeDtypeStruct((sp_count, fs_count) + pack, query.dtype),
             jax.ShapeDtypeStruct(shard.shape, shard.dtype),
+            jax.ShapeDtypeStruct((TOPK, count), jnp.int32),
+            jax.ShapeDtypeStruct((total * CAP, count), BF16),
+            jax.ShapeDtypeStruct(slot_rows, BF16),
+            jax.ShapeDtypeStruct(slot_rows, BF16),
         ],
-        scratch_shapes=[fs_sems] * 8
+        scratch_shapes=[pltpu.VMEM((sp_count,) + pack, query.dtype)]
+        + [fs_sems] * 8
         + [sp_sems] * 2
         + [fs_sems] * 4
         + [pltpu.SemaphoreType.DMA((2,))]
+        + swap_semaphores(total)
         + cross_scratch(shard),
         compiler_params=remote_params(5),
         cost_estimate=pl.CostEstimate(
             flops=40_000_000_000, bytes_accessed=4_000_000, transcendentals=0
         ),
         name="gather_start",
-    )(tokens, pack, shard)
+    )(tokens, query, key, value, small, ids, fill, cots, shard)
 
 
 def attend_kernel(
@@ -1053,17 +1129,25 @@
     sin_ref,
     crossed_ref,
     shard_ref,
+    other_shard_ref,
+    cot_out_ref,
+    cots_in_ref,
     o_ref,
     lse_ref,
     got_ref,
     shared_ref,
     full_ref,
+    other_full_ref,
+    cots_ref,
     k_rot,
     send,
     recv,
     local,
     dp_send,
     dp_recv,
+    cot_send,
+    cot_recv,
+    cot_local,
     *cross,
 ):
     heads, length, _ = k_rot.shape
@@ -1085,8 +1169,21 @@
     await_places(1)
     share = sharing(shared_ref, dp_send, dp_recv)
     share.start_share()
-    weights = crossing(shard_ref, full_ref, *cross)
+    cap = cots_ref.shape[1]
+    cots = cot_swap(
+        cot_out_ref,
+        cots_ref,
+        pl.ds(FIRST_ROWS, cap - FIRST_ROWS),
+        cot_send,
+        cot_recv,
+        cot_local,
+    )
+    cots.start_all()
+    half = len(cross) // 2
+    weights = crossing(shard_ref, full_ref, *cross[:half])
     weights.start_cross()
+    other_weights = crossing(other_shard_ref, other_full_ref, *cross[half:])
+    other_weights.start_cross()
     exchange = Swap(
         lambda place: o_ref.at[:, columns(place, seg)],
         lambda place: got_ref.at[
@@ -1156,6 +1253,8 @@
     exchange.finish()
     share.finish_share()
     weights.finish_cross()
+    other_weights.finish_cross()
+    cots.finish()
 
 
 def attend_grad_kernel(
@@ -1167,8 +1266,19 @@
     o_ref,
     lse_ref,
     ga_ref,
+    normed_ref,
+    weight_ref,
+    back_out_ref,
+    sums_ref,
+    got_ref,
+    tail_ref,
+    back_ref,
+    spread_ref,
     grad_ref,
-    got_ref,
+    part_send,
+    part_got,
+    own_part,
+    reduced,
     go_feat,
     q_feat,
     q_rows,
@@ -1178,18 +1288,33 @@
     dq_acc,
     dk_acc,
     dv_acc,
+    weight_acc,
+    tail_send,
+    stage,
     send_in,
     recv_in,
     local_in,
-    send,
-    recv,
-    local,
+    send_part,
+    recv_part,
+    send_z,
+    recv_z,
+    local_z,
+    send_tail,
+    recv_tail,
+    local_tail,
+    send_back,
+    recv_back,
+    local_back,
+    send_sums,
+    recv_sums,
+    local_sums,
 ):
     heads, length, _ = q_rows.shape
     wide = heads * HEAD_DIM
     total, own = places()
     seg = length // total
-    fs_count = lax.axis_size("fs")
+    fs_count, sp_count = lax.axis_size("fs"), lax.axis_size("sp")
+    fs_place, sp_place = lax.axis_index("fs"), lax.axis_index("sp")
     greet_places()
 
     def head_rows(kind, head):
@@ -1214,8 +1339,17 @@
     )
     await_places()
     arrival.start_all()
+    back = Swap(
+        lambda place: back_out_ref.at[place],
+        lambda place: back_ref.at[place],
+        send_back,
+        recv_back,
+        local_back,
+    )
+    back.start_all()
     lax.fori_loop(0, heads, prepare, 0)
     dq_acc[...] = jnp.zeros_like(dq_acc)
+    weight_acc[...] = jnp.zeros_like(weight_acc)
     arrival.finish()
 
     def prepare_grad(head, _):
@@ -1227,15 +1361,27 @@
         return 0
 
     lax.fori_loop(0, heads, prepare_grad, 0)
-    exchange = Swap(
-        lambda place: grad_ref.at[:, columns(place, seg)],
-        lambda place: got_ref.at[
-            columns(place // fs_count, 3 * wide), columns(lax.rem(place, fs_count), seg)
-        ],
-        send,
-        recv,
-        local,
-    )
+
+    def to_sp(place, mark):
+        return pltpu.make_async_remote_copy(
+            src_ref=part_send.at[place],
+            dst_ref=part_got.at[mark],
+            send_sem=send_part.at[place],
+            recv_sem=recv_part.at[mark],
+            device_id={"sp": place},
+            device_id_type=pl.DeviceIdType.MESH,
+        )
+
+    def to_fs(place, mark):
+        return pltpu.make_async_remote_copy(
+            src_ref=reduced.at[:, columns(place, seg)],
+            dst_ref=got_ref.at[:, columns(mark, seg)],
+            send_sem=send_z.at[place],
+            recv_sem=recv_z.at[mark],
+            device_id={"fs": place},
+            device_id_type=pl.DeviceIdType.MESH,
+        )
+
     count = length // block
 
     def key_block(place, _):
@@ -1281,22 +1427,109 @@
 
         lax.fori_loop(0, heads, key_head, 0)
 
-        def begin(part, _):
-            exchange.start(place * (block // seg) + part)
-            return 0
-
-        lax.fori_loop(0, block // seg, begin, 0)
+        part = dot32(weight_ref[...], grad_ref[:, own_columns])
+
+        @pl.when(place == sp_place)
+        def _():
+            own_part[...] = part
+
+        @pl.when(place != sp_place)
+        def _():
+            part_send[place] = part.astype(BF16)
+            to_sp(place, sp_place).start()
+
+        weight_acc[...] += dot32(grad_ref[:, own_columns], normed_ref[own_columns, :])
         return 0
 
     lax.fori_loop(0, count, key_block, 0)
-    exchange.finish()
+
+    def to_owner(place, mark):
+        return pltpu.make_async_remote_copy(
+            src_ref=sums_ref.at[place],
+            dst_ref=spread_ref.at[mark],
+            send_sem=send_sums.at[place],
+            recv_sem=recv_sums.at[mark],
+            device_id={"sp": place},
+            device_id_type=pl.DeviceIdType.MESH,
+        )
+
+    def begin_sums(step, _):
+        to_owner(lax.rem(sp_place + step, sp_count), sp_place).start()
+        return 0
+
+    lax.fori_loop(1, sp_count, begin_sums, 0)
+    own_in = pltpu.make_async_copy(sums_ref.at[sp_place], stage, local_sums.at[0])
+    own_out = pltpu.make_async_copy(stage, spread_ref.at[sp_place], local_sums.at[1])
+    own_in.start()
+    shard, wide_all = tail_send.shape[1], 3 * wide
+    flipped = weight_acc[...].T
+    for place in range(tail_send.shape[0]):
+        tail_send[place, :, :wide_all] = flipped[place * shard : (place + 1) * shard].astype(BF16)
+    tail = Swap(
+        lambda place: tail_send.at[place],
+        lambda place: tail_ref.at[place],
+        send_tail,
+        recv_tail,
+        local_tail,
+    )
+
+    def add_part(step, _):
+        mark = lax.rem(sp_place + step, sp_count)
+        to_sp(mark, mark).wait_recv()
+        own_part[...] += part_got[mark].astype(F32)
+        return 0
+
+    lax.fori_loop(1, sp_count, add_part, 0)
+    reduced[...] = own_part[...].astype(BF16)
+
+    def begin_z(step, _):
+        to_fs(lax.rem(fs_place + step, fs_count), fs_place).start()
+        return 0
+
+    lax.fori_loop(1, fs_count, begin_z, 0)
+    own_z = pltpu.make_async_copy(
+        reduced.at[:, columns(fs_place, seg)], got_ref.at[:, columns(fs_place, seg)], local_z
+    )
+    own_z.start()
+    tail.start_all()
+
+    def end_part(step, _):
+        place = lax.rem(sp_place + step, sp_count)
+        to_sp(place, place).wait_send()
+        return 0
+
+    lax.fori_loop(1, sp_count, end_part, 0)
+
+    def end_z(step, _):
+        place = lax.rem(fs_place + step, fs_count)
+        to_fs(place, place).wait_recv()
+        to_fs(place, place).wait_send()
+        return 0
+
+    lax.fori_loop(1, fs_count, end_z, 0)
+    own_z.wait()
+    own_in.wait()
+    own_out.start()
+
+    def end_sums(step, _):
+        place = lax.rem(sp_place + step, sp_count)
+        to_owner(place, place).wait_recv()
+        to_owner(place, place).wait_send()
+        return 0
+
+    lax.fori_loop(1, sp_count, end_sums, 0)
+    own_out.wait()
+    back.finish()
+    tail.finish()
 
 
 def attention_block(length, seg):
-    return math.gcd(length, 4 * seg)
-
-
-def attend(qkv, cosine, sine, crossed, shard, heads, score_scale):
+    return lax.axis_size("fs") * seg
+
+
+def attend(
+    qkv, cosine, sine, crossed, shard, other_shard, cot_out, cots, heads, score_scale
+):
     length = qkv.shape[1]
     total = lax.axis_size("sp") * lax.axis_size("fs")
     seg = length // total
@@ -1304,44 +1537,61 @@
     tokens_here = lax.axis_size("fs") * seg
     return pl.pallas_call(
         functools.partial(attend_kernel, attention_block(length, seg), score_scale),
-        in_specs=[VMEM_WHOLE] * 3 + [IN_PLACE] * 2,
-        out_specs=[VMEM_WHOLE] * 2 + [IN_PLACE] * 3,
+        in_specs=[VMEM_WHOLE] * 3 + [IN_PLACE] * 5,
+        out_specs=[VMEM_WHOLE] * 2 + [IN_PLACE] * 5,
         out_shape=[
             jax.ShapeDtypeStruct((wide, length), BF16),
             jax.ShapeDtypeStruct((heads, 1, length), F32),
             jax.ShapeDtypeStruct((lax.axis_size("sp") * wide, tokens_here), BF16),
             jax.ShapeDtypeStruct(crossed.shape, crossed.dtype),
             jax.ShapeDtypeStruct(shard.shape, shard.dtype),
+            jax.ShapeDtypeStruct(other_shard.shape, other_shard.dtype),
+            jax.ShapeDtypeStruct(cots.shape, cots.dtype),
         ],
-        input_output_aliases={3: 3},
+        input_output_aliases={3: 3, 7: 6},
         scratch_shapes=[pltpu.VMEM((heads, length, HEAD_DIM), BF16)]
         + swap_semaphores(total)
         + share_scratch()
-        + cross_scratch(shard),
+        + swap_semaphores(total)
+        + cross_scratch(shard)
+        + cross_scratch(other_shard),
         compiler_params=remote_params(1),
         cost_estimate=pl.CostEstimate(
             flops=30_000_000_000, bytes_accessed=4_000_000, transcendentals=0
         ),
         name="attend",
-    )(qkv, cosine, sine, crossed, shard)
-
-
-def attend_grad(qkv, cosine, sine, out, lse, grad_attended, heads, score_scale):
+    )(qkv, cosine, sine, crossed, shard, other_shard, cot_out, cots)
+
+
+def attend_grad(
+    qkv, cosine, sine, out, lse, grad_attended, normed, weight, back, sums, heads, score_scale
+):
     length = qkv.shape[1]
-    total = lax.axis_size("sp") * lax.axis_size("fs")
+    sp_count, fs_count = lax.axis_size("sp"), lax.axis_size("fs")
+    total = sp_count * fs_count
     seg = length // total
     block = attention_block(length, seg)
     wide = heads * HEAD_DIM
-    tokens_here = lax.axis_size("fs") * seg
+    width = normed.shape[1]
+    tail = (total, width // total, -(-3 * wide // LANES) * LANES)
+    sp_sems = pltpu.SemaphoreType.DMA((sp_count,))
+    fs_sems = pltpu.SemaphoreType.DMA((fs_count,))
     return pl.pallas_call(
         functools.partial(attend_grad_kernel, block, score_scale),
-        in_specs=[VMEM_WHOLE] * 6,
-        out_specs=[VMEM_WHOLE, IN_PLACE],
+        in_specs=[VMEM_WHOLE] * 8 + [IN_PLACE] * 2,
+        out_specs=[IN_PLACE] * 4,
         out_shape=[
-            jax.ShapeDtypeStruct((3 * wide, length), BF16),
-            jax.ShapeDtypeStruct((lax.axis_size("sp") * 3 * wide, tokens_here), BF16),
+            jax.ShapeDtypeStruct((width, block), BF16),
+            jax.ShapeDtypeStruct(tail, BF16),
+            jax.ShapeDtypeStruct(back.shape, BF16),
+            jax.ShapeDtypeStruct(sums.shape, BF16),
         ],
         scratch_shapes=[
+            pltpu.VMEM((3 * wide, length), BF16),
+            pltpu.VMEM((sp_count, width, block), BF16),
+            pltpu.VMEM((sp_count, width, block), BF16),
+            pltpu.VMEM((width, block), F32),
+            pltpu.VMEM((width, block), BF16),
             pltpu.VMEM((wide, length), BF16),
             pltpu.VMEM((wide, length), BF16),
             pltpu.VMEM((heads, length, HEAD_DIM), BF16),
@@ -1351,15 +1601,21 @@
             pltpu.VMEM((wide, length), F32),
             pltpu.VMEM((block, HEAD_DIM), F32),
             pltpu.VMEM((block, HEAD_DIM), F32),
+            pltpu.VMEM((3 * wide, width), F32),
+            pltpu.VMEM(tail, BF16),
+            pltpu.VMEM(sums.shape[1:], BF16),
         ]
         + swap_semaphores(total)
-        + swap_semaphores(total),
+        + [sp_sems, sp_sems, fs_sems, fs_sems, pltpu.SemaphoreType.DMA]
+        + swap_semaphores(total)
+        + swap_semaphores(total)
+        + [sp_sems, sp_sems, pair_semaphores()],
         compiler_params=remote_params(2),
         cost_estimate=pl.CostEstimate(
             flops=60_000_000_000, bytes_accessed=8_000_000, transcendentals=0
         ),
         name="attend_grad",
-    )(qkv, cosine, sine, out, lse, grad_attended)
+    )(qkv, cosine, sine, out, lse, grad_attended, normed, weight, back, sums)
 
 
 def slope_of(gate_val, sigmoid):
@@ -1369,23 +1625,22 @@
 def dispatch_kernel(
     rows_ref,
     note_ref,
-    crossed_ref,
-    shard_ref,
+    up_in_ref,
+    down_in_ref,
     got_ref,
     got_note_ref,
-    shared_ref,
-    full_ref,
+    up_ref,
+    down_ref,
     send,
     recv,
     local,
     send_note,
     recv_note,
     local_note,
-    dp_send,
-    dp_recv,
-    last_dp_send,
-    last_dp_recv,
-    *cross,
+    up_send,
+    up_recv,
+    down_send,
+    down_recv,
 ):
     greet_places()
     greet_dp()
@@ -1400,22 +1655,19 @@
         local_note,
     )
     await_places(1)
-    weights = crossing(shard_ref, full_ref, *cross)
-    weights.start_cross()
-    share = sharing(shared_ref, dp_send, dp_recv)
-    share.start_share()
     notes.start_all()
     rows.start_all()
-    weights.finish_cross()
-    last = sharing(full_ref, last_dp_send, last_dp_recv)
-    last.start_share()
+    up_share = sharing(up_ref, up_send, up_recv)
+    down_share = sharing(down_ref, down_send, down_recv)
+    up_share.start_share()
+    down_share.start_share()
     notes.finish()
-    share.finish_share()
     rows.finish()
-    last.finish_share()
-
-
-def dispatch(sent, note, crossed, shard):
+    up_share.finish_share()
+    down_share.finish_share()
+
+
+def dispatch(sent, note, up_crossed, down_crossed):
     total = sent.shape[0]
     return pl.pallas_call(
         dispatch_kernel,
@@ -1423,20 +1675,19 @@
         out_specs=[IN_PLACE] * 4,
         out_shape=[
             jax.ShapeDtypeStruct(array.shape, array.dtype)
-            for array in (sent, note, crossed, shard)
+            for array in (sent, note, up_crossed, down_crossed)
         ],
-        input_output_aliases={2: 2},
+        input_output_aliases={2: 2, 3: 3},
         scratch_shapes=swap_semaphores(total)
         + swap_semaphores(total)
         + share_scratch()
-        + share_scratch()
-        + cross_scratch(shard),
+        + share_scratch(),
         compiler_params=remote_params(3),
         cost_estimate=pl.CostEstimate(
             flops=40_000_000_000, bytes_accessed=20_000_000, transcendentals=0
         ),
         name="dispatch",
-    )(sent, note, crossed, shard)
+    )(sent, note, up_crossed, down_crossed)
 
 
 def expert_kernel(
@@ -1457,9 +1708,8 @@
     ddown_ref,
     own_y_ref,
     own_gx_ref,
-    own_dgate_ref,
-    own_dup_ref,
-    own_ddown_ref,
+    own_grads_ref,
+    other_ddown_ref,
     got_ref,
     got_note_ref,
     x_feat,
@@ -1473,17 +1723,25 @@
     gx_send,
     dots_send,
     own_x_feat,
+    ddown_all,
+    gate_stage,
+    up_stage,
+    down_stage,
     send,
     recv,
     local,
     send_note,
     recv_note,
     local_note,
+    ddown_send,
+    ddown_recv,
+    stage_sem,
 ):
     step = pl.program_id(0)
     tiles = pl.num_programs(0) // 3
     total, cap, width = gx_send.shape
     tile = hidden_all.shape[2]
+    own_tile = own_gate_ref.shape[1]
     lanes = dots.shape[1]
     rows = Swap(
         lambda place: gx_send.at[place], lambda place: got_ref.at[place], send, recv, local
@@ -1496,12 +1754,48 @@
         local_note,
     )
 
+    def to_dp(index):
+        return pltpu.make_async_remote_copy(
+            src_ref=ddown_all.at[index],
+            dst_ref=other_ddown_ref.at[:, columns(index, tile)],
+            send_sem=ddown_send.at[index],
+            recv_sem=ddown_recv.at[index],
+            device_id={"dp": 1 - lax.axis_index("dp")},
+            device_id_type=pl.DeviceIdType.MESH,
+        )
+
+    def to_grads(index):
+        turn = lax.rem(index, 2)
+        high = gate_stage.shape[2]
+        weight_rows = own_grads_ref.shape[1] // 3
+        owners, lane_rows = down_stage.shape[1], down_stage.shape[2]
+        return [
+            pltpu.make_async_copy(
+                gate_stage.at[turn], own_grads_ref.at[:, columns(index, high)], stage_sem.at[0, turn]
+            ),
+            pltpu.make_async_copy(
+                up_stage.at[turn],
+                own_grads_ref.at[
+                    :, pl.ds(pl.multiple_of(weight_rows + index * high, high), high)
+                ],
+                stage_sem.at[1, turn],
+            ),
+            pltpu.make_async_copy(
+                down_stage.at[turn],
+                own_grads_ref.at[
+                    pl.ds(index * owners, owners), pl.ds(2 * weight_rows, lane_rows)
+                ],
+                stage_sem.at[2, turn],
+            ),
+        ]
+
     def block(place):
         return slice(place * cap, (place + 1) * cap)
 
     @pl.when(step == 0)
     def _():
         greet_places()
+        greet_dp()
         x_feat[...] = x_ref[...].T
         for place in range(total):
             gate_of_row[block(place), :] = jnp.broadcast_to(
@@ -1511,7 +1805,7 @@
         g_feat[...] = grads.astype(BF16).T
         acc[...] = jnp.zeros_like(acc)
         dots[...] = jnp.zeros_like(dots)
-        await_places()
+        await_places(1)
 
     @pl.when(step < tiles)
     def _():
@@ -1531,6 +1825,10 @@
         hidden_all[step] = hidden
         gate_all[step] = gate_part
         up_all[step] = up_part
+        ddown = dot32(g_feat[...], hidden).astype(BF16)
+        ddown_ref[...] = ddown
+        ddown_all[step] = ddown
+        to_dp(step).start()
 
     @pl.when(step == tiles - 1)
     def _():
@@ -1546,7 +1844,6 @@
         here = step - tiles
         hidden = hidden_all[here]
         acc[...] += dot_nt(hidden, down_ref[...])
-        ddown_ref[...] = dot32(g_feat[...], hidden).astype(BF16)
         dgate_ref[...] = dot32(x_feat[...], gate_all[here]).astype(BF16)
         dup_ref[...] = dot32(x_feat[...], up_all[here]).astype(BF16)
 
@@ -1571,23 +1868,53 @@
         up_part = (grad_hidden * swished).astype(BF16)
         own_y_ref[...] += dot32(hidden_low, own_down_ref[...])
         own_gx_ref[...] += dot_nt(gate_part, own_gate_ref[...]) + dot_nt(up_part, own_up_ref[...])
-        own_ddown_ref[...] = dot32(hidden.T.astype(BF16), own_g_ref[...]).astype(BF16)
-        own_dgate_ref[...] = dot32(own_x_feat[...], gate_part).astype(BF16)
-        own_dup_ref[...] = dot32(own_x_feat[...], up_part).astype(BF16)
+        ddown = dot32(hidden.T.astype(BF16), own_g_ref[...]).astype(BF16)
+        dgate = dot32(own_x_feat[...], gate_part).astype(BF16)
+        dup = dot32(own_x_feat[...], up_part).astype(BF16)
+        here = step - 2 * tiles
+        turn = lax.rem(here, 2)
+
+        @pl.when(here >= 2)
+        def _():
+            for copy in to_grads(here - 2):
+                copy.wait()
+
+        shard = width // total
+        for part in range(own_tile // LANES):
+            lanes_here = slice(part * LANES, (part + 1) * LANES)
+            rows_here = slice(part * shard, (part + 1) * shard)
+            gate_stage[turn, :, rows_here, :] = dgate[:, lanes_here].reshape(total, shard, LANES)
+            up_stage[turn, :, rows_here, :] = dup[:, lanes_here].reshape(total, shard, LANES)
+        owners, owned = down_stage.shape[1], own_tile // down_stage.shape[1]
+        for part in range(width // LANES):
+            down_stage[turn, :, part * owned : (part + 1) * owned, :] = ddown[
+                :, part * LANES : (part + 1) * LANES
+            ].reshape(owners, owned, LANES)
+        for copy in to_grads(here):
+            copy.start()
 
     @pl.when(step == 3 * tiles - 1)
     def _():
+        for index in (tiles - 2, tiles - 1):
+            for copy in to_grads(index):
+                copy.wait()
         rows.finish()
         notes.finish()
 
-
-def expert_pass(rows, cots, note, gate, up, down, own_x, own_g, own_gate, own_up, own_down):
+        def end(index, _):
+            to_dp(index).wait()
+            return 0
+
+        lax.fori_loop(0, tiles, end, 0)
+
+
+def expert_pass(rows, cots, note, gate, up, down, own_x, own_g, own_pack, own_down):
     total, cap, width = rows.shape
     count = total * cap
     hidden = gate.shape[1]
     tile = 256
     tiles = hidden // tile
-    own_tile = own_gate.shape[1] // tiles
+    own_tile = own_down.shape[0] // tiles
     own_count = own_x.shape[0]
     lanes = note.shape[2]
     once = pl.Buffered(1)
@@ -1600,22 +1927,25 @@
     )
     late = pl.BlockSpec((width, tile), lambda i: (0, jnp.clip(i - tiles, 0, tiles - 1)))
     last = pl.BlockSpec((width, own_tile), lambda i: (0, jnp.maximum(i - 2 * tiles, 0)))
+    last_up = pl.BlockSpec((width, own_tile), lambda i: (0, jnp.maximum(i - tiles, tiles)))
+    owners = own_tile * total // own_down.shape[0]
+    high = own_tile // LANES * (width // total)
     last_flat = pl.BlockSpec((own_tile, width), lambda i: (jnp.maximum(i - 2 * tiles, 0), 0))
     return pl.pallas_call(
         expert_kernel,
         grid=(3 * tiles,),
         in_specs=[whole, whole, whole_note, early, early, both]
-        + [whole_own, whole_own, last, last, last_flat],
+        + [whole_own, whole_own, last, last_up, last_flat],
         out_specs=[pl.BlockSpec(rows.shape, lambda i: (0, 0, 0), pipeline_mode=once)]
-        + [late] * 3
-        + [whole_own, whole_own, last, last, last_flat]
-        + [IN_PLACE] * 2,
+        + [late, late, early]
+        + [whole_own, whole_own]
+        + [IN_PLACE] * 4,
         out_shape=[jax.ShapeDtypeStruct(rows.shape, BF16)]
         + [jax.ShapeDtypeStruct((width, hidden), BF16)] * 3
         + [jax.ShapeDtypeStruct((own_count, width), F32)] * 2
-        + [jax.ShapeDtypeStruct(own_gate.shape, BF16)] * 2
         + [
-            jax.ShapeDtypeStruct(own_down.shape, BF16),
+            jax.ShapeDtypeStruct((total, 3 * own_down.size // total // LANES, LANES), BF16),
+            jax.ShapeDtypeStruct((width, hidden), BF16),
             jax.ShapeDtypeStruct(rows.shape, BF16),
             jax.ShapeDtypeStruct(note.shape, F32),
         ],
@@ -1631,9 +1961,18 @@
             pltpu.VMEM(rows.shape, BF16),
             pltpu.VMEM(note.shape, F32),
             pltpu.VMEM((width, own_count), BF16),
+            pltpu.VMEM((tiles, width, tile), BF16),
+            pltpu.VMEM((2, total, high, LANES), BF16),
+            pltpu.VMEM((2, total, high, LANES), BF16),
+            pltpu.VMEM((2, owners, own_tile // owners * (width // LANES), LANES), BF16),
         ]
         + swap_semaphores(total)
-        + swap_semaphores(total),
+        + swap_semaphores(total)
+        + [
+            pltpu.SemaphoreType.DMA((tiles,)),
+            pltpu.SemaphoreType.DMA((tiles,)),
+            pltpu.SemaphoreType.DMA((3, 2)),
+        ],
         compiler_params=remote_params(4),
         cost_estimate=pl.CostEstimate(
             flops=80_000_000_000, bytes_accessed=30_000_000, transcendentals=0
@@ -1648,8 +1987,8 @@
         down,
         own_x,
         own_g,
-        own_gate,
-        own_up,
+        own_pack,
+        own_pack,
         own_down,
     )
 
@@ -1695,43 +2034,30 @@
     length = place_count * seg_rows
     shard_rows = query_weight.shape[0]
     qkv_width = 3 * flat_width
-    shared_width = shared_gate.shape[1]
-
-    choices = expert_ids.reshape(token_count, TOPK)
-    expert_onehot = choices[:, :, None] == jnp.arange(EXPERTS, dtype=jnp.int32)[None, None, :]
-    onehot_float = expert_onehot.astype(F32)
-
-    fill_rank = fill_order.reshape(token_count)
-    earlier = (fill_rank[None, :] < fill_rank[:, None]).astype(BF16)
-    per_token = jnp.sum(onehot_float, axis=1).astype(BF16)
-    counts = dot32(earlier, per_token)
-    slot_ranks = jnp.sum(counts[:, None, :] * onehot_float, axis=2).astype(jnp.int32)
-    group = EXPERTS // fs_count
-    holder = (choices % group) * fs_count + choices // group
-    slots = jnp.where(slot_ranks < CAP, holder * CAP + slot_ranks, -1)
-    slot_total = CAP * EXPERTS
-    slot_ids = jnp.arange(slot_total, dtype=jnp.int32)
-    takes_a = slot_ids[:, None] == slots[None, :, 0]
-    takes_b = slot_ids[:, None] == slots[None, :, 1]
-    taking = (takes_a | takes_b).astype(BF16)
+
     cot_rows = cotangent.reshape(token_count, width)
-    cot_outgoing = dot32(taking, cot_rows).astype(BF16).reshape(place_count, CAP, width)
-    grouped = jnp.stack([query_weight, key_weight, value_weight], axis=1)
-    grouped = grouped.reshape(shard_rows, 3, sp_count, flat_width)
-    small = jnp.concatenate([attention_gain[:, None], mixer_gain[:, None], router_weight], axis=1)
-    grouped = jnp.transpose(grouped, (2, 0, 1, 3)).reshape(sp_count, shard_rows, qkv_width)
-    pack_width = -(-(qkv_width + small.shape[1]) // LANES) * LANES
-    pack = jnp.concatenate(
+    small = jnp.concatenate(
         [
-            grouped,
-            jnp.broadcast_to(small[None], (sp_count,) + small.shape),
-            jnp.zeros((sp_count, shard_rows, pack_width - qkv_width - small.shape[1]), BF16),
+            attention_gain[:, None],
+            mixer_gain[:, None],
+            router_weight,
+            jnp.zeros((shard_rows, LANES - 2 - EXPERTS), BF16),
         ],
-        axis=2,
-    )
-    seq_tokens, own_pack, gate_crossed = gather_start(tokens, pack, expert_gate)
+        axis=1,
+    )
+    seq_tokens, own_pack, gate_crossed, slots, taking, cot_outgoing, cots = gather_start(
+        tokens,
+        query_weight,
+        key_weight,
+        value_weight,
+        small,
+        expert_ids.reshape(token_count, TOPK).T,
+        fill_order.reshape(1, token_count),
+        cot_rows,
+        expert_gate,
+    )
     seq_tokens = seq_tokens.reshape(length, width)
-    own_pack = own_pack.reshape(width, pack_width)
+    own_pack = own_pack.reshape(width, own_pack.shape[-1])
     qkv_own = own_pack[:, :qkv_width]
     gain_one = own_pack[:, qkv_width].astype(F32)
     gain_two = own_pack[:, qkv_width + 1].astype(F32)
@@ -1740,20 +2066,18 @@
     def gather_all(shard):
         return lax.all_gather(shard, ("sp", "fs"), axis=0, tiled=True)
 
-    output_full = gather_all(output_weight)
-    shared_pack, shared_down_sent, cot_sent, seq_tokens = lax.optimization_barrier(
+    output_sent, shared_pack, shared_down_sent, seq_tokens = lax.optimization_barrier(
         (
+            output_weight,
             jnp.concatenate([shared_gate, shared_up], axis=1),
             shared_down,
-            cot_outgoing,
             seq_tokens,
         )
     )
-    arrived_cots = exchange(cot_sent)
+    output_full = gather_all(output_sent)
     shared_pack = gather_all(shared_pack)
     shared_down_full = gather_all(shared_down_sent)
-    shared_gate_full = shared_pack[:, :shared_width]
-    shared_up_full = shared_pack[:, shared_width:]
+    slot_total = CAP * EXPERTS
 
     half = HEAD_DIM // 2
     frequency = 10000.0 ** (-jnp.arange(half, dtype=F32) / half)
@@ -1762,8 +2086,17 @@
 
     normed_seq = norm_apply(seq_tokens.astype(F32), gain_one).astype(BF16)
     qkv = jnp.einsum("de,ld->el", qkv_own, normed_seq, preferred_element_type=F32).astype(BF16)
-    out_heads, lse, attended, gate_own, up_crossed = attend(
-        qkv, cosine, sine, gate_crossed, expert_up, local_heads, score_scale
+    out_heads, lse, attended, gate_own, up_crossed, down_crossed, arrived_cots = attend(
+        qkv,
+        cosine,
+        sine,
+        gate_crossed,
+        expert_up,
+        expert_down,
+        cot_outgoing,
+        cots,
+        local_heads,
+        score_scale,
     )
     residual = tokens.astype(F32).reshape(token_count, width)
 
@@ -1780,7 +2113,13 @@
         picked = jnp.sum(router_probs[:, None, :] * onehot_float, axis=2)
         return picked / jnp.sum(picked, axis=1, keepdims=True)
 
+    choices = expert_ids.reshape(token_count, TOPK)
+    expert_onehot = choices[:, :, None] == jnp.arange(EXPERTS, dtype=jnp.int32)[None, None, :]
+    onehot_float = expert_onehot.astype(F32)
     gate_weights, gate_pull = jax.vjp(gate_values, logits)
+    slot_ids = jnp.arange(slot_total, dtype=jnp.int32)
+    takes_a = slot_ids[:, None] == slots[0][None, :]
+    takes_b = slot_ids[:, None] == slots[1][None, :]
 
     gate_of_slot = jnp.sum(
         jnp.where(takes_a, gate_weights[None, :, 0], 0.0)
@@ -1792,12 +2131,8 @@
         gate_of_slot.reshape(place_count, 1, CAP), ((0, 0), (0, NOTE_ROWS - 1), (0, LANES - CAP))
     )
     rows, notes, up_own, down_own = dispatch(
-        outgoing.reshape(place_count, CAP, width), note, up_crossed, expert_down
-    )
-    qkv_pack, rows = lax.optimization_barrier(
-        (jnp.transpose(grouped, (1, 0, 2)).reshape(shard_rows, sp_count * qkv_width), rows)
-    )
-    qkv_full = gather_all(qkv_pack)
+        outgoing.reshape(place_count, CAP, width), note, up_crossed, down_crossed
+    )
     (
         expert_out,
         dgate,
@@ -1805,9 +2140,8 @@
         ddown,
         shared_out,
         grad_mixed_shared,
-        grad_shared_gate,
-        grad_shared_up,
-        grad_shared_down,
+        grad_shared,
+        ddown_other,
         grad_returned,
         dots,
     ) = expert_pass(
@@ -1819,61 +2153,29 @@
         down_own.reshape(width, -1),
         mixed_in,
         cot_rows,
-        shared_gate_full,
-        shared_up_full,
+        shared_pack,
         shared_down_full,
     )
-    returned = exchange(expert_out).reshape(slot_total, width)
+    grad_shared = lax.psum_scatter(grad_shared, ("sp", "fs"), scatter_dimension=0)
     grad_returned = grad_returned.reshape(slot_total, width)
     dots = dots[:, 0, :CAP].reshape(slot_total)
 
-    sp_place = lax.axis_index("sp")
-    part_rows = width // sp_count
-
-    def partner(step):
-        return lax.bitwise_xor(sp_place, step)
-
-    def rows_of(grad, step):
-        return lax.dynamic_slice_in_dim(grad, partner(step) * part_rows, part_rows, 0)
-
-    def to_sp(value, step):
-        return lax.ppermute(value, "sp", [(i, i ^ step) for i in range(sp_count)])
-
     def to_dp(value):
         return lax.ppermute(value, "dp", [(0, 1), (1, 0)])
 
-    def placed(parts):
-        whole = jnp.zeros((sp_count,) + parts[0].shape, F32)
-        for step, part in enumerate(parts):
-            whole = lax.dynamic_update_slice(whole, part[None], (partner(step), 0, 0))
-        return whole
-
-    def sum_then_spread(grad):
-        other = to_dp(grad)
-        sums = [
-            rows_of(grad, step).astype(F32) + rows_of(other, step).astype(F32)
-            for step in range(sp_count)
-        ]
-        moved = [to_sp(sums[step].astype(BF16), step).astype(F32) for step in range(1, sp_count)]
-        return placed([sums[0]] + moved)
-
-    def spread_then_sum(grad):
-        parts = [rows_of(grad, 0)] + [
-            to_sp(rows_of(grad, step), step) for step in range(1, sp_count)
-        ]
-        return placed([part.astype(F32) + to_dp(part).astype(F32) for part in parts])
-
-    sum_gate, sum_up, sum_down = (
-        spread_then_sum(dgate),
-        spread_then_sum(dup),
-        sum_then_spread(ddown),
-    )
+    def sum_of(grad, other):
+        total = (grad.astype(F32) + other.astype(F32)).astype(BF16)
+        return total.reshape(sp_count, width // sp_count, grad.shape[1])
+
+    def spread(parts):
+        return lax.all_to_all(parts, "sp", split_axis=0, concat_axis=0, tiled=True).astype(F32)
+
+    other_gate, other_up = to_dp(dgate), to_dp(dup)
 
     grad_result = cot_rows.astype(F32)
-    output = (middle + shared_out + outer(taking, returned)).astype(BF16)
     grad_gates = jnp.stack(
         [
-            jnp.sum(jnp.where(slots[:, j : j + 1] == slot_ids[None, :], dots[None, :], 0.0), axis=1)
+            jnp.sum(jnp.where(slots[j][:, None] == slot_ids[None, :], dots[None, :], 0.0), axis=1)
             for j in range(TOPK)
         ],
         axis=1,
@@ -1890,43 +2192,61 @@
     grad_proj = grad_middle.astype(BF16)
     grad_output_matrix = dot32(attended, grad_proj)
     grad_attended = dot_nt(output_full, grad_proj).astype(BF16)
-    dqkv, token_grads = attend_grad(
-        qkv, cosine, sine, out_heads, lse, grad_attended, local_heads, score_scale
-    )
-    grad_qkv_matrix = jnp.einsum("ld,el->de", normed_seq, dqkv, preferred_element_type=F32)
-    grad_normed = jnp.einsum("et,de->td", token_grads, qkv_full, preferred_element_type=F32)
-    _, norm_one_pull = jax.vjp(norm_apply, residual, gain_one)
-    grad_residual_part, grad_gain_one = norm_one_pull(grad_normed)
+    grad_normed, tail, returned, sum_down = attend_grad(
+        qkv,
+        cosine,
+        sine,
+        out_heads,
+        lse,
+        grad_attended,
+        normed_seq,
+        qkv_own,
+        expert_out,
+        sum_of(ddown, ddown_other),
+        local_heads,
+        score_scale,
+    )
+    sum_down = sum_down.astype(F32)
+    other_gate, other_up, grad_normed = lax.optimization_barrier(
+        (other_gate, other_up, grad_normed)
+    )
+    sum_up = spread(sum_of(dup, other_up))
+    sum_gate = spread(sum_of(dgate, other_gate))
+    output = (middle + shared_out + outer(taking, returned.reshape(slot_total, width))).astype(BF16)
+    grad_normed = grad_normed.T.astype(F32)
+    _, norm_one_pull = jax.vjp(lambda values: norm_apply(values, gain_one), residual)
+    (grad_residual_part,) = norm_one_pull(grad_normed)
     grad_tokens = grad_middle + grad_residual_part
-
-    def column(vector, columns):
-        return jnp.pad(vector[:, None], ((0, 0), (0, columns - 1)))
 
     dense = jnp.concatenate(
         [
             grad_output_matrix.astype(BF16),
-            grad_shared_gate,
-            grad_shared_up,
             grad_router.astype(BF16),
-            column(grad_gain_two, 128 - EXPERTS).astype(BF16),
+            jnp.pad(grad_gain_two[:, None], ((0, 0), (0, LANES - EXPERTS - 1))).astype(BF16),
         ],
         axis=1,
     )
     dense = lax.psum_scatter(dense, ("sp", "fs"), scatter_dimension=0, tiled=True)
-    own_shared_down = lax.psum_scatter(
-        grad_shared_down, ("sp", "fs"), scatter_dimension=0, tiled=True
-    )
-    tail = jnp.concatenate([grad_qkv_matrix, column(grad_gain_one, 128)], axis=1).astype(BF16)
-    tail = exchange(tail.reshape(place_count, shard_rows, tail.shape[1]))
-    tail = tail.reshape(sp_count, fs_count, shard_rows, tail.shape[2]).astype(F32)
-    tail = jnp.sum(tail, axis=1).astype(BF16)
+    tail = tail.reshape(sp_count, fs_count, shard_rows, tail.shape[2])[:, :, :, :qkv_width]
+    tail = jnp.sum(tail.astype(F32), axis=1).astype(BF16)
     sum_dense = swap_sum(dense, "dp")
-    sum_shared_down = swap_sum(own_shared_down, "dp")
+    sum_shared = swap_sum(grad_shared, "dp")
     sum_tail = swap_sum(tail, "dp")
-    sum_qkv = sum_tail[:, :, :qkv_width].reshape(sp_count, shard_rows, 3, flat_width)
+    sum_qkv = sum_tail.reshape(sp_count, shard_rows, 3, flat_width)
     sum_qkv = jnp.transpose(sum_qkv, (2, 1, 0, 3)).reshape(3, shard_rows, width)
-    sum_gain_one = jnp.sum(sum_tail[:, :, qkv_width], axis=0)
-    edge = width + 2 * shared_width
+    sum_gain_one = sum(
+        jnp.sum(weight.astype(F32) * grad, axis=1)
+        for weight, grad in zip((query_weight, key_weight, value_weight), sum_qkv)
+    ) / attention_gain.astype(F32)
+    weight_rows = grad_shared.shape[0] // 3
+
+    def lane_blocks(flat, high):
+        blocks = flat.reshape(-1, high, LANES)
+        return jnp.transpose(blocks, (1, 0, 2)).reshape(high, -1)
+
+    sum_shared_gate = lane_blocks(sum_shared[:weight_rows], shard_rows)
+    sum_shared_up = lane_blocks(sum_shared[weight_rows : 2 * weight_rows], shard_rows)
+    sum_shared_down = lane_blocks(sum_shared[2 * weight_rows :], shared_down.shape[0])
     return (
         output.reshape(tokens.shape),
         grad_tokens.reshape(tokens.shape),
@@ -1935,10 +2255,10 @@
         sum_qkv[1],
         sum_qkv[2],
         sum_dense[:, :width],
-        sum_dense[:, edge + EXPERTS],
-        sum_dense[:, edge : edge + EXPERTS],
-        sum_dense[:, width : width + shared_width],
-        sum_dense[:, width + shared_width : edge],
+        sum_dense[:, width + EXPERTS],
+        sum_dense[:, width : width + EXPERTS],
+        sum_shared_gate,
+        sum_shared_up,
         sum_shared_down,
         sum_gate,
         sum_up,

time: 769 us -> 671 us (0.87)
  waiting for transfers between devices: 156 us -> 65.7 us
  Pallas kernels: 408 us -> 460 us
  local copies, waits for them, and re-layouts: 52.3 us -> 28.3 us
  starting transfers between devices: 37.1 us -> 19 us
  matrix products: 39.3 us -> 26.5 us
    ppermute x9 -> x2, waiting for transfers between devices: 94.7 us -> 0.01 us  [to_dp(): return lax.ppermute(value, 'dp', [(0, 1), (1, 0)])]
    ppermute x9 -> x0, waiting for transfers between devices: 56.8 us -> none  [to_sp(): return lax.ppermute(value, 'sp', [(i, i ^ step) for i in range(sp_count)])]
    pallas_call x1, Pallas kernels: 123 us -> 176 us  [attend_grad(): pl.pallas_call(functools.partial(attend_grad_kernel, block, score_scale),...]
    all_gather x4 -> x3, waiting for transfers between devices: 0.06 us -> 29.6 us  [gather_all(): return lax.all_gather(shard, ('sp', 'fs'), axis=0, tiled=True)]
    dynamic_update_slice x12 -> x0, other arithmetic: 28.9 us -> none  [placed(): whole = lax.dynamic_update_slice(whole, part[None], (partner(step), 0, 0))]
    all_to_all x3 -> x2, waiting for transfers between devices: 0.01 us -> 28.4 us  [spread(): lax.all_to_all(parts, 'sp', split_axis=0, concat_axis=0, tiled=True)]
    convert_element_type x2 -> x7, other arithmetic: 4.5 us -> 32.4 us  [the longest x3 17.1 us: sum_of(): total = (grad.astype(F32) + other.astype(F32)).astype(BF16)]
    pallas_call x1, Pallas kernels: 50 us -> 70.7 us  [gather_start(): pl.pallas_call(functools.partial(gather_kernel, FIRST_ROWS), in_specs=[IN...]
  transfers between devices with their start and end apart: 30 -> 12, of which waited for: 9 -> 3; matrix products, arithmetic and copies ran while one was open for 19% -> 12% of each run, Pallas kernels for 54% -> 46%
where the time goes in v3:
time: 671 us; the launch traced here: 666 us
  Pallas kernels  460 us (69%)
  waiting for transfers between devices  65.7 us (10%)
  other arithmetic  51.9 us (8%)
  local copies, waits for them, and re-layouts  28.3 us (4%)
  matrix products  26.5 us (4%)
  starting transfers between devices  19 us (3%)
  between operations  14.5 us (2%)
    pallas_call x1, Pallas kernels, attend_grad(): pl.pallas_call(functools.partial(attend_grad_kernel, block, score_scale),...  176 us
    pallas_call x1, Pallas kernels, expert_pass(): pl.pallas_call(expert_kernel, grid=(3 * tiles,), in_specs=[whole, whole,...  83.1 us
    pallas_call x1, Pallas kernels, attend(): pl.pallas_call(functools.partial(attend_kernel, attention_block(length, s...  72.6 us
    pallas_call x1, Pallas kernels, gather_start(): pl.pallas_call(functools.partial(gather_kernel, FIRST_ROWS), in_specs=[IN...  70.7 us
    pallas_call x1, Pallas kernels, dispatch(): pl.pallas_call(dispatch_kernel, in_specs=[IN_PLACE] * 4, out_specs=[IN_PL...  57.6 us
    all_gather x3, waiting for transfers between devices, gather_all(): return lax.all_gather(shard, ('sp', 'fs'), axis=0, tiled=True)  29.6 us
    all_to_all x2, waiting for transfers between devices, spread(): lax.all_to_all(parts, 'sp', split_axis=0, concat_axis=0, tiled=True)  28.4 us
    convert_element_type x3, other arithmetic, sum_of(): total = (grad.astype(F32) + other.astype(F32)).astype(BF16)  17.1 us
  transfers between devices with their start and end apart: 12, of which 3 were waited for; matrix products, arithmetic and copies ran while one was open for 12% of the time, Pallas kernels for 46%

profile of v3, /device:TPU:12, one launch (start us, length us, event | category | flops | bytes accessed | tf_op | source)
XLA Modules:
  0.0 665.9 jit_solution(1589053000787026768)
XLA Ops:
  12.1 70.7 %gather_start.1 = (bf16[4,4,128,768]{3,2,1,0:T(8,128)(2,1)}, bf16[4,4,48,640]{3,2,1,0:T(8,128)(2,1)}, bf16[4,192,2048]{2,1,0:T(8,128)(2,1)}, s32[2,512]{1,0:T(2,...) custom-call(bf16[4,128,768]{2,1,0:T(8,128)(2,1)} %tokens_ref.1, ...), custom_call_target="tpu_custom_call" | custom-call | flops 40000000000 | bytes 4000000 | tf_op jit(solution)/shard_map/gather_start/pallas_call | solution.py:1096
  93.7 3.8 convolution_convert_fusion.1.qkv_ref
  97.5 72.6 %attend.1 = (bf16[192,2048]{1,0:T(8,128)(2,1)}, f32[3,1,2048]{2,1,0:T(1,128)}, bf16[768,512]{1,0:T(8,128)(2,1)}, bf16[4,192,2048]{2,1,0:T(8,128)(2,1)}, bf16[4,1...) custom-call(bf16[576,2048]{1,0:T(8,128)(2,1)} %convolution_convert_f, ...), custom_call_target="tpu_custom_call", output_to_operand_aliasing={{3}: (3, {}), {6}: (7, {})} | custom-call | flops 30000001024 | bytes 4000000 | tf_op jit(solution)/shard_map/attend/pallas_call | solution.py:1538
  176.7 3.6 convolution_convert_fusion
  180.3 57.6 %dispatch.1 = (bf16[16,72,768]{2,1,0:T(8,128)(2,1)}, f32[16,8,128]{2,1,0:T(8,128)}, bf16[4,192,2048]{2,1,0:T(8,128)(2,1)}, bf16[4,192,2048]{2,1,0:T(8,128)(2,1)}) custom-call(bf16[16,72,768]{2,1,0:T(8,128)(2,1)} %bitcast.127, f32[16,8,128]{2,1,0:T(8,128)} %pad.9.note_ref, ...), custom_call_target="tpu_custom_call", output_to_operand_aliasing={{2}: (2, {}), {3}: (3, {})} | custom-call | flops 40000000000 | bytes 20000000 | tf_op jit(solution)/shard_map/dispatch/pallas_call | solution.py:1672
  237.9 29.6 %all-gather.6.cloned.1.call-done.own_gate_ref.own_up_ref = bf16[768,4096]{1,0:T(8,128)(2,1)} async-done(((bf16[48,4096]{1,0:T(8,128)(2,1)}), bf16[768,4096]{1,0:T(8,128)(2,1)}) %all-gather.6.cloned.1.call-update) | async-done | bytes 6291472 | tf_op jit(solution)/shard_map/all_gather | solution.py:2067
  267.5 83.1 %expert_pass.1 = (bf16[16,72,768]{2,1,0:T(8,128)(2,1)}, bf16[768,2048]{1,0:T(8,128)(2,1)}, bf16[768,2048]{1,0:T(8,128)(2,1)}, bf16[768,2048]{1,0:T(8,128)(2,1)},...) custom-call(bf16[1152,768]{1,0:T(8,128)(2,1)} %bitcast.126, ...), custom_call_target="tpu_custom_call" | custom-call | flops 80000000000 | bytes 30000000 | tf_op jit(solution)/shard_map/expert_pass/pallas_call | solution.py:1934
  352.5 4.2 fusion.23
  356.7 3.0 copy.153
  360.0 2.8 multiply_reduce_fusion
  371.2 3.2 convolution_convert_fusion.3.ga_ref
  374.4 4.9 add_convert_fusion.2
  379.4 175.9 %attend_grad.1 = (bf16[768,512]{1,0:T(8,128)(2,1)}, bf16[16,48,640]{2,1,0:T(8,128)(2,1)}, bf16[16,72,768]{2,1,0:T(8,128)(2,1)}, bf16[4,192,2048]{2,1,0:T(8,128)(2,1)}) custom-call(bf16[576,2048]{1,0:T(8,128)(2,1)} %convolution_convert_fusion.1.qkv_ref, f32[32,2048]{1,0:T(8,128)} %get-tuple-element.188.cos_ref, f32[32,2048]{1,0:T(8,128)} %get-tuple-element.187.sin_ref, ...), custom_call_target="tpu_custom_call" | custom-call | flops 60000002048 | bytes 8000000 | tf_op jit(solution)/shard_map/attend_grad/pallas_call | solution.py:1579
  555.3 6.1 add_convert_fusion
  561.4 6.1 all-to-all-start.1
  572.4 6.1 add_convert_fusion.1
  578.5 28.4 %all-to-all-done.1 = bf16[4,192,2048]{2,1,0:T(8,128)(2,1)} async-done(((bf16[4,192,2048]{2,1,0:T(8,128)(2,1)}), bf16[4,192,2048]{2,1,0:T(8,128)(2,1)}, u32[]{:S(2)}, u32[]{:S(2)}) %all-to-all-start.1) | async-done | bytes 3145760 | tf_op jit(solution)/shard_map/all_to_all | solution.py:2171
  606.9 6.2 all-to-all-start
  613.1 4.1 add_convert_fusion.3
  617.2 3.6 convert_element_type.194
  628.2 5.7 collective-permute-done.3
  641.9 3.0 copy.172
  644.9 5.4 convert_element_type.193
  650.3 5.5 convert_element_type.189
  (162 shorter events, 56.0 us)
Async XLA Ops:
  7.2 163.0 %all-gather.4.cloned.1.call-start = ((), (), s32[]{:S(2)}) async-start(), calls=%async_computation.4 | async-start | bytes 1253376 | tf_op jit(solution)/shard_map/all_gather | solution.py:2067
  12.1 72.5 %copy-start.14 = (bf16[4,128,768]{2,1,0:T(8,128)(2,1)S(1)}, bf16[4,128,768]{2,1,0:T(8,128)(2,1)}, u32[]{:S(2)}) copy-start(bf16[4,128,768]{2,1,0:T(8,128)(2,1)} %param.33) | copy-start | bytes 2359300
  82.8 155.1 %all-gather.8.cloned.1.call-start = ((), (), s32[]{:S(2)}) async-start(), calls=%async_computation.6 | async-start | bytes 3342336 | tf_op jit(solution)/shard_map/all_gather | solution.py:2067
  83.6 184.0 %all-gather.6.cloned.1.call-start = ((), (), s32[]{:S(2)}) async-start(), calls=%async_computation.5 | async-start | bytes 6684672 | tf_op jit(solution)/shard_map/all_gather | solution.py:2067
  84.3 540.7 %reduce-scatter.7.cloned.1.call-start = ((), (), s32[]{:S(2)}) async-start(), calls=%async_computation.8 | async-start | bytes 1462272
  86.1 84.1 %copy-start = (f32[512,768]{0,1:T(8,128)}, f32[512,768]{0,1:T(8,128)S(1)}, u32[]{:S(2)}) copy-start(f32[512,768]{0,1:T(8,128)S(1)} %copy.169) | copy-start | bytes 4718596
  87.9 4.6 copy-start.24
  87.9 4.6 copy-start.4
  364.0 7.3 %copy-start.2 = (f32[512,768]{0,1:T(8,128)}, f32[512,768]{0,1:T(8,128)S(1)}, u32[]{:S(2)}) copy-start(f32[512,768]{0,1:T(8,128)S(1)} %fusion.4) | copy-start | bytes 4718596
  368.5 268.8 %reduce-scatter.5.cloned.1.call-start = ((), (), s32[]{:S(2)}) async-start(), calls=%async_computation.7 | async-start | bytes 10027008 | tf_op jit(solution)/shard_map/reduce_scatter | solution.py:2159
  369.1 186.2 %collective-permute-start = (bf16[768,2048]{1,0:T(8,128)(2,1)}, bf16[768,2048]{1,0:T(8,128)(2,1)}, u32[]{:S(2)}, u32[]{:S(2)}) collective-permute-start(bf16[768,2048]{1,0:T(8,128)(2,1)} %get-tuple-element.84), channel_id=1, source_target_pairs={{0,16},{16,0},{1,17},{17,1},{2,18},{18,2},{3,19},{19,3},{4,20},{20... | collective-permute-start | bytes 9437192 | tf_op jit(solution)/shard_map/ppermute | solution.py:2164
  370.7 184.7 %collective-permute-start.1 = (bf16[768,2048]{1,0:T(8,128)(2,1)}, bf16[768,2048]{1,0:T(8,128)(2,1)}, u32[]{:S(2)}, u32[]{:S(2)}) collective-permute-start(bf16[768,2048]{1,0:T(8,128)(2,1)} %get-tuple-element.85), channel_id=1, source_target_pairs={{0,16},{16,0},{1,17},{17,1},{2,18},{18,2},{3,19},{19,3},{4,20},{20... | collective-permute-start | bytes 9437192 | tf_op jit(solution)/shard_map/ppermute | solution.py:2164
  561.4 6.1 copy-start.7
  561.4 45.4 %all-to-all-start.1 = ((bf16[4,192,2048]{2,1,0:T(8,128)(2,1)}), bf16[4,192,2048]{2,1,0:T(8,128)(2,1)}, u32[]{:S(2)}, u32[]{:S(2)}) async-start(bf16[4,192,2048]{2,1,0:T(8,128)(2,1)} %bitcast.84), calls=%async_computation.2 | async-start | bytes 6291456 | tf_op jit(solution)/shard_map/all_to_all | solution.py:2171
  569.1 52.7 %collective-permute-start.2 = (bf16[4,48,576]{2,1,0:T(8,128)(2,1)S(1)}, bf16[4,48,576]{2,1,0:T(8,128)(2,1)}, u32[]{:S(2)}, u32[]{:S(2)}) collective-permute-start(bf16[4,48,576]{2,1,0:T(8,128)(2,1)S(1)} %slice_reduce_fusion), channel_id=1, source_target_pairs={{0,16},{16,0},{1,17},{17,1},{2,18},{18,2},{3,19},{19,3},{4,20},{20... | collective-permute-start | bytes 663560 | tf_op jit(solution)/shard_map/ppermute | solution.py:1998
  606.9 43.4 %all-to-all-start = ((bf16[4,192,2048]{2,1,0:T(8,128)(2,1)}), bf16[4,192,2048]{2,1,0:T(8,128)(2,1)}, u32[]{:S(2)}, u32[]{:S(2)}) async-start(bf16[4,192,2048]{2,1,0:T(8,128)(2,1)} %bitcast.81), calls=%async_computation.1 | async-start | bytes 6291456 | tf_op jit(solution)/shard_map/all_to_all | solution.py:2171
  613.1 4.1 copy-start.10
  624.6 9.4 %copy-start.19 = (f32[48,768]{1,0:T(8,128)}, f32[48,768]{1,0:T(8,128)S(1)}, u32[]{:S(2)}) copy-start(f32[48,768]{1,0:T(8,128)S(1)} %unstack.19) | copy-start | bytes 442372
  624.6 14.2 %copy-start.1 = (f32[512,768]{0,1:T(8,128)S(1)}, f32[512,768]{0,1:T(8,128)}, u32[]{:S(2)}) copy-start(f32[512,768]{0,1:T(8,128)} %copy-done) | copy-start | bytes 4718596
  624.6 14.2 %copy-start.25 = (f32[768]{0:T(1024)S(1)}, f32[768]{0:T(1024)}, u32[]{:S(2)}) copy-start(f32[768]{0:T(1024)} %copy-done.24) | copy-start | bytes 9220
  626.2 7.7 %collective-permute-start.3 = (bf16[48,896]{0,1:T(8,128)(2,1)S(1)}, bf16[48,896]{0,1:T(8,128)(2,1)S(1)}, u32[]{:S(2)}, u32[]{:S(2)}) collective-permute-start(bf16[48,896]{0,1:T(8,128)(2,1)S(1)} %copy.174), channel_id=1, source_target_pairs={{0,16},{16,0},{1,17},{17,1},{2,18},{18,2},{3,19},{19,3},{4,20},{20... | collective-permute-start | bytes 258056 | tf_op jit(solution)/shard_map/ppermute | solution.py:1998
  634.8 5.5 copy-start.3
  637.4 18.5 %collective-permute-start.4 = (bf16[2304,128]{1,0:T(8,128)(2,1)}, bf16[2304,128]{1,0:T(8,128)(2,1)}, u32[]{:S(2)}, u32[]{:S(2)}) collective-permute-start(bf16[2304,128]{1,0:T(8,128)(2,1)} %bitcast.103), channel_id=1, source_target_pairs={{0,16},{16,0},{1,17},{17,1},{2,18},{18,2},{3,19},{19,3},{4,20},{20... | collective-permute-start | bytes 1769480 | tf_op jit(solution)/shard_map/ppermute | solution.py:1998
  650.3 5.5 copy-start.20
  (17 other events, 36.1 us)
Sparse Core Ops, SparseCore 0:
  82.9 50.4 all-gather.3
  135.7 47.6 all-gather.7
  186.3 81.1 all-gather.5
  368.7 71.6 reduce-scatter.6
  444.3 147.5 reduce-scatter.4

commit v4 on v3

--- a/solution.py
+++ b/solution.py
@@ -847,14 +847,8 @@
             out_ref[first + place] = rows[place * cap : (place + 1) * cap].astype(BF16)
 
 
-def cot_swap(source, target, rows, send, recv, local):
-    return Swap(
-        lambda place: source.at[place, rows], lambda place: target.at[place, rows], send, recv, local
-    )
-
-
-def gather_kernel(
-    first_rows,
+def front_kernel(
+    scale,
     tokens_ref,
     query_ref,
     key_ref,
@@ -863,15 +857,29 @@
     ids_ref,
     fill_ref,
     cot_ref,
-    shard_ref,
-    seq_ref,
-    got_ref,
-    full_ref,
+    cos_ref,
+    sin_ref,
+    gate_shard,
+    up_shard,
+    down_shard,
     slots_ref,
     taking_ref,
-    cot_out_ref,
+    normed_ref,
+    weight_ref,
+    qkv_ref,
+    o_ref,
+    lse_ref,
+    got_ref,
     cots_ref,
-    pack_ref,
+    gate_full,
+    up_full,
+    down_full,
+    seq,
+    pack,
+    pack_got,
+    weight_feat,
+    cot_out,
+    k_rot,
     z_send,
     z_recv,
     core_send,
@@ -880,22 +888,34 @@
     y_recv,
     late_send,
     late_recv,
-    pack_send,
-    pack_recv,
     up_send,
     up_recv,
     down_send,
     down_recv,
+    pack_send,
+    pack_recv,
     local,
     cot_send,
     cot_recv,
     cot_local,
+    send,
+    recv,
+    out_local,
+    gate_dp_send,
+    gate_dp_recv,
+    up_dp_send,
+    up_dp_recv,
     *cross,
 ):
     fs_count, sp_count = lax.axis_size("fs"), lax.axis_size("sp")
     fs_place, sp_place = lax.axis_index("fs"), lax.axis_index("sp")
+    heads, length, _ = k_rot.shape
+    wide = heads * HEAD_DIM
+    seg = tokens_ref.shape[1]
+    block = fs_count * seg
     core = sp_place + 1 - 2 * lax.rem(sp_place, 2)
     across = lax.rem(sp_place + 2, sp_count)
+    beyond = lax.rem(core + 2, sp_count)
 
     def fs_peer(step):
         return lax.rem(fs_place + step, fs_count)
@@ -903,12 +923,12 @@
     def sp_peer(step):
         return lax.rem(sp_place + step, sp_count)
 
-    def move(source, target, send, recv, where):
+    def move(source, target, send_sem, recv_sem, where):
         return pltpu.make_async_remote_copy(
             src_ref=source,
             dst_ref=target,
-            send_sem=send,
-            recv_sem=recv,
+            send_sem=send_sem,
+            recv_sem=recv_sem,
             device_id=where,
             device_id_type=pl.DeviceIdType.MESH,
         )
@@ -921,89 +941,76 @@
         lax.fori_loop(1, count, run, 0)
 
     greet_places()
+    greet_dp()
     part = query_ref.shape[1] // sp_count
     for place in range(sp_count):
         for kind, source in enumerate((query_ref, key_ref, value_ref)):
-            pack_ref[place, :, kind * part : (kind + 1) * part] = source[
+            pack[place, :, kind * part : (kind + 1) * part] = source[
                 :, place * part : (place + 1) * part
             ]
-        pack_ref[place, :, 3 * part :] = small_ref[:, : pack_ref.shape[2] - 3 * part]
-    await_places()
-
-    def pack_move(place, mark):
+        pack[place, :, 3 * part :] = small_ref[:, : pack.shape[2] - 3 * part]
+    await_places(1)
+
+    def pack_move(place, owner, mark):
         return move(
-            pack_ref.at[place],
-            got_ref.at[sp_place, fs_place],
+            pack.at[place],
+            pack_got.at[owner, fs_place],
             pack_send.at[place],
             pack_recv.at[mark],
             {"sp": place},
         )
 
-    def pack_landed(mark):
-        return move(
-            pack_ref.at[mark],
-            got_ref.at[mark, fs_place],
-            pack_send.at[mark],
-            pack_recv.at[mark],
-            {"sp": mark},
-        )
-
-    def z_move(place):
+    def z_move(place, owner):
         return move(
             tokens_ref.at[place],
-            seq_ref.at[sp_place, fs_place],
+            seq.at[sp_place, owner],
             z_send.at[place],
-            z_recv.at[fs_place],
+            z_recv.at[owner],
             {"fs": place},
-        )
-
-    def z_landed(mark):
-        return move(
-            tokens_ref.at[mark],
-            seq_ref.at[sp_place, mark],
-            z_send.at[mark],
-            z_recv.at[mark],
-            {"fs": mark},
         )
 
     def to_core(source, mark):
         return move(
-            source, seq_ref.at[sp_place, mark], core_send.at[mark], core_recv.at[mark], {"sp": core}
+            source, seq.at[sp_place, mark], core_send.at[mark], core_recv.at[mark], {"sp": core}
         )
 
     def to_across(source, mark):
         return move(
-            source, seq_ref.at[sp_place, mark], y_send.at[mark], y_recv.at[mark], {"sp": across}
+            source, seq.at[sp_place, mark], y_send.at[mark], y_recv.at[mark], {"sp": across}
         )
 
     def late(mark):
-        block = seq_ref.at[across, mark]
-        return move(block, block, late_send.at[mark], late_recv.at[mark], {"sp": core})
+        rows = seq.at[across, mark]
+        return move(rows, rows, late_send.at[mark], late_recv.at[mark], {"sp": core})
 
     def upward(mark):
-        block = got_ref.at[:, mark]
-        return move(block, block, up_send.at[mark], up_recv.at[mark], {"fs": fs_peer(1)})
+        rows = pack_got.at[:, mark]
+        return move(rows, rows, up_send.at[mark], up_recv.at[mark], {"fs": fs_peer(1)})
 
     def downward(mark):
-        block = got_ref.at[:, mark]
+        rows = pack_got.at[:, mark]
         return move(
-            block, block, down_send.at[mark], down_recv.at[mark], {"fs": fs_peer(fs_count - 1)}
-        )
-
-    each(sp_count, lambda step: pack_move(sp_peer(step), sp_place).start())
-    each(fs_count, lambda step: z_move(fs_peer(step)).start())
+            rows, rows, down_send.at[mark], down_recv.at[mark], {"fs": fs_peer(fs_count - 1)}
+        )
+
+    each(sp_count, lambda step: pack_move(sp_peer(step), sp_place, sp_place).start())
+    each(fs_count, lambda step: z_move(fs_peer(step), fs_place).start())
     own_tokens = tokens_ref.at[fs_place]
     to_across(own_tokens, fs_place).start()
     to_core(own_tokens, fs_place).start()
-    own_seq = pltpu.make_async_copy(own_tokens, seq_ref.at[sp_place, fs_place], local.at[0])
+    own_seq = pltpu.make_async_copy(own_tokens, seq.at[sp_place, fs_place], local.at[0])
     own_pack = pltpu.make_async_copy(
-        pack_ref.at[sp_place], got_ref.at[sp_place, fs_place], local.at[1]
+        pack.at[sp_place], pack_got.at[sp_place, fs_place], local.at[1]
     )
     own_seq.start()
     own_pack.start()
     own_pack.wait()
-    each(sp_count, lambda step: pack_landed(sp_peer(step)).wait_recv())
-
+
+    def pack_here(step):
+        mark = sp_peer(step)
+        pack_move(mark, mark, mark).wait_recv()
+
+    each(sp_count, pack_here)
     has_up = fs_place < fs_count - 1
     has_down = fs_place > 0
 
@@ -1016,7 +1023,7 @@
         downward(fs_place).start()
 
     route(ids_ref, fill_ref, slots_ref, taking_ref)
-    spread_rows(taking_ref, cot_ref, cot_out_ref)
+    spread_rows(taking_ref, cot_ref, cot_out)
 
     def relay(step):
         below, above = fs_place - step, fs_place + step
@@ -1038,161 +1045,87 @@
             downward(above).start()
 
         mark = fs_peer(step)
-        z_landed(mark).wait_recv()
-        block = seq_ref.at[sp_place, mark]
-        to_across(block, mark).start()
-        to_core(block, mark).start()
+        z_move(mark, mark).wait_recv()
+        rows = seq.at[sp_place, mark]
+        to_across(rows, mark).start()
+        to_core(rows, mark).start()
 
     each(fs_count, relay)
+    cots = Swap(
+        lambda place: cot_out.at[place],
+        lambda place: cots_ref.at[place],
+        cot_send,
+        cot_recv,
+        cot_local,
+    )
+    cots.start_all()
+    size = len(cross) // 3
+    gate = crossing(gate_shard, gate_full, *cross[:size])
+    up = crossing(up_shard, up_full, *cross[size : 2 * size])
+    down = crossing(down_shard, down_full, *cross[2 * size :])
+    gate.start_cross()
+    up.start_cross()
+    down.start_cross()
 
     def pass_on(mark, _):
         to_across(own_tokens, mark).wait_recv()
         late(mark).start()
         return 0
 
-    cots = cot_swap(cot_out_ref, cots_ref, pl.ds(0, first_rows), cot_send, cot_recv, cot_local)
-    cots.start_all()
-    weights = crossing(shard_ref, full_ref, *cross)
-    weights.start_cross()
     lax.fori_loop(0, fs_count, pass_on, 0)
-
-    def end(mark, _):
-        to_core(own_tokens, mark).wait_recv()
-        late(mark).wait_recv()
-        to_core(own_tokens, mark).wait_send()
-        to_across(own_tokens, mark).wait_send()
-        late(mark).wait_send()
-
-        @pl.when(has_up & (mark <= fs_place))
-        def _():
-            upward(mark).wait_send()
-
-        @pl.when(has_down & (mark >= fs_place))
-        def _():
-            downward(mark).wait_send()
-
-        return 0
-
-    lax.fori_loop(0, fs_count, end, 0)
-    each(sp_count, lambda step: pack_move(sp_peer(step), sp_place).wait_send())
-    each(fs_count, lambda step: z_move(fs_peer(step)).wait_send())
     own_seq.wait()
-    cots.finish()
-    weights.finish_cross()
-
-
-FIRST_ROWS = 32
-
-
-def gather_start(tokens, query, key, value, small, ids, fill, cots, shard):
-    sp_count, fs_count = lax.axis_size("sp"), lax.axis_size("fs")
-    total = sp_count * fs_count
-    fs_sems = pltpu.SemaphoreType.DMA((fs_count,))
-    sp_sems = pltpu.SemaphoreType.DMA((sp_count,))
-    rows, width = query.shape
-    pack = (rows, -(-(3 * width // sp_count + 2 + EXPERTS) // LANES) * LANES)
-    count = ids.shape[1]
-    slot_rows = (total, CAP, width)
-    return pl.pallas_call(
-        functools.partial(gather_kernel, FIRST_ROWS),
-        in_specs=[IN_PLACE] + [VMEM_WHOLE] * 7 + [IN_PLACE],
-        out_specs=[IN_PLACE] * 3 + [VMEM_WHOLE] * 3 + [IN_PLACE],
-        out_shape=[
-            jax.ShapeDtypeStruct((sp_count, fs_count) + tokens.shape[1:], tokens.dtype),
-            jax.ShapeDtypeStruct((sp_count, fs_count) + pack, query.dtype),
-            jax.ShapeDtypeStruct(shard.shape, shard.dtype),
-            jax.ShapeDtypeStruct((TOPK, count), jnp.int32),
-            jax.ShapeDtypeStruct((total * CAP, count), BF16),
-            jax.ShapeDtypeStruct(slot_rows, BF16),
-            jax.ShapeDtypeStruct(slot_rows, BF16),
-        ],
-        scratch_shapes=[pltpu.VMEM((sp_count,) + pack, query.dtype)]
-        + [fs_sems] * 8
-        + [sp_sems] * 2
-        + [fs_sems] * 4
-        + [pltpu.SemaphoreType.DMA((2,))]
-        + swap_semaphores(total)
-        + cross_scratch(shard),
-        compiler_params=remote_params(5),
-        cost_estimate=pl.CostEstimate(
-            flops=40_000_000_000, bytes_accessed=4_000_000, transcendentals=0
-        ),
-        name="gather_start",
-    )(tokens, query, key, value, small, ids, fill, cots, shard)
-
-
-def attend_kernel(
-    block,
-    scale,
-    qkv_ref,
-    cos_ref,
-    sin_ref,
-    crossed_ref,
-    shard_ref,
-    other_shard_ref,
-    cot_out_ref,
-    cots_in_ref,
-    o_ref,
-    lse_ref,
-    got_ref,
-    shared_ref,
-    full_ref,
-    other_full_ref,
-    cots_ref,
-    k_rot,
-    send,
-    recv,
-    local,
-    dp_send,
-    dp_recv,
-    cot_send,
-    cot_recv,
-    cot_local,
-    *cross,
-):
-    heads, length, _ = k_rot.shape
-    wide = heads * HEAD_DIM
-    total, own = places()
-    seg = length // total
-    greet_places()
-    greet_dp()
+    packed = pack_got[...].reshape(weight_ref.shape)
+    weight_ref[...] = packed
+    weight_feat[...] = packed.T
+    gain_row = weight_feat[3 * wide : 3 * wide + 1, :].astype(F32)
 
     def head_rows(kind, head):
         return columns(kind * heads + head, HEAD_DIM)
 
-    def turn_keys(head, _):
-        rotated = turn(qkv_ref[head_rows(1, head), :].astype(F32), cos_ref[...], sin_ref[...])
-        k_rot[head] = rotated.T.astype(BF16)
+    def project(place):
+        own_columns = columns(place, block)
+        rows = seq[place].reshape(block, seq.shape[3]).astype(F32)
+        scaled = lax.rsqrt(jnp.mean(rows * rows, axis=-1, keepdims=True) + EPSILON)
+        normed = (rows * scaled * gain_row).astype(BF16)
+        normed_ref[own_columns, :] = normed
+        qkv_ref[:, own_columns] = dot_nt(weight_feat[: 3 * wide, :], normed).astype(BF16)
+
+        def turn_keys(head, _):
+            rotated = turn(
+                qkv_ref[head_rows(1, head), own_columns].astype(F32),
+                cos_ref[:, own_columns],
+                sin_ref[:, own_columns],
+            )
+            k_rot[head, own_columns, :] = rotated.T.astype(BF16)
+            return 0
+
+        lax.fori_loop(0, heads, turn_keys, 0)
+
+    def from_core(mark, _):
+        to_core(own_tokens, mark).wait_recv()
         return 0
 
-    lax.fori_loop(0, heads, turn_keys, 0)
-    await_places(1)
-    share = sharing(shared_ref, dp_send, dp_recv)
-    share.start_share()
-    cap = cots_ref.shape[1]
-    cots = cot_swap(
-        cot_out_ref,
-        cots_ref,
-        pl.ds(FIRST_ROWS, cap - FIRST_ROWS),
-        cot_send,
-        cot_recv,
-        cot_local,
-    )
-    cots.start_all()
-    half = len(cross) // 2
-    weights = crossing(shard_ref, full_ref, *cross[:half])
-    weights.start_cross()
-    other_weights = crossing(other_shard_ref, other_full_ref, *cross[half:])
-    other_weights.start_cross()
+    def from_late(mark, _):
+        late(mark).wait_recv()
+        return 0
+
+    lax.fori_loop(0, fs_count, from_core, 0)
+    lax.fori_loop(0, fs_count, from_late, 0)
+
+    def project_step(step, _):
+        project(sp_peer(step))
+        return 0
+
+    lax.fori_loop(0, sp_count, project_step, 0)
+
     exchange = Swap(
         lambda place: o_ref.at[:, columns(place, seg)],
         lambda place: got_ref.at[
-            columns(place // lax.axis_size("fs"), wide),
-            columns(lax.rem(place, lax.axis_size("fs")), seg),
+            columns(place // fs_count, wide), columns(lax.rem(place, fs_count), seg)
         ],
         send,
         recv,
-        local,
+        out_local,
     )
 
     def attend_block(place):
@@ -1238,23 +1171,113 @@
 
         lax.fori_loop(0, heads, attend_head, 0)
 
+    gate_share = sharing(gate_full, gate_dp_send, gate_dp_recv)
+    up_share = sharing(up_full, up_dp_send, up_dp_recv)
+
     def step(index, _):
         place = length // block - 1 - index
         attend_block(place)
 
         def begin(part, _):
-            exchange.start(place * (block // seg) + part)
+            exchange.start(place * fs_count + part)
             return 0
 
-        lax.fori_loop(0, block // seg, begin, 0)
+        lax.fori_loop(0, fs_count, begin, 0)
+
+        @pl.when(index == 0)
+        def _():
+            gate.finish_cross()
+            gate_share.start_share()
+
+        @pl.when(index == 1)
+        def _():
+            up.finish_cross()
+            up_share.start_share()
+
         return 0
 
     lax.fori_loop(0, length // block, step, 0)
     exchange.finish()
-    share.finish_share()
-    weights.finish_cross()
-    other_weights.finish_cross()
     cots.finish()
+    down.finish_cross()
+    gate_share.finish_share()
+    up_share.finish_share()
+
+    def end(mark, _):
+        to_core(own_tokens, mark).wait_send()
+        to_across(own_tokens, mark).wait_send()
+        late(mark).wait_send()
+
+        @pl.when(has_up & (mark <= fs_place))
+        def _():
+            upward(mark).wait_send()
+
+        @pl.when(has_down & (mark >= fs_place))
+        def _():
+            downward(mark).wait_send()
+
+        return 0
+
+    lax.fori_loop(0, fs_count, end, 0)
+    each(sp_count, lambda step: pack_move(sp_peer(step), sp_place, sp_place).wait_send())
+    each(fs_count, lambda step: z_move(fs_peer(step), fs_place).wait_send())
+
+
+def front(
+    tokens, query, key, value, small, ids, fill, cots, cosine, sine, gate, up, down, score_scale
+):
+    sp_count, fs_count = lax.axis_size("sp"), lax.axis_size("fs")
+    total = sp_count * fs_count
+    fs_sems = pltpu.SemaphoreType.DMA((fs_count,))
+    sp_sems = pltpu.SemaphoreType.DMA((sp_count,))
+    rows, width = query.shape
+    wide = width // sp_count
+    heads = wide // HEAD_DIM
+    seg = tokens.shape[1]
+    length = total * seg
+    pack = (rows, -(-(3 * wide + 2 + EXPERTS) // LANES) * LANES)
+    count = ids.shape[1]
+    slot_rows = (total, CAP, width)
+    return pl.pallas_call(
+        functools.partial(front_kernel, score_scale),
+        in_specs=[IN_PLACE] + [VMEM_WHOLE] * 9 + [IN_PLACE] * 3,
+        out_specs=[VMEM_WHOLE] * 7 + [IN_PLACE] * 5,
+        out_shape=[
+            jax.ShapeDtypeStruct((TOPK, count), jnp.int32),
+            jax.ShapeDtypeStruct((total * CAP, count), BF16),
+            jax.ShapeDtypeStruct((length, width), BF16),
+            jax.ShapeDtypeStruct((width, pack[1]), BF16),
+            jax.ShapeDtypeStruct((3 * wide, length), BF16),
+            jax.ShapeDtypeStruct((wide, length), BF16),
+            jax.ShapeDtypeStruct((heads, 1, length), F32),
+            jax.ShapeDtypeStruct((width, fs_count * seg), BF16),
+            jax.ShapeDtypeStruct(slot_rows, BF16),
+        ]
+        + [jax.ShapeDtypeStruct(shard.shape, shard.dtype) for shard in (gate, up, down)],
+        scratch_shapes=[
+            pltpu.VMEM((sp_count, fs_count) + tokens.shape[1:], BF16),
+            pltpu.VMEM((sp_count,) + pack, BF16),
+            pltpu.VMEM((sp_count, fs_count) + pack, BF16),
+            pltpu.VMEM((pack[1], width), BF16),
+            pltpu.VMEM(slot_rows, BF16),
+            pltpu.VMEM((heads, length, HEAD_DIM), BF16),
+        ]
+        + [fs_sems] * 12
+        + [sp_sems] * 2
+        + [pair_semaphores()]
+        + swap_semaphores(total)
+        + swap_semaphores(total)
+        + share_scratch()
+        + share_scratch()
+        + cross_scratch(gate)
+        + cross_scratch(up)
+        + cross_scratch(down),
+        compiler_params=remote_params(1),
+        cost_estimate=pl.CostEstimate(
+            flops=100_000_000_000, bytes_accessed=4_000_000, transcendentals=0
+        ),
+        name="front",
+    )(tokens, query, key, value, small, ids, fill, cots, cosine, sine, gate, up, down)
 
 
 def attend_grad_kernel(
@@ -1268,46 +1291,52 @@
     ga_ref,
     normed_ref,
     weight_ref,
+    sums_ref,
     back_out_ref,
-    sums_ref,
     got_ref,
+    spread_ref,
+    back_ref,
     tail_ref,
-    back_ref,
-    spread_ref,
     grad_ref,
-    part_send,
-    part_got,
+    near_out,
+    near_got,
+    pair_out,
+    pair_got,
+    far_out,
+    far_got,
     own_part,
     reduced,
     go_feat,
     q_feat,
     q_rows,
     k_feat,
+    k_rows,
+    v_rows,
     go_rows,
     delta,
     dq_acc,
     dk_acc,
     dv_acc,
+    probs,
     weight_acc,
     tail_send,
     stage,
     send_in,
     recv_in,
     local_in,
-    send_part,
-    recv_part,
+    part_sems,
     send_z,
     recv_z,
     local_z,
+    send_sums,
+    recv_sums,
+    local_sums,
+    send_back,
+    recv_back,
+    local_back,
     send_tail,
     recv_tail,
     local_tail,
-    send_back,
-    recv_back,
-    local_back,
-    send_sums,
-    recv_sums,
-    local_sums,
 ):
     heads, length, _ = q_rows.shape
     wide = heads * HEAD_DIM
@@ -1326,6 +1355,8 @@
         q_rows[head] = rotated.T.astype(BF16)
         rotated = turn(qkv_ref[head_rows(1, head), :].astype(F32), cos_ref[...], sin_ref[...])
         k_feat[columns(head, HEAD_DIM), :] = rotated.astype(BF16)
+        k_rows[head] = rotated.T.astype(BF16)
+        v_rows[head] = qkv_ref[head_rows(2, head), :].astype(F32).T.astype(BF16)
         return 0
 
     arrival = Swap(
@@ -1350,6 +1381,45 @@
     lax.fori_loop(0, heads, prepare, 0)
     dq_acc[...] = jnp.zeros_like(dq_acc)
     weight_acc[...] = jnp.zeros_like(weight_acc)
+    dk_acc[...] = jnp.zeros_like(dk_acc)
+    dv_acc[...] = jnp.zeros_like(dv_acc)
+    count = length // block
+    down = 1 - sp_place // (sp_count // 2)
+
+    def pair_columns(turn_index, step):
+        place = turn_index + down * (count - 1 - 2 * turn_index)
+        other = place + step - 2 * step * down
+        queries = columns(other + down * (place - other), block)
+        return queries, columns(place + down * (other - place), block)
+
+    def pair_slot(turn_index, step):
+        return turn_index * (2 * count - turn_index + 1) // 2 + step
+
+    def form(head, _):
+        rows = columns(head, HEAD_DIM)
+
+        def pair(turn_index, step, masked):
+            queries, keys = pair_columns(turn_index, step)
+            scores = dot32(k_rows[head, keys, :], q_feat[rows, queries]) * scale
+            weights = jnp.exp(scores - lse_ref[head, :, queries])
+            if masked:
+                weights = jnp.where(causal(block), weights, 0.0)
+            probs[head, pair_slot(turn_index, step)] = weights.astype(BF16)
+
+        def turns(turn_index, _):
+            pair(turn_index, 0, True)
+
+            def steps(step, _):
+                pair(turn_index, step, False)
+                return 0
+
+            lax.fori_loop(1, count - turn_index, steps, 0)
+            return 0
+
+        lax.fori_loop(0, count, turns, 0)
+        return 0
+
+    lax.fori_loop(0, heads, form, 0)
     arrival.finish()
 
     def prepare_grad(head, _):
@@ -1362,86 +1432,95 @@
 
     lax.fori_loop(0, heads, prepare_grad, 0)
 
-    def to_sp(place, mark):
+    core = sp_place + 1 - 2 * lax.rem(sp_place, 2)
+    across = lax.rem(sp_place + 2, sp_count)
+
+    def part_move(index, source, target, place):
         return pltpu.make_async_remote_copy(
-            src_ref=part_send.at[place],
-            dst_ref=part_got.at[mark],
-            send_sem=send_part.at[place],
-            recv_sem=recv_part.at[mark],
+            src_ref=source,
+            dst_ref=target,
+            send_sem=part_sems.at[0, index],
+            recv_sem=part_sems.at[1, index],
             device_id={"sp": place},
             device_id_type=pl.DeviceIdType.MESH,
         )
 
+    to_near = part_move(0, near_out, near_got, core)
+    to_pair = part_move(1, pair_out, pair_got, core)
+    to_far = part_move(2, far_out, far_got, across)
+
     def to_fs(place, mark):
         return pltpu.make_async_remote_copy(
-            src_ref=reduced.at[:, columns(place, seg)],
-            dst_ref=got_ref.at[:, columns(mark, seg)],
+            src_ref=reduced.at[columns(place, seg), :],
+            dst_ref=got_ref.at[columns(mark, seg), :],
             send_sem=send_z.at[place],
             recv_sem=recv_z.at[mark],
             device_id={"fs": place},
             device_id_type=pl.DeviceIdType.MESH,
         )
 
-    count = length // block
-
-    def key_block(place, _):
+
+    def segment(turn_index, _):
+        place = turn_index + down * (count - 1 - 2 * turn_index)
         own_columns = columns(place, block)
         own_cos, own_sin = cos_ref[:, own_columns], sin_ref[:, own_columns]
 
-        def key_head(head, _):
+        def segment_head(head, _):
             rows = columns(head, HEAD_DIM)
-            key_feat = k_feat[rows, own_columns]
-            key_rows = key_feat.astype(F32).T.astype(BF16)
-            value_rows = qkv_ref[head_rows(2, head), own_columns].astype(F32).T.astype(BF16)
-
-            def terms(index, masked):
-                here = columns(index, block)
-                scores = dot32(key_rows, q_feat[rows, here]) * scale
-                weights = jnp.exp(scores - lse_ref[head, :, here])
-                if masked:
-                    weights = jnp.where(causal(block), weights, 0.0)
-                reach = dot32(value_rows, go_feat[rows, here])
-                slopes = (weights * (reach - delta[head, :, here]) * scale).astype(BF16)
-                dq_acc[rows, here] += dot32(key_feat, slopes)
-                part_key = dot32(slopes, q_rows[head, here, :])
-                part_value = dot32(weights.astype(BF16), go_rows[head, here, :])
-                return part_key, part_value
-
-            dk_acc[...], dv_acc[...] = terms(place, True)
+
+            def pair(step):
+                queries, keys = pair_columns(turn_index, step)
+                low = probs[head, pair_slot(turn_index, step)]
+                weights = low.astype(F32)
+                reach = dot32(v_rows[head, keys, :], go_feat[rows, queries])
+                slopes = (weights * (reach - delta[head, :, queries]) * scale).astype(BF16)
+                dq_acc[rows, queries] += dot32(k_feat[rows, keys], slopes)
+                dk_acc[head, keys, :] += dot32(slopes, q_rows[head, queries, :])
+                dv_acc[head, keys, :] += dot32(low, go_rows[head, queries, :])
+
+            pair(0)
 
             def step(index, _):
-                part_key, part_value = terms(index, False)
-                dk_acc[...] += part_key
-                dv_acc[...] += part_value
+                pair(index)
                 return 0
 
-            lax.fori_loop(place + 1, count, step, 0)
+            lax.fori_loop(1, count - turn_index, step, 0)
             grad_ref[head_rows(0, head), own_columns] = turn_back(
                 dq_acc[rows, own_columns], own_cos, own_sin
             ).astype(BF16)
             grad_ref[head_rows(1, head), own_columns] = turn_back(
-                dk_acc[...].T, own_cos, own_sin
+                dk_acc[head, own_columns, :].T, own_cos, own_sin
             ).astype(BF16)
-            grad_ref[head_rows(2, head), own_columns] = dv_acc[...].T.astype(BF16)
+            grad_ref[head_rows(2, head), own_columns] = dv_acc[head, own_columns, :].T.astype(BF16)
             return 0
 
-        lax.fori_loop(0, heads, key_head, 0)
-
+        lax.fori_loop(0, heads, segment_head, 0)
         part = dot32(weight_ref[...], grad_ref[:, own_columns])
 
         @pl.when(place == sp_place)
         def _():
             own_part[...] = part
 
-        @pl.when(place != sp_place)
+        @pl.when(place == core)
         def _():
-            part_send[place] = part.astype(BF16)
-            to_sp(place, sp_place).start()
+            near_out[...] = part.astype(BF16)
+            to_near.start()
+
+        @pl.when(place == lax.rem(core + 2, sp_count))
+        def _():
+            pair_out[...] = part.astype(BF16)
+            to_pair.start()
+
+        @pl.when(place == across)
+        def _():
+            to_pair.wait_recv()
+            far_out[...] = (part + pair_got[...].astype(F32)).astype(BF16)
+            to_far.start()
 
         weight_acc[...] += dot32(grad_ref[:, own_columns], normed_ref[own_columns, :])
         return 0
 
-    lax.fori_loop(0, count, key_block, 0)
+    lax.fori_loop(0, count, segment, 0)
 
     def to_owner(place, mark):
         return pltpu.make_async_remote_copy(
@@ -1473,14 +1552,11 @@
         local_tail,
     )
 
-    def add_part(step, _):
-        mark = lax.rem(sp_place + step, sp_count)
-        to_sp(mark, mark).wait_recv()
-        own_part[...] += part_got[mark].astype(F32)
-        return 0
-
-    lax.fori_loop(1, sp_count, add_part, 0)
-    reduced[...] = own_part[...].astype(BF16)
+    to_near.wait_recv()
+    own_part[...] += near_got[...].astype(F32)
+    to_far.wait_recv()
+    own_part[...] += far_got[...].astype(F32)
+    reduced[...] = own_part[...].T.astype(BF16)
 
     def begin_z(step, _):
         to_fs(lax.rem(fs_place + step, fs_count), fs_place).start()
@@ -1488,17 +1564,14 @@
 
     lax.fori_loop(1, fs_count, begin_z, 0)
     own_z = pltpu.make_async_copy(
-        reduced.at[:, columns(fs_place, seg)], got_ref.at[:, columns(fs_place, seg)], local_z
+        reduced.at[columns(fs_place, seg), :], got_ref.at[columns(fs_place, seg), :], local_z
     )
     own_z.start()
     tail.start_all()
 
-    def end_part(step, _):
-        place = lax.rem(sp_place + step, sp_count)
-        to_sp(place, place).wait_send()
-        return 0
-
-    lax.fori_loop(1, sp_count, end_part, 0)
+    to_near.wait_send()
+    to_pair.wait_send()
+    to_far.wait_send()
 
     def end_z(step, _):
         place = lax.rem(fs_place + step, fs_count)
@@ -1527,46 +1600,11 @@
     return lax.axis_size("fs") * seg
 
 
-def attend(
-    qkv, cosine, sine, crossed, shard, other_shard, cot_out, cots, heads, score_scale
+def attend_grad(
+    qkv, cosine, sine, out, lse, grad_attended, normed, weight, sums, back, score_scale
 ):
     length = qkv.shape[1]
-    total = lax.axis_size("sp") * lax.axis_size("fs")
-    seg = length // total
-    wide = heads * HEAD_DIM
-    tokens_here = lax.axis_size("fs") * seg
-    return pl.pallas_call(
-        functools.partial(attend_kernel, attention_block(length, seg), score_scale),
-        in_specs=[VMEM_WHOLE] * 3 + [IN_PLACE] * 5,
-        out_specs=[VMEM_WHOLE] * 2 + [IN_PLACE] * 5,
-        out_shape=[
-            jax.ShapeDtypeStruct((wide, length), BF16),
-            jax.ShapeDtypeStruct((heads, 1, length), F32),
-            jax.ShapeDtypeStruct((lax.axis_size("sp") * wide, tokens_here), BF16),
-            jax.ShapeDtypeStruct(crossed.shape, crossed.dtype),
-            jax.ShapeDtypeStruct(shard.shape, shard.dtype),
-            jax.ShapeDtypeStruct(other_shard.shape, other_shard.dtype),
-            jax.ShapeDtypeStruct(cots.shape, cots.dtype),
-        ],
-        input_output_aliases={3: 3, 7: 6},
-        scratch_shapes=[pltpu.VMEM((heads, length, HEAD_DIM), BF16)]
-        + swap_semaphores(total)
-        + share_scratch()
-        + swap_semaphores(total)
-        + cross_scratch(shard)
-        + cross_scratch(other_shard),
-        compiler_params=remote_params(1),
-        cost_estimate=pl.CostEstimate(
-            flops=30_000_000_000, bytes_accessed=4_000_000, transcendentals=0
-        ),
-        name="attend",
-    )(qkv, cosine, sine, crossed, shard, other_shard, cot_out, cots)
-
-
-def attend_grad(
-    qkv, cosine, sine, out, lse, grad_attended, normed, weight, back, sums, heads, score_scale
-):
-    length = qkv.shape[1]
+    heads = qkv.shape[0] // (3 * HEAD_DIM)
     sp_count, fs_count = lax.axis_size("sp"), lax.axis_size("fs")
     total = sp_count * fs_count
     seg = length // total
@@ -1581,41 +1619,48 @@
         in_specs=[VMEM_WHOLE] * 8 + [IN_PLACE] * 2,
         out_specs=[IN_PLACE] * 4,
         out_shape=[
-            jax.ShapeDtypeStruct((width, block), BF16),
+            jax.ShapeDtypeStruct((block, width), BF16),
+            jax.ShapeDtypeStruct(sums.shape, BF16),
+            jax.ShapeDtypeStruct(back.shape, BF16),
             jax.ShapeDtypeStruct(tail, BF16),
-            jax.ShapeDtypeStruct(back.shape, BF16),
-            jax.ShapeDtypeStruct(sums.shape, BF16),
         ],
         scratch_shapes=[
             pltpu.VMEM((3 * wide, length), BF16),
-            pltpu.VMEM((sp_count, width, block), BF16),
-            pltpu.VMEM((sp_count, width, block), BF16),
+            pltpu.VMEM((width, block), BF16),
+            pltpu.VMEM((width, block), BF16),
+            pltpu.VMEM((width, block), BF16),
+            pltpu.VMEM((width, block), BF16),
+            pltpu.VMEM((width, block), BF16),
+            pltpu.VMEM((width, block), BF16),
             pltpu.VMEM((width, block), F32),
-            pltpu.VMEM((width, block), BF16),
+            pltpu.VMEM((block, width), BF16),
             pltpu.VMEM((wide, length), BF16),
             pltpu.VMEM((wide, length), BF16),
             pltpu.VMEM((heads, length, HEAD_DIM), BF16),
             pltpu.VMEM((wide, length), BF16),
             pltpu.VMEM((heads, length, HEAD_DIM), BF16),
+            pltpu.VMEM((heads, length, HEAD_DIM), BF16),
+            pltpu.VMEM((heads, length, HEAD_DIM), BF16),
             pltpu.VMEM((heads, 1, length), F32),
             pltpu.VMEM((wide, length), F32),
-            pltpu.VMEM((block, HEAD_DIM), F32),
-            pltpu.VMEM((block, HEAD_DIM), F32),
+            pltpu.VMEM((heads, length, HEAD_DIM), F32),
+            pltpu.VMEM((heads, length, HEAD_DIM), F32),
+            pltpu.VMEM((heads, sp_count * (sp_count + 1) // 2, block, block), BF16),
             pltpu.VMEM((3 * wide, width), F32),
             pltpu.VMEM(tail, BF16),
             pltpu.VMEM(sums.shape[1:], BF16),
         ]
         + swap_semaphores(total)
-        + [sp_sems, sp_sems, fs_sems, fs_sems, pltpu.SemaphoreType.DMA]
+        + [pltpu.SemaphoreType.DMA((2, 3)), fs_sems, fs_sems, pltpu.SemaphoreType.DMA]
+        + [sp_sems, sp_sems, pair_semaphores()]
         + swap_semaphores(total)
-        + swap_semaphores(total)
-        + [sp_sems, sp_sems, pair_semaphores()],
+        + swap_semaphores(total),
         compiler_params=remote_params(2),
         cost_estimate=pl.CostEstimate(
             flops=60_000_000_000, bytes_accessed=8_000_000, transcendentals=0
         ),
         name="attend_grad",
-    )(qkv, cosine, sine, out, lse, grad_attended, normed, weight, back, sums)
+    )(qkv, cosine, sine, out, lse, grad_attended, normed, weight, sums, back)
 
 
 def slope_of(gate_val, sigmoid):
@@ -1623,27 +1668,39 @@
 
 
 def dispatch_kernel(
+    x_ref,
+    g_ref,
+    gate_ref,
+    up_ref,
+    down_ref,
     rows_ref,
     note_ref,
-    up_in_ref,
-    down_in_ref,
+    crossed_ref,
+    y_ref,
+    gx_ref,
+    grads_ref,
     got_ref,
     got_note_ref,
-    up_ref,
-    down_ref,
+    full_ref,
+    x_feat,
+    gate_stage,
+    up_stage,
+    down_stage,
     send,
     recv,
     local,
     send_note,
     recv_note,
     local_note,
-    up_send,
-    up_recv,
-    down_send,
-    down_recv,
+    dp_send,
+    dp_recv,
+    stage_sem,
 ):
-    greet_places()
-    greet_dp()
+    step = pl.program_id(0)
+    tiles = pl.num_programs(0)
+    total = rows_ref.shape[0]
+    width = x_ref.shape[1]
+    own_tile = gate_ref.shape[1] // (width // total) * LANES
     rows = Swap(
         lambda place: rows_ref.at[place], lambda place: got_ref.at[place], send, recv, local
     )
@@ -1654,40 +1711,152 @@
         recv_note,
         local_note,
     )
-    await_places(1)
-    notes.start_all()
-    rows.start_all()
-    up_share = sharing(up_ref, up_send, up_recv)
-    down_share = sharing(down_ref, down_send, down_recv)
-    up_share.start_share()
-    down_share.start_share()
-    notes.finish()
-    rows.finish()
-    up_share.finish_share()
-    down_share.finish_share()
-
-
-def dispatch(sent, note, up_crossed, down_crossed):
-    total = sent.shape[0]
+    share = sharing(full_ref, dp_send, dp_recv)
+
+    def to_grads(index):
+        turn = lax.rem(index, 2)
+        high = gate_stage.shape[2]
+        weight_rows = grads_ref.shape[1] // 3
+        owners, lane_rows = down_stage.shape[1], down_stage.shape[2]
+        return [
+            pltpu.make_async_copy(
+                gate_stage.at[turn], grads_ref.at[:, columns(index, high)], stage_sem.at[0, turn]
+            ),
+            pltpu.make_async_copy(
+                up_stage.at[turn],
+                grads_ref.at[
+                    :, pl.ds(pl.multiple_of(weight_rows + index * high, high), high)
+                ],
+                stage_sem.at[1, turn],
+            ),
+            pltpu.make_async_copy(
+                down_stage.at[turn],
+                grads_ref.at[
+                    pl.ds(index * owners, owners), pl.ds(2 * weight_rows, lane_rows)
+                ],
+                stage_sem.at[2, turn],
+            ),
+        ]
+
+    @pl.when(step == 0)
+    def _():
+        greet_places()
+        greet_dp()
+        x_feat[...] = x_ref[...].T
+        y_ref[...] = jnp.zeros_like(y_ref)
+        gx_ref[...] = jnp.zeros_like(gx_ref)
+        await_places(1)
+        notes.start_all()
+        rows.start_all()
+        share.start_share()
+
+    own_gate = from_lane_blocks(gate_ref, width // total)
+    own_up = from_lane_blocks(up_ref, width // total)
+    own_down = from_lane_blocks(down_ref, LANES * down_ref.shape[1] // width)
+    gate_val = dot32(x_ref[...], own_gate)
+    up_val = dot32(x_ref[...], own_up)
+    sigmoid = jax.nn.sigmoid(gate_val)
+    swished = gate_val * sigmoid
+    hidden = swished * up_val
+    hidden_low = hidden.astype(BF16)
+    grad_hidden = dot_nt(g_ref[...], own_down)
+    gate_part = (grad_hidden * up_val * slope_of(gate_val, sigmoid)).astype(BF16)
+    up_part = (grad_hidden * swished).astype(BF16)
+    y_ref[...] += dot32(hidden_low, own_down)
+    gx_ref[...] += dot_nt(gate_part, own_gate) + dot_nt(up_part, own_up)
+    ddown = dot32(hidden.T.astype(BF16), g_ref[...]).astype(BF16)
+    dgate = dot32(x_feat[...], gate_part).astype(BF16)
+    dup = dot32(x_feat[...], up_part).astype(BF16)
+    turn = lax.rem(step, 2)
+
+    @pl.when(step >= 2)
+    def _():
+        for copy in to_grads(step - 2):
+            copy.wait()
+
+    shard = width // total
+    for part in range(own_tile // LANES):
+        lanes_here = slice(part * LANES, (part + 1) * LANES)
+        rows_here = slice(part * shard, (part + 1) * shard)
+        gate_stage[turn, :, rows_here, :] = dgate[:, lanes_here].reshape(total, shard, LANES)
+        up_stage[turn, :, rows_here, :] = dup[:, lanes_here].reshape(total, shard, LANES)
+    owners, owned = down_stage.shape[1], own_tile // down_stage.shape[1]
+    for part in range(width // LANES):
+        down_stage[turn, :, part * owned : (part + 1) * owned, :] = ddown[
+            :, part * LANES : (part + 1) * LANES
+        ].reshape(owners, owned, LANES)
+    for copy in to_grads(step):
+        copy.start()
+
+    @pl.when(step == tiles - 1)
+    def _():
+        for index in (tiles - 2, tiles - 1):
+            for copy in to_grads(index):
+                copy.wait()
+        notes.finish()
+        rows.finish()
+        share.finish_share()
+
+
+def dispatch(own_x, own_g, own_pack, sent, note, crossed):
+    total, cap, width = sent.shape
+    own_rows = own_pack.shape[1] // 3
+    tiles = own_rows * total * LANES // width // 256
+    own_count = own_x.shape[0]
+    high = own_rows // tiles
+    owners = total // tiles
+    whole = pl.BlockSpec((own_count, width), lambda i: (0, 0), pipeline_mode=pl.Buffered(1))
     return pl.pallas_call(
         dispatch_kernel,
-        in_specs=[IN_PLACE] * 4,
-        out_specs=[IN_PLACE] * 4,
-        out_shape=[
+        grid=(tiles,),
+        in_specs=[
+            whole,
+            whole,
+            pl.BlockSpec((total, high, LANES), lambda i: (0, i, 0)),
+            pl.BlockSpec((total, high, LANES), lambda i: (0, tiles + i, 0)),
+            pl.BlockSpec((owners, own_rows, LANES), lambda i: (i, 2, 0)),
+        ]
+        + [IN_PLACE] * 3,
+        out_specs=[whole, whole] + [IN_PLACE] * 4,
+        out_shape=[jax.ShapeDtypeStruct((own_count, width), F32)] * 2
+        + [
             jax.ShapeDtypeStruct(array.shape, array.dtype)
-            for array in (sent, note, up_crossed, down_crossed)
+            for array in (own_pack, sent, note, crossed)
         ],
-        input_output_aliases={2: 2, 3: 3},
-        scratch_shapes=swap_semaphores(total)
+        input_output_aliases={7: 5},
+        scratch_shapes=[
+            pltpu.VMEM((width, own_count), BF16),
+            pltpu.VMEM((2, total, high, LANES), BF16),
+            pltpu.VMEM((2, total, high, LANES), BF16),
+            pltpu.VMEM((2, owners, own_rows, LANES), BF16),
+        ]
+        + swap_semaphores(total)
         + swap_semaphores(total)
         + share_scratch()
-        + share_scratch(),
+        + [pltpu.SemaphoreType.DMA((3, 2))],
         compiler_params=remote_params(3),
         cost_estimate=pl.CostEstimate(
             flops=40_000_000_000, bytes_accessed=20_000_000, transcendentals=0
         ),
         name="dispatch",
-    )(sent, note, up_crossed, down_crossed)
+    )(own_x, own_g, own_pack, own_pack, own_pack, sent, note, crossed)
+
+
+def from_lane_blocks(ref, rows):
+    owners, high, lanes = ref.shape
+    return jnp.concatenate(
+        [
+            ref[:, part * rows : (part + 1) * rows, :].reshape(owners * rows, lanes)
+            for part in range(high // rows)
+        ],
+        axis=1,
+    )
+
+
+def to_lane_blocks(matrix):
+    rows, wide = matrix.shape
+    blocks = jnp.transpose(matrix.reshape(rows, wide // LANES, LANES), (1, 0, 2))
+    return blocks.reshape(rows * wide // LANES, LANES)
 
 
 def expert_kernel(
@@ -1697,19 +1866,10 @@
     gate_ref,
     up_ref,
     down_ref,
-    own_x_ref,
-    own_g_ref,
-    own_gate_ref,
-    own_up_ref,
-    own_down_ref,
     y_ref,
     dgate_ref,
     dup_ref,
-    ddown_ref,
-    own_y_ref,
-    own_gx_ref,
-    own_grads_ref,
-    other_ddown_ref,
+    sum_ref,
     got_ref,
     got_note_ref,
     x_feat,
@@ -1722,11 +1882,8 @@
     up_all,
     gx_send,
     dots_send,
-    own_x_feat,
     ddown_all,
-    gate_stage,
-    up_stage,
-    down_stage,
+    other_all,
     send,
     recv,
     local,
@@ -1735,13 +1892,12 @@
     local_note,
     ddown_send,
     ddown_recv,
-    stage_sem,
+    sum_sem,
 ):
     step = pl.program_id(0)
-    tiles = pl.num_programs(0) // 3
+    tiles = pl.num_programs(0) // 2
     total, cap, width = gx_send.shape
     tile = hidden_all.shape[2]
-    own_tile = own_gate_ref.shape[1]
     lanes = dots.shape[1]
     rows = Swap(
         lambda place: gx_send.at[place], lambda place: got_ref.at[place], send, recv, local
@@ -1757,37 +1913,12 @@
     def to_dp(index):
         return pltpu.make_async_remote_copy(
             src_ref=ddown_all.at[index],
-            dst_ref=other_ddown_ref.at[:, columns(index, tile)],
+            dst_ref=other_all.at[index],
             send_sem=ddown_send.at[index],
             recv_sem=ddown_recv.at[index],
             device_id={"dp": 1 - lax.axis_index("dp")},
             device_id_type=pl.DeviceIdType.MESH,
         )
-
-    def to_grads(index):
-        turn = lax.rem(index, 2)
-        high = gate_stage.shape[2]
-        weight_rows = own_grads_ref.shape[1] // 3
-        owners, lane_rows = down_stage.shape[1], down_stage.shape[2]
-        return [
-            pltpu.make_async_copy(
-                gate_stage.at[turn], own_grads_ref.at[:, columns(index, high)], stage_sem.at[0, turn]
-            ),
-            pltpu.make_async_copy(
-                up_stage.at[turn],
-                own_grads_ref.at[
-                    :, pl.ds(pl.multiple_of(weight_rows + index * high, high), high)
-                ],
-                stage_sem.at[1, turn],
-            ),
-            pltpu.make_async_copy(
-                down_stage.at[turn],
-                own_grads_ref.at[
-                    pl.ds(index * owners, owners), pl.ds(2 * weight_rows, lane_rows)
-                ],
-                stage_sem.at[2, turn],
-            ),
-        ]
 
     def block(place):
         return slice(place * cap, (place + 1) * cap)
@@ -1826,7 +1957,6 @@
         gate_all[step] = gate_part
         up_all[step] = up_part
         ddown = dot32(g_feat[...], hidden).astype(BF16)
-        ddown_ref[...] = ddown
         ddown_all[step] = ddown
         to_dp(step).start()
 
@@ -1839,7 +1969,7 @@
         rows.start_all()
         notes.start_all()
 
-    @pl.when((step >= tiles) & (step < 2 * tiles))
+    @pl.when(step >= tiles)
     def _():
         here = step - tiles
         hidden = hidden_all[here]
@@ -1851,100 +1981,53 @@
     def _():
         for place in range(total):
             y_ref[place] = (gate_of_row[block(place), 0:1] * acc[block(place), :]).astype(BF16)
-        own_x_feat[...] = own_x_ref[...].T
-        own_y_ref[...] = jnp.zeros_like(own_y_ref)
-        own_gx_ref[...] = jnp.zeros_like(own_gx_ref)
-
-    @pl.when(step >= 2 * tiles)
-    def _():
-        gate_val = dot32(own_x_ref[...], own_gate_ref[...])
-        up_val = dot32(own_x_ref[...], own_up_ref[...])
-        sigmoid = jax.nn.sigmoid(gate_val)
-        swished = gate_val * sigmoid
-        hidden = swished * up_val
-        hidden_low = hidden.astype(BF16)
-        grad_hidden = dot_nt(own_g_ref[...], own_down_ref[...])
-        gate_part = (grad_hidden * up_val * slope_of(gate_val, sigmoid)).astype(BF16)
-        up_part = (grad_hidden * swished).astype(BF16)
-        own_y_ref[...] += dot32(hidden_low, own_down_ref[...])
-        own_gx_ref[...] += dot_nt(gate_part, own_gate_ref[...]) + dot_nt(up_part, own_up_ref[...])
-        ddown = dot32(hidden.T.astype(BF16), own_g_ref[...]).astype(BF16)
-        dgate = dot32(own_x_feat[...], gate_part).astype(BF16)
-        dup = dot32(own_x_feat[...], up_part).astype(BF16)
-        here = step - 2 * tiles
-        turn = lax.rem(here, 2)
-
-        @pl.when(here >= 2)
-        def _():
-            for copy in to_grads(here - 2):
-                copy.wait()
-
-        shard = width // total
-        for part in range(own_tile // LANES):
-            lanes_here = slice(part * LANES, (part + 1) * LANES)
-            rows_here = slice(part * shard, (part + 1) * shard)
-            gate_stage[turn, :, rows_here, :] = dgate[:, lanes_here].reshape(total, shard, LANES)
-            up_stage[turn, :, rows_here, :] = dup[:, lanes_here].reshape(total, shard, LANES)
-        owners, owned = down_stage.shape[1], own_tile // down_stage.shape[1]
-        for part in range(width // LANES):
-            down_stage[turn, :, part * owned : (part + 1) * owned, :] = ddown[
-                :, part * LANES : (part + 1) * LANES
-            ].reshape(owners, owned, LANES)
-        for copy in to_grads(here):
-            copy.start()
-
-    @pl.when(step == 3 * tiles - 1)
-    def _():
-        for index in (tiles - 2, tiles - 1):
-            for copy in to_grads(index):
-                copy.wait()
+
+        def out(index):
+            return pltpu.make_async_copy(
+                other_all.at[index], sum_ref.at[:, columns(index, tile)], sum_sem.at[index]
+            )
+
+        def add(index, _):
+            to_dp(index).wait()
+            total = ddown_all[index].astype(F32) + other_all[index].astype(F32)
+            other_all[index] = total.astype(BF16)
+            out(index).start()
+            return 0
+
+        lax.fori_loop(0, tiles, add, 0)
         rows.finish()
         notes.finish()
 
         def end(index, _):
-            to_dp(index).wait()
+            out(index).wait()
             return 0
 
         lax.fori_loop(0, tiles, end, 0)
 
 
-def expert_pass(rows, cots, note, gate, up, down, own_x, own_g, own_pack, own_down):
+def expert_pass(rows, cots, note, gate, up, down):
     total, cap, width = rows.shape
     count = total * cap
     hidden = gate.shape[1]
     tile = 256
     tiles = hidden // tile
-    own_tile = own_down.shape[0] // tiles
-    own_count = own_x.shape[0]
     lanes = note.shape[2]
     once = pl.Buffered(1)
     whole = pl.BlockSpec((count, width), lambda i: (0, 0), pipeline_mode=once)
     whole_note = pl.BlockSpec(note.shape, lambda i: (0, 0, 0), pipeline_mode=once)
-    whole_own = pl.BlockSpec((own_count, width), lambda i: (0, 0), pipeline_mode=once)
     early = pl.BlockSpec((width, tile), lambda i: (0, jnp.minimum(i, tiles - 1)))
-    both = pl.BlockSpec(
-        (width, tile), lambda i: (0, jnp.where(i < 2 * tiles, lax.rem(i, tiles), tiles - 1))
-    )
+    both = pl.BlockSpec((width, tile), lambda i: (0, lax.rem(i, tiles)))
     late = pl.BlockSpec((width, tile), lambda i: (0, jnp.clip(i - tiles, 0, tiles - 1)))
-    last = pl.BlockSpec((width, own_tile), lambda i: (0, jnp.maximum(i - 2 * tiles, 0)))
-    last_up = pl.BlockSpec((width, own_tile), lambda i: (0, jnp.maximum(i - tiles, tiles)))
-    owners = own_tile * total // own_down.shape[0]
-    high = own_tile // LANES * (width // total)
-    last_flat = pl.BlockSpec((own_tile, width), lambda i: (jnp.maximum(i - 2 * tiles, 0), 0))
     return pl.pallas_call(
         expert_kernel,
-        grid=(3 * tiles,),
-        in_specs=[whole, whole, whole_note, early, early, both]
-        + [whole_own, whole_own, last, last_up, last_flat],
+        grid=(2 * tiles,),
+        in_specs=[whole, whole, whole_note, early, early, both],
         out_specs=[pl.BlockSpec(rows.shape, lambda i: (0, 0, 0), pipeline_mode=once)]
-        + [late, late, early]
-        + [whole_own, whole_own]
-        + [IN_PLACE] * 4,
+        + [late, late]
+        + [IN_PLACE] * 3,
         out_shape=[jax.ShapeDtypeStruct(rows.shape, BF16)]
-        + [jax.ShapeDtypeStruct((width, hidden), BF16)] * 3
-        + [jax.ShapeDtypeStruct((own_count, width), F32)] * 2
+        + [jax.ShapeDtypeStruct((width, hidden), BF16)] * 2
         + [
-            jax.ShapeDtypeStruct((total, 3 * own_down.size // total // LANES, LANES), BF16),
             jax.ShapeDtypeStruct((width, hidden), BF16),
             jax.ShapeDtypeStruct(rows.shape, BF16),
             jax.ShapeDtypeStruct(note.shape, F32),
@@ -1960,18 +2043,15 @@
             pltpu.VMEM((tiles, count, tile), BF16),
             pltpu.VMEM(rows.shape, BF16),
             pltpu.VMEM(note.shape, F32),
-            pltpu.VMEM((width, own_count), BF16),
             pltpu.VMEM((tiles, width, tile), BF16),
-            pltpu.VMEM((2, total, high, LANES), BF16),
-            pltpu.VMEM((2, total, high, LANES), BF16),
-            pltpu.VMEM((2, owners, own_tile // owners * (width // LANES), LANES), BF16),
+            pltpu.VMEM((tiles, width, tile), BF16),
         ]
         + swap_semaphores(total)
         + swap_semaphores(total)
         + [
             pltpu.SemaphoreType.DMA((tiles,)),
             pltpu.SemaphoreType.DMA((tiles,)),
-            pltpu.SemaphoreType.DMA((3, 2)),
+            pltpu.SemaphoreType.DMA((tiles,)),
         ],
         compiler_params=remote_params(4),
         cost_estimate=pl.CostEstimate(
@@ -1985,11 +2065,6 @@
         gate,
         up,
         down,
-        own_x,
-        own_g,
-        own_pack,
-        own_pack,
-        own_down,
     )
 
 
@@ -2045,7 +2120,34 @@
         ],
         axis=1,
     )
-    seq_tokens, own_pack, gate_crossed, slots, taking, cot_outgoing, cots = gather_start(
+    def gather_all(shard):
+        return lax.all_gather(shard, ("sp", "fs"), axis=0, tiled=True)
+
+    half = HEAD_DIM // 2
+    frequency = 10000.0 ** (-jnp.arange(half, dtype=F32) / half)
+    angles = frequency[:, None] * jnp.arange(length, dtype=jnp.int32).astype(F32)[None, :]
+    cosine, sine = jnp.cos(angles), jnp.sin(angles)
+    output_full = gather_all(output_weight)
+    shared_pack = gather_all(
+        jnp.concatenate(
+            [to_lane_blocks(shared_gate), to_lane_blocks(shared_up), to_lane_blocks(shared_down)]
+        )[None]
+    )
+    slot_total = CAP * EXPERTS
+    (
+        slots,
+        taking,
+        normed_seq,
+        own_pack,
+        qkv,
+        out_heads,
+        lse,
+        attended,
+        arrived_cots,
+        gate_own,
+        up_own,
+        down_crossed,
+    ) = front(
         tokens,
         query_weight,
         key_weight,
@@ -2054,50 +2156,17 @@
         expert_ids.reshape(token_count, TOPK).T,
         fill_order.reshape(1, token_count),
         cot_rows,
+        cosine,
+        sine,
         expert_gate,
-    )
-    seq_tokens = seq_tokens.reshape(length, width)
-    own_pack = own_pack.reshape(width, own_pack.shape[-1])
+        expert_up,
+        expert_down,
+        score_scale,
+    )
     qkv_own = own_pack[:, :qkv_width]
     gain_one = own_pack[:, qkv_width].astype(F32)
     gain_two = own_pack[:, qkv_width + 1].astype(F32)
     router_full = own_pack[:, qkv_width + 2 : qkv_width + 2 + EXPERTS]
-
-    def gather_all(shard):
-        return lax.all_gather(shard, ("sp", "fs"), axis=0, tiled=True)
-
-    output_sent, shared_pack, shared_down_sent, seq_tokens = lax.optimization_barrier(
-        (
-            output_weight,
-            jnp.concatenate([shared_gate, shared_up], axis=1),
-            shared_down,
-            seq_tokens,
-        )
-    )
-    output_full = gather_all(output_sent)
-    shared_pack = gather_all(shared_pack)
-    shared_down_full = gather_all(shared_down_sent)
-    slot_total = CAP * EXPERTS
-
-    half = HEAD_DIM // 2
-    frequency = 10000.0 ** (-jnp.arange(half, dtype=F32) / half)
-    angles = frequency[:, None] * jnp.arange(length, dtype=jnp.int32).astype(F32)[None, :]
-    cosine, sine = jnp.cos(angles), jnp.sin(angles)
-
-    normed_seq = norm_apply(seq_tokens.astype(F32), gain_one).astype(BF16)
-    qkv = jnp.einsum("de,ld->el", qkv_own, normed_seq, preferred_element_type=F32).astype(BF16)
-    out_heads, lse, attended, gate_own, up_crossed, down_crossed, arrived_cots = attend(
-        qkv,
-        cosine,
-        sine,
-        gate_crossed,
-        expert_up,
-        expert_down,
-        cot_outgoing,
-        cots,
-        local_heads,
-        score_scale,
-    )
     residual = tokens.astype(F32).reshape(token_count, width)
 
     def outer(left, right):
@@ -2130,33 +2199,23 @@
     note = jnp.pad(
         gate_of_slot.reshape(place_count, 1, CAP), ((0, 0), (0, NOTE_ROWS - 1), (0, LANES - CAP))
     )
-    rows, notes, up_own, down_own = dispatch(
-        outgoing.reshape(place_count, CAP, width), note, up_crossed, down_crossed
-    )
-    (
-        expert_out,
-        dgate,
-        dup,
-        ddown,
-        shared_out,
-        grad_mixed_shared,
-        grad_shared,
-        ddown_other,
-        grad_returned,
-        dots,
-    ) = expert_pass(
+    shared_out, grad_mixed_shared, grad_shared, rows, notes, down_own = dispatch(
+        mixed_in,
+        cot_rows,
+        shared_pack,
+        outgoing.reshape(place_count, CAP, width),
+        note,
+        down_crossed,
+    )
+    grad_shared = lax.psum_scatter(grad_shared, ("sp", "fs"), scatter_dimension=0)
+    expert_out, dgate, dup, sum_down, grad_returned, dots = expert_pass(
         rows,
         arrived_cots,
         notes,
         gate_own.reshape(width, -1),
         up_own.reshape(width, -1),
         down_own.reshape(width, -1),
-        mixed_in,
-        cot_rows,
-        shared_pack,
-        shared_down_full,
-    )
-    grad_shared = lax.psum_scatter(grad_shared, ("sp", "fs"), scatter_dimension=0)
+    )
     grad_returned = grad_returned.reshape(slot_total, width)
     dots = dots[:, 0, :CAP].reshape(slot_total)
 
@@ -2192,7 +2251,15 @@
     grad_proj = grad_middle.astype(BF16)
     grad_output_matrix = dot32(attended, grad_proj)
     grad_attended = dot_nt(output_full, grad_proj).astype(BF16)
-    grad_normed, tail, returned, sum_down = attend_grad(
+    dense = jnp.concatenate(
+        [
+            grad_output_matrix.astype(BF16),
+            grad_router.astype(BF16),
+            jnp.pad(grad_gain_two[:, None], ((0, 0), (0, LANES - EXPERTS - 1))).astype(BF16),
+        ],
+        axis=1,
+    )
+    grad_normed, sum_down, returned, tail = attend_grad(
         qkv,
         cosine,
         sine,
@@ -2201,32 +2268,23 @@
         grad_attended,
         normed_seq,
         qkv_own,
+        sum_down.reshape(sp_count, width // sp_count, -1),
         expert_out,
-        sum_of(ddown, ddown_other),
-        local_heads,
         score_scale,
     )
-    sum_down = sum_down.astype(F32)
-    other_gate, other_up, grad_normed = lax.optimization_barrier(
-        (other_gate, other_up, grad_normed)
-    )
+    other_gate, other_up, grad_shared, dense, grad_normed = lax.optimization_barrier(
+        (other_gate, other_up, grad_shared, dense, grad_normed)
+    )
+    dense = lax.psum_scatter(dense, ("sp", "fs"), scatter_dimension=0, tiled=True)
     sum_up = spread(sum_of(dup, other_up))
     sum_gate = spread(sum_of(dgate, other_gate))
+    sum_down = sum_down.astype(F32)
     output = (middle + shared_out + outer(taking, returned.reshape(slot_total, width))).astype(BF16)
-    grad_normed = grad_normed.T.astype(F32)
+    grad_normed = grad_normed.astype(F32)
     _, norm_one_pull = jax.vjp(lambda values: norm_apply(values, gain_one), residual)
     (grad_residual_part,) = norm_one_pull(grad_normed)
     grad_tokens = grad_middle + grad_residual_part
 
-    dense = jnp.concatenate(
-        [
-            grad_output_matrix.astype(BF16),
-            grad_router.astype(BF16),
-            jnp.pad(grad_gain_two[:, None], ((0, 0), (0, LANES - EXPERTS - 1))).astype(BF16),
-        ],
-        axis=1,
-    )
-    dense = lax.psum_scatter(dense, ("sp", "fs"), scatter_dimension=0, tiled=True)
     tail = tail.reshape(sp_count, fs_count, shard_rows, tail.shape[2])[:, :, :, :qkv_width]
     tail = jnp.sum(tail.astype(F32), axis=1).astype(BF16)
     sum_dense = swap_sum(dense, "dp")

time: 671 us -> 637 us (0.949); the launches traced: 666 us -> 625 us
  waiting for transfers between devices: 65.7 us -> 50.9 us
  local copies, waits for them, and re-layouts: 28.3 us -> 16.2 us
  other arithmetic: 51.9 us -> 43.7 us
  matrix products: 26.5 us -> 19.6 us
    pallas_call x4 -> x3, Pallas kernels: 284 us -> 335 us  [the longest x1 168 us: front(): pl.pallas_call(functools.partial(front_kernel, score_scale), in_specs=[IN...]
    pallas_call x1, Pallas kernels: 176 us -> 127 us  [attend_grad(): pl.pallas_call(functools.partial(attend_grad_kernel, block, score_scale),...]
    unnamed x6 -> x5, waiting for transfers between devices: 1.95 us -> 35.4 us
    all_gather x3 -> x2, waiting for transfers between devices: 29.6 us -> 0.01 us  [gather_all(): return lax.all_gather(shard, ('sp', 'fs'), axis=0, tiled=True)]
    all_to_all x2, waiting for transfers between devices: 28.4 us -> 9.64 us  [spread(): lax.all_to_all(parts, 'sp', split_axis=0, concat_axis=0, tiled=True)]
    convert_element_type x3 -> x2, other arithmetic: 17.1 us -> 12.3 us  [sum_of(): total = (grad.astype(F32) + other.astype(F32)).astype(BF16)]
  transfers between devices with their start and end apart: 12 -> 11, of which waited for: 3 -> 4; matrix products, arithmetic and copies ran while one was open for 12% -> 11% of each run, Pallas kernels for 46% -> 66%
where the time goes in v4:
time: 637 us; the launch traced here: 625 us
  Pallas kernels  461 us (72%)
  waiting for transfers between devices  50.9 us (8%)
  other arithmetic  43.7 us (7%)
  matrix products  19.6 us (3%)
  starting transfers between devices  18.3 us (3%)
  local copies, waits for them, and re-layouts  16.2 us (3%)
  between operations  14.7 us (2%)
    pallas_call x1, Pallas kernels, front(): pl.pallas_call(functools.partial(front_kernel, score_scale), in_specs=[IN...  168 us
    pallas_call x1, Pallas kernels, attend_grad(): pl.pallas_call(functools.partial(attend_grad_kernel, block, score_scale),...  127 us
    pallas_call x1, Pallas kernels, expert_pass(): pl.pallas_call(expert_kernel, grid=(2 * tiles,), in_specs=[whole, whole,...  115 us
    pallas_call x1, Pallas kernels, dispatch(): pl.pallas_call(dispatch_kernel, grid=(tiles,), in_specs=[whole, whole, pl...  51.8 us
    unnamed x5, waiting for transfers between devices  35.4 us
  transfers between devices with their start and end apart: 11, of which 4 were waited for; matrix products, arithmetic and copies ran while one was open for 11% of the time, Pallas kernels for 66%

profile of v4, /device:TPU:12, one launch (start us, length us, event | category | flops | bytes accessed | tf_op | source)
XLA Modules:
  0.0 624.7 jit_solution(18017353124171670997)
XLA Ops:
  12.3 1.8 multiply_sine_fusion
  14.1 167.5 %front.1 = (s32[2,512]{1,0:T(2,128)}, bf16[1152,512]{1,0:T(8,128)(2,1)}, bf16[2048,768]{1,0:T(8,128)(2,1)}, bf16[768,640]{1,0:T(8,128)(2,1)}, bf16[576,2048]{1,0...) custom-call(bf16[4,128,768]{2,1,0:T(8,128)(2,1)} %tokens_ref.1, ...), custom_call_target="tpu_custom_call" | custom-call | flops 99999997952 | bytes 4000000 | tf_op jit(solution)/shard_map/front/pallas_call | solution.py:1241
  181.7 1.9 convert_reduce_fusion
  185.2 2.4 multiply_reduce_fusion.2
  190.9 3.6 convolution_convert_fusion
  194.4 51.8 %dispatch.1 = (f32[512,768]{1,0:T(8,128)}, f32[512,768]{1,0:T(8,128)}, bf16[16,2304,128]{2,1,0:T(8,128)(2,1)}, bf16[16,72,768]{2,1,0:T(8,128)(2,1)}, f32[16,8,12...) custom-call(bf16[512,768]{1,0:T(8,128)(2,1)} %copy-done.4, ...), custom_call_target="tpu_custom_call", output_to_operand_aliasing={{5}: (7, {})} | custom-call | flops 40000000000 | bytes 20000000 | tf_op jit(solution)/shard_map/dispatch/pallas_call | solution.py:1809
  246.2 115.4 %expert_pass.1 = (bf16[16,72,768]{2,1,0:T(8,128)(2,1)}, bf16[768,2048]{1,0:T(8,128)(2,1)}, bf16[768,2048]{1,0:T(8,128)(2,1)}, bf16[768,2048]{1,0:T(8,128)(2,1)},...) custom-call(bf16[1152,768]{1,0:T(8,128)(2,1)} %bitcast.142, bf16[1152,768]{1,0:T(8,128)(2,1)} %bitcast.140, ...), custom_call_target="tpu_custom_call" | custom-call | flops 80000000000 | bytes 30000000 | tf_op jit(solution)/shard_map/expert_pass/pallas_call | solution.py:2021
  363.5 2.8 fusion.21
  366.4 1.9 multiply_reduce_fusion
  374.4 1.7 fusion.6.ga_ref
  376.1 126.6 %attend_grad.1 = (bf16[512,768]{1,0:T(8,128)(2,1)}, bf16[4,192,2048]{2,1,0:T(8,128)(2,1)}, bf16[16,72,768]{2,1,0:T(8,128)(2,1)}, bf16[16,48,640]{2,1,0:T(8,128)(2,1)}) custom-call(bf16[576,2048]{1,0:T(8,128)(2,1)} %get-tuple-element.54.qkv_ref, f32[32,2048]{1,0:T(8,128)} %get-tuple-element.176.cos_ref, f32[32,2048]{1,0:T(8,128)} %get-tuple-element.175.sin_ref, ...), custom_call_target="tpu_custom_call" | custom-call | flops 60000002048 | bytes 8000000 | tf_op jit(solution)/shard_map/attend_grad/pallas_call | solution.py:1617
  502.7 3.4 collective-permute-done.1
  506.1 6.1 add_convert_fusion
  512.2 6.0 all-to-all-start.1
  521.1 4.6 add_convert_fusion.2
  525.7 3.5 convert_element_type.172
  535.0 1.8 copy.121
  536.9 6.2 add_convert_fusion.1
  543.9 9.6 %all-to-all-done.1 = bf16[4,192,2048]{2,1,0:T(8,128)(2,1)} async-done(((bf16[4,192,2048]{2,1,0:T(8,128)(2,1)}), bf16[4,192,2048]{2,1,0:T(8,128)(2,1)}, u32[]{:S(2)}, u32[]{:S(2)}) %all-to-all-start.1) | async-done | bytes 3145760 | tf_op jit(solution)/shard_map/all_to_all | solution.py:2230
  553.6 6.4 %all-to-all-start = ((bf16[4,192,2048]{2,1,0:T(8,128)(2,1)}), bf16[4,192,2048]{2,1,0:T(8,128)(2,1)}, u32[]{:S(2)}, u32[]{:S(2)}) async-start(bf16[4,192,2048]{2,1,0:T(8,128)(2,1)} %bitcast.101), calls=%async_computation.1 | async-start | bytes 6291456 | tf_op jit(solution)/shard_map/all_to_all | solution.py:2230
  563.0 34.7 %reduce-scatter.7.cloned.1.call-done = bf16[48,896]{1,0:T(8,128)(2,1)} async-done(((bf16[768,896]{1,0:T(8,128)(2,1)}), bf16[48,896]{1,0:T(8,128)(2,1)}) %reduce-scatter.7.cloned.1.call-update) | async-done | bytes 86032
  602.3 2.5 collective-permute-done.3
  606.8 5.4 convert_element_type.171
  612.3 5.5 convert_element_type.167
  (136 shorter events, 36.9 us)
Async XLA Ops:
  7.2 178.0 %all-gather.4.cloned.1.call-start = ((), (), s32[]{:S(2)}) async-start(), calls=%async_computation.4 | async-start | bytes 1253376 | tf_op jit(solution)/shard_map/all_gather | solution.py:2124
  7.9 186.5 %all-gather.6.cloned.1.call-start = ((), (), s32[]{:S(2)}) async-start(), calls=%async_computation.6 | async-start | bytes 10027008 | tf_op jit(solution)/shard_map/all_gather | solution.py:2124
  11.2 494.9 %reduce-scatter.5.cloned.1.call-start = ((), (), s32[]{:S(2)}) async-start(), calls=%async_computation.5 | async-start | bytes 10027008 | tf_op jit(solution)/shard_map/reduce_scatter | solution.py:2210
  14.1 169.5 %copy-start.2 = (bf16[4,128,768]{2,1,0:T(8,128)(2,1)S(1)}, bf16[4,128,768]{2,1,0:T(8,128)(2,1)}, u32[]{:S(2)}) copy-start(bf16[4,128,768]{2,1,0:T(8,128)(2,1)} %tokens_ref.1) | copy-start | bytes 2359300
  187.8 6.6 %copy-start.4 = (bf16[512,768]{1,0:T(8,128)(2,1)}, bf16[512,768]{1,0:T(8,128)(2,1)S(1)}, u32[]{:S(2)}) copy-start(bf16[512,768]{1,0:T(8,128)(2,1)S(1)} %multiply_convert_fusion.x_ref) | copy-start | bytes 2359300
  246.2 117.3 %copy-start.10 = (bf16[1152,512]{1,0:T(8,128)(2,1)S(1)}, bf16[1152,512]{1,0:T(8,128)(2,1)}, u32[]{:S(2)}) copy-start(bf16[1152,512]{1,0:T(8,128)(2,1)} %get-tuple-element.50) | copy-start | bytes 3538948
  366.4 4.3 copy-start.12
  368.3 134.4 %collective-permute-start = (bf16[768,2048]{1,0:T(8,128)(2,1)}, bf16[768,2048]{1,0:T(8,128)(2,1)}, u32[]{:S(2)}, u32[]{:S(2)}) collective-permute-start(bf16[768,2048]{1,0:T(8,128)(2,1)} %get-tuple-element.70), channel_id=1, source_target_pairs={{0,16},{16,0},{1,17},{17,1},{2,18},{18,2},{3,19},{19,3},{4,20},{20... | collective-permute-start | bytes 9437192 | tf_op jit(solution)/shard_map/ppermute | solution.py:2223
  369.9 136.2 %collective-permute-start.1 = (bf16[768,2048]{1,0:T(8,128)(2,1)}, bf16[768,2048]{1,0:T(8,128)(2,1)}, u32[]{:S(2)}, u32[]{:S(2)}) collective-permute-start(bf16[768,2048]{1,0:T(8,128)(2,1)} %get-tuple-element.71), channel_id=1, source_target_pairs={{0,16},{16,0},{1,17},{17,1},{2,18},{18,2},{3,19},{19,3},{4,20},{20... | collective-permute-start | bytes 9437192 | tf_op jit(solution)/shard_map/ppermute | solution.py:2223
  512.2 41.4 %all-to-all-start.1 = ((bf16[4,192,2048]{2,1,0:T(8,128)(2,1)}), bf16[4,192,2048]{2,1,0:T(8,128)(2,1)}, u32[]{:S(2)}, u32[]{:S(2)}) async-start(bf16[4,192,2048]{2,1,0:T(8,128)(2,1)} %bitcast.100), calls=%async_computation.2 | async-start | bytes 6291456 | tf_op jit(solution)/shard_map/all_to_all | solution.py:2230
  518.2 79.5 %reduce-scatter.7.cloned.1.call-start = ((), (), s32[]{:S(2)}) async-start(), calls=%async_computation.7 | async-start | bytes 1462272
  519.5 9.7 %collective-permute-start.2 = (bf16[4,48,576]{2,1,0:T(8,128)(2,1)S(1)}, bf16[4,48,576]{2,1,0:T(8,128)(2,1)S(1)}, u32[]{:S(2)}, u32[]{:S(2)}) collective-permute-start(bf16[4,48,576]{2,1,0:T(8,128)(2,1)S(1)} %slice_reduce_fusion), channel_id=1, source_target_pairs={{0,16},{16,0},{1,17},{17,1},{2,18},{18,2},{3,19},{19,3},{4,20},{20... | collective-permute-start | bytes 663560 | tf_op jit(solution)/shard_map/ppermute | solution.py:2073
  521.1 4.6 copy-start.8
  530.0 4.5 copy-start.19
  530.0 5.0 copy-start.6
  532.2 4.6 copy-start.13
  536.8 6.8 %copy-start.3 = (bf16[4,128,768]{2,1,0:T(8,128)(2,1)S(1)}, bf16[4,128,768]{2,1,0:T(8,128)(2,1)}, u32[]{:S(2)}) copy-start(bf16[4,128,768]{2,1,0:T(8,128)(2,1)} %tokens_ref.1) | copy-start | bytes 2359300
  536.8 6.8 %copy-start.7 = (bf16[512,768]{1,0:T(8,128)(2,1)S(1)}, bf16[512,768]{1,0:T(8,128)(2,1)}, u32[]{:S(2)}) copy-start(bf16[512,768]{1,0:T(8,128)(2,1)} %get-tuple-element.74) | copy-start | bytes 2359300
  536.8 6.8 %copy-start.14 = (f32[768]{0:T(1024)S(1)}, f32[768]{0:T(1024)}, u32[]{:S(2)}) copy-start(f32[768]{0:T(1024)} %get-tuple-element.158) | copy-start | bytes 9220
  543.0 18.5 %collective-permute-start.4 = (bf16[2304,128]{1,0:T(8,128)(2,1)}, bf16[2304,128]{1,0:T(8,128)(2,1)}, u32[]{:S(2)}, u32[]{:S(2)}) collective-permute-start(bf16[2304,128]{1,0:T(8,128)(2,1)} %bitcast.32), channel_id=1, source_target_pairs={{0,16},{16,0},{1,17},{17,1},{2,18},{18,2},{3,19},{19,3},{4,20},{20... | collective-permute-start | bytes 1769480 | tf_op jit(solution)/shard_map/ppermute | solution.py:2073
  553.6 6.4 %copy-start.16 = (f32[4,128]{1,0:T(4,128)S(1)}, f32[4,128]{1,0:T(4,128)}, u32[]{:S(2)}) copy-start(f32[4,128]{1,0:T(4,128)} %fusion.3) | copy-start | bytes 6148
  553.6 58.7 %all-to-all-start = ((bf16[4,192,2048]{2,1,0:T(8,128)(2,1)}), bf16[4,192,2048]{2,1,0:T(8,128)(2,1)}, u32[]{:S(2)}, u32[]{:S(2)}) async-start(bf16[4,192,2048]{2,1,0:T(8,128)(2,1)} %bitcast.101), calls=%async_computation.1 | async-start | bytes 6291456 | tf_op jit(solution)/shard_map/all_to_all | solution.py:2230
  598.7 6.1 collective-permute-start.3
  612.3 5.5 copy-start.1
  (9 other events, 20.6 us)
Sparse Core Ops, SparseCore 0:
  10.3 50.8 all-gather.3
  64.1 129.9 all-gather.5
  246.3 161.9 reduce-scatter.4
  536.9 60.6 reduce-scatter.6

commit v5 on v4

--- a/solution.py
+++ b/solution.py
@@ -1870,6 +1870,7 @@
     dgate_ref,
     dup_ref,
     sum_ref,
+    other_up_ref,
     got_ref,
     got_note_ref,
     x_feat,
@@ -1884,6 +1885,7 @@
     dots_send,
     ddown_all,
     other_all,
+    up_sent,
     send,
     recv,
     local,
@@ -1893,6 +1895,8 @@
     ddown_send,
     ddown_recv,
     sum_sem,
+    half_send,
+    half_recv,
 ):
     step = pl.program_id(0)
     tiles = pl.num_programs(0) // 2
@@ -1916,6 +1920,16 @@
             dst_ref=other_all.at[index],
             send_sem=ddown_send.at[index],
             recv_sem=ddown_recv.at[index],
+            device_id={"dp": 1 - lax.axis_index("dp")},
+            device_id_type=pl.DeviceIdType.MESH,
+        )
+
+    def up_to_dp(index):
+        return pltpu.make_async_remote_copy(
+            src_ref=up_sent.at[index],
+            dst_ref=other_up_ref.at[:, columns(index, tile)],
+            send_sem=half_send.at[index],
+            recv_sem=half_recv.at[index],
             device_id={"dp": 1 - lax.axis_index("dp")},
             device_id_type=pl.DeviceIdType.MESH,
         )
@@ -1975,7 +1989,13 @@
         hidden = hidden_all[here]
         acc[...] += dot_nt(hidden, down_ref[...])
         dgate_ref[...] = dot32(x_feat[...], gate_all[here]).astype(BF16)
-        dup_ref[...] = dot32(x_feat[...], up_all[here]).astype(BF16)
+        dup = dot32(x_feat[...], up_all[here]).astype(BF16)
+        dup_ref[...] = dup
+
+        @pl.when(here < tiles // 2)
+        def _():
+            up_sent[here] = dup
+            up_to_dp(here).start()
 
     @pl.when(step == 2 * tiles - 1)
     def _():
@@ -2003,6 +2023,12 @@
             return 0
 
         lax.fori_loop(0, tiles, end, 0)
+
+        def end_half(index, _):
+            up_to_dp(index).wait()
+            return 0
+
+        lax.fori_loop(0, tiles // 2, end_half, 0)
 
 
 def expert_pass(rows, cots, note, gate, up, down):
@@ -2024,11 +2050,12 @@
         in_specs=[whole, whole, whole_note, early, early, both],
         out_specs=[pl.BlockSpec(rows.shape, lambda i: (0, 0, 0), pipeline_mode=once)]
         + [late, late]
-        + [IN_PLACE] * 3,
+        + [IN_PLACE] * 4,
         out_shape=[jax.ShapeDtypeStruct(rows.shape, BF16)]
         + [jax.ShapeDtypeStruct((width, hidden), BF16)] * 2
         + [
             jax.ShapeDtypeStruct((width, hidden), BF16),
+            jax.ShapeDtypeStruct((width, hidden // 2), BF16),
             jax.ShapeDtypeStruct(rows.shape, BF16),
             jax.ShapeDtypeStruct(note.shape, F32),
         ],
@@ -2045,6 +2072,7 @@
             pltpu.VMEM(note.shape, F32),
             pltpu.VMEM((tiles, width, tile), BF16),
             pltpu.VMEM((tiles, width, tile), BF16),
+            pltpu.VMEM((tiles // 2, width, tile), BF16),
         ]
         + swap_semaphores(total)
         + swap_semaphores(total)
@@ -2052,6 +2080,8 @@
             pltpu.SemaphoreType.DMA((tiles,)),
             pltpu.SemaphoreType.DMA((tiles,)),
             pltpu.SemaphoreType.DMA((tiles,)),
+            pltpu.SemaphoreType.DMA((tiles // 2,)),
+            pltpu.SemaphoreType.DMA((tiles // 2,)),
         ],
         compiler_params=remote_params(4),
         cost_estimate=pl.CostEstimate(
@@ -2208,7 +2238,7 @@
         down_crossed,
     )
     grad_shared = lax.psum_scatter(grad_shared, ("sp", "fs"), scatter_dimension=0)
-    expert_out, dgate, dup, sum_down, grad_returned, dots = expert_pass(
+    expert_out, dgate, dup, sum_down, other_up_half, grad_returned, dots = expert_pass(
         rows,
         arrived_cots,
         notes,
@@ -2229,7 +2259,7 @@
     def spread(parts):
         return lax.all_to_all(parts, "sp", split_axis=0, concat_axis=0, tiled=True).astype(F32)
 
-    other_gate, other_up = to_dp(dgate), to_dp(dup)
+    other_gate, other_up = to_dp(dgate), to_dp(dup[:, other_up_half.shape[1] :])
 
     grad_result = cot_rows.astype(F32)
     grad_gates = jnp.stack(
@@ -2272,12 +2302,22 @@
         expert_out,
         score_scale,
     )
-    other_gate, other_up, grad_shared, dense, grad_normed = lax.optimization_barrier(
-        (other_gate, other_up, grad_shared, dense, grad_normed)
+    other_gate, other_up, grad_shared, grad_normed = lax.optimization_barrier(
+        (other_gate, other_up, grad_shared, grad_normed)
     )
     dense = lax.psum_scatter(dense, ("sp", "fs"), scatter_dimension=0, tiled=True)
-    sum_up = spread(sum_of(dup, other_up))
+    parts_up, tail, sum_down, returned, grad_normed = lax.optimization_barrier(
+        (
+            sum_of(dup, jnp.concatenate([other_up_half, other_up], axis=1)),
+            tail,
+            sum_down,
+            returned,
+            grad_normed,
+        )
+    )
+    sum_up = spread(parts_up)
     sum_gate = spread(sum_of(dgate, other_gate))
+    dense, sum_gate = lax.optimization_barrier((dense, sum_gate))
     sum_down = sum_down.astype(F32)
     output = (middle + shared_out + outer(taking, returned.reshape(slot_total, width))).astype(BF16)
     grad_normed = grad_normed.astype(F32)

time: 637 us -> 617 us (0.969)
  waiting for transfers between devices: 50.9 us -> 22.6 us
  local copies, waits for them, and re-layouts: 16.2 us -> 31.5 us
    unnamed x5, waiting for transfers between devices: 35.4 us -> 0.75 us
    all_to_all x2, waiting for transfers between devices: 9.64 us -> 21.3 us  [spread(): lax.all_to_all(parts, 'sp', split_axis=0, concat_axis=0, tiled=True)]
  transfers between devices with their start and end apart: 11 -> 11, of which waited for: 4 -> 3; matrix products, arithmetic and copies ran while one was open for 11% -> 15% of each run, Pallas kernels for 66% -> 67%
where the time goes in v5:
time: 617 us; the launch traced here: 607 us
  Pallas kernels  457 us (74%)
  other arithmetic  44.7 us (7%)
  local copies, waits for them, and re-layouts  31.5 us (5%)
  waiting for transfers between devices  22.6 us (4%)
  matrix products  18.4 us (3%)
  starting transfers between devices  17.5 us (3%)
  between operations  14.7 us (2%)
    pallas_call x1, Pallas kernels, front(): pl.pallas_call(functools.partial(front_kernel, score_scale), in_specs=[IN...  168 us
    pallas_call x1, Pallas kernels, attend_grad(): pl.pallas_call(functools.partial(attend_grad_kernel, block, score_scale),...  123 us
    pallas_call x1, Pallas kernels, expert_pass(): pl.pallas_call(expert_kernel, grid=(2 * tiles,), in_specs=[whole, whole,...  115 us
    pallas_call x1, Pallas kernels, dispatch(): pl.pallas_call(dispatch_kernel, grid=(tiles,), in_specs=[whole, whole, pl...  51.3 us
    all_to_all x2, waiting for transfers between devices, spread(): lax.all_to_all(parts, 'sp', split_axis=0, concat_axis=0, tiled=True)  21.3 us
  transfers between devices with their start and end apart: 11, of which 3 were waited for; matrix products, arithmetic and copies ran while one was open for 15% of the time, Pallas kernels for 67%

profile of v5, /device:TPU:12, one launch (start us, length us, event | category | flops | bytes accessed | tf_op | source)
XLA Modules:
  0.0 606.8 jit_solution(9237757273496512325)
XLA Ops:
  14.1 167.6 %front.1 = (s32[2,512]{1,0:T(2,128)}, bf16[1152,512]{1,0:T(8,128)(2,1)}, bf16[2048,768]{1,0:T(8,128)(2,1)}, bf16[768,640]{1,0:T(8,128)(2,1)}, bf16[576,2048]{1,0...) custom-call(bf16[4,128,768]{2,1,0:T(8,128)(2,1)} %tokens_ref.1, ...), custom_call_target="tpu_custom_call" | custom-call | flops 99999997952 | bytes 4000000 | tf_op jit(solution)/shard_map/front/pallas_call | solution.py:1241
  181.7 1.9 convert_reduce_fusion
  184.4 2.4 multiply_reduce_fusion.2
  190.1 3.6 convolution_convert_fusion
  194.2 51.3 %dispatch.1 = (f32[512,768]{1,0:T(8,128)}, f32[512,768]{1,0:T(8,128)}, bf16[16,2304,128]{2,1,0:T(8,128)(2,1)}, bf16[16,72,768]{2,1,0:T(8,128)(2,1)}, f32[16,8,12...) custom-call(bf16[512,768]{1,0:T(8,128)(2,1)} %copy-done.4, ...), custom_call_target="tpu_custom_call", output_to_operand_aliasing={{5}: (7, {})} | custom-call | flops 40000000000 | bytes 20000000 | tf_op jit(solution)/shard_map/dispatch/pallas_call | solution.py:1809
  245.7 115.4 %expert_pass.1 = (bf16[16,72,768]{2,1,0:T(8,128)(2,1)}, bf16[768,2048]{1,0:T(8,128)(2,1)}, bf16[768,2048]{1,0:T(8,128)(2,1)}, bf16[768,2048]{1,0:T(8,128)(2,1)},...) custom-call(bf16[1152,768]{1,0:T(8,128)(2,1)} %bitcast.142, ...), custom_call_target="tpu_custom_call" | custom-call | flops 80000000000 | bytes 30000000 | tf_op jit(solution)/shard_map/expert_pass/pallas_call | solution.py:2047
  363.0 2.8 fusion.21
  365.9 1.9 multiply_reduce_fusion
  371.2 2.7 copy.121
  373.9 2.7 slice.65
  378.6 3.0 fusion.6.ga_ref
  381.6 123.1 %attend_grad.1 = (bf16[512,768]{1,0:T(8,128)(2,1)}, bf16[4,192,2048]{2,1,0:T(8,128)(2,1)}, bf16[16,72,768]{2,1,0:T(8,128)(2,1)}, bf16[16,48,640]{2,1,0:T(8,128)(2,1)}) custom-call(bf16[576,2048]{1,0:T(8,128)(2,1)} %get-tuple-element.71.qkv_ref, f32[32,2048]{1,0:T(8,128)} %get-tuple-element.190.cos_ref, f32[32,2048]{1,0:T(8,128)} %get-tuple-element.189.sin_ref, ...), custom_call_target="tpu_custom_call" | custom-call | flops 60000002048 | bytes 8000000 | tf_op jit(solution)/shard_map/attend_grad/pallas_call | solution.py:1617
  504.8 6.1 %add_convert_fusion = bf16[768,2048]{1,0:T(8,128)(2,1)} fusion(bf16[768,2048]{1,0:T(8,128)(2,1)} %collective-permute-done, bf16[768,2048]{1,0:T(8,128)(2,1)} %get-tuple-element.69), kind=kLoop, calls=%fused_computation | loop fusion | flops 6291456 | bytes 9437184 | tf_op jit(solution)/shard_map/convert_element_type | solution.py:2256
  510.9 6.3 %all-to-all-start = ((bf16[4,192,2048]{2,1,0:T(8,128)(2,1)}), bf16[4,192,2048]{2,1,0:T(8,128)(2,1)}, u32[]{:S(2)}, u32[]{:S(2)}) async-start(bf16[4,192,2048]{2,1,0:T(8,128)(2,1)} %bitcast.101), calls=%async_computation.1 | async-start | bytes 6291456 | tf_op jit(solution)/shard_map/all_to_all | solution.py:2260
  520.3 6.2 %add_convert_fusion.1 = bf16[768,2048]{1,0:T(8,128)(2,1)} fusion(bf16[768,2048]{1,0:T(8,128)(2,1)} %get-tuple-element.67, bf16[768,1024]{1,0:T(8,128)(2,1)} %collective-permute-done.1, bf16[768,1024]{1,0:T(8,128)(2,1)} %get-tuple-element.68), kind=kLoop, calls=%fused_computation.1 | loop fusion | flops 11010048 | bytes 9437184 | tf_op jit(solution)/shard_map/convert_element_type | solution.py:2256
  529.4 3.5 convert_element_type.172
  534.2 2.1 add_convert_fusion.2
  537.9 14.7 %all-to-all-done = bf16[4,192,2048]{2,1,0:T(8,128)(2,1)} async-done(((bf16[4,192,2048]{2,1,0:T(8,128)(2,1)}), bf16[4,192,2048]{2,1,0:T(8,128)(2,1)}, u32[]{:S(2)}, u32[]{:S(2)}) %all-to-all-start) | async-done | bytes 3145760 | tf_op jit(solution)/shard_map/all_to_all | solution.py:2260
  552.6 5.3 all-to-all-start.1
  559.8 2.2 reshape.262
  562.0 2.5 fusion.17
  574.9 5.4 convert_element_type.166
  586.6 6.6 %all-to-all-done.1 = bf16[4,192,2048]{2,1,0:T(8,128)(2,1)S(1)} async-done(((bf16[4,192,2048]{2,1,0:T(8,128)(2,1)}), bf16[4,192,2048]{2,1,0:T(8,128)(2,1)S(1)}, u32[]{:S(2)}, u32[]{:S(2)}) %all-to-all-start.1) | async-done | bytes 3145760 | tf_op jit(solution)/shard_map/all_to_all | solution.py:2260
  593.2 3.5 convert_element_type.171
  (139 shorter events, 49.2 us)
Async XLA Ops:
  7.2 177.2 %all-gather.4.cloned.1.call-start = ((), (), s32[]{:S(2)}) async-start(), calls=%async_computation.4 | async-start | bytes 1253376 | tf_op jit(solution)/shard_map/all_gather | solution.py:2154
  7.9 186.2 %all-gather.6.cloned.1.call-start = ((), (), s32[]{:S(2)}) async-start(), calls=%async_computation.6 | async-start | bytes 10027008 | tf_op jit(solution)/shard_map/all_gather | solution.py:2154
  11.2 493.6 %reduce-scatter.5.cloned.1.call-start = ((), (), s32[]{:S(2)}) async-start(), calls=%async_computation.5 | async-start | bytes 10027008 | tf_op jit(solution)/shard_map/reduce_scatter | solution.py:2240
  14.1 170.3 %copy-start.2 = (bf16[4,128,768]{2,1,0:T(8,128)(2,1)S(1)}, bf16[4,128,768]{2,1,0:T(8,128)(2,1)}, u32[]{:S(2)}) copy-start(bf16[4,128,768]{2,1,0:T(8,128)(2,1)} %tokens_ref.1) | copy-start | bytes 2359300
  187.0 6.6 %copy-start.4 = (bf16[512,768]{1,0:T(8,128)(2,1)}, bf16[512,768]{1,0:T(8,128)(2,1)S(1)}, u32[]{:S(2)}) copy-start(bf16[512,768]{1,0:T(8,128)(2,1)S(1)} %multiply_convert_fusion.x_ref) | copy-start | bytes 2359300
  245.5 273.1 %reduce-scatter.7.cloned.1.call-start = ((), (), s32[]{:S(2)}) async-start(), calls=%async_computation.7 | async-start | bytes 1462272
  245.7 117.3 %copy-start.9 = (bf16[1152,512]{1,0:T(8,128)(2,1)S(1)}, bf16[1152,512]{1,0:T(8,128)(2,1)}, u32[]{:S(2)}) copy-start(bf16[1152,512]{1,0:T(8,128)(2,1)} %get-tuple-element.57) | copy-start | bytes 3538948
  376.6 128.2 %collective-permute-start.1 = (bf16[768,1024]{1,0:T(8,128)(2,1)}, bf16[768,1024]{1,0:T(8,128)(2,1)}, u32[]{:S(2)}, u32[]{:S(2)}) collective-permute-start(bf16[768,1024]{1,0:T(8,128)(2,1)} %slice.65), channel_id=1, source_target_pairs={{0,16},{16,0},{1,17},{17,1},{2,18},{18,2},{3,19},{19,3},{4,20},{20... | collective-permute-start | bytes 4718600 | tf_op jit(solution)/shard_map/ppermute | solution.py:2253
  378.1 126.7 %collective-permute-start = (bf16[768,2048]{1,0:T(8,128)(2,1)}, bf16[768,2048]{1,0:T(8,128)(2,1)}, u32[]{:S(2)}, u32[]{:S(2)}) collective-permute-start(bf16[768,2048]{1,0:T(8,128)(2,1)} %get-tuple-element.69), channel_id=1, source_target_pairs={{0,16},{16,0},{1,17},{17,1},{2,18},{18,2},{3,19},{19,3},{4,20},{20... | collective-permute-start | bytes 9437192 | tf_op jit(solution)/shard_map/ppermute | solution.py:2253
  510.9 41.7 %all-to-all-start = ((bf16[4,192,2048]{2,1,0:T(8,128)(2,1)}), bf16[4,192,2048]{2,1,0:T(8,128)(2,1)}, u32[]{:S(2)}, u32[]{:S(2)}) async-start(bf16[4,192,2048]{2,1,0:T(8,128)(2,1)} %bitcast.101), calls=%async_computation.1 | async-start | bytes 6291456 | tf_op jit(solution)/shard_map/all_to_all | solution.py:2260
  520.3 6.2 %copy-start.11 = (bf16[16,48,640]{2,1,0:T(8,128)(2,1)S(1)}, bf16[16,48,640]{2,1,0:T(8,128)(2,1)}, u32[]{:S(2)}) copy-start(bf16[16,48,640]{2,1,0:T(8,128)(2,1)} %get-tuple-element.88) | copy-start | bytes 2949124
  520.3 9.1 %copy-start.7 = (bf16[4,192,2048]{2,1,0:T(8,128)(2,1)S(1)}, bf16[4,192,2048]{2,1,0:T(8,128)(2,1)}, u32[]{:S(2)}) copy-start(bf16[4,192,2048]{2,1,0:T(8,128)(2,1)} %get-tuple-element.94) | copy-start | bytes 9437188
  527.4 5.6 copy-start.3
  527.4 5.6 copy-start.6
  527.4 5.6 copy-start.15
  527.4 30.5 %collective-permute-start.2 = (bf16[4,48,576]{2,1,0:T(8,128)(2,1)}, bf16[4,48,576]{2,1,0:T(8,128)(2,1)}, u32[]{:S(2)}, u32[]{:S(2)}) collective-permute-start(bf16[4,48,576]{2,1,0:T(8,128)(2,1)} %slice_reduce_fusion), channel_id=1, source_target_pairs={{0,16},{16,0},{1,17},{17,1},{2,18},{18,2},{3,19},{19,3},{4,20},{20... | collective-permute-start | bytes 663560 | tf_op jit(solution)/shard_map/ppermute | solution.py:2103
  528.9 43.8 %collective-permute-start.4 = (bf16[2304,128]{1,0:T(8,128)(2,1)}, bf16[2304,128]{1,0:T(8,128)(2,1)}, u32[]{:S(2)}, u32[]{:S(2)}) collective-permute-start(bf16[2304,128]{1,0:T(8,128)(2,1)} %bitcast.25), channel_id=1, source_target_pairs={{0,16},{16,0},{1,17},{17,1},{2,18},{18,2},{3,19},{19,3},{4,20},{20... | collective-permute-start | bytes 1769480 | tf_op jit(solution)/shard_map/ppermute | solution.py:2103
  529.4 3.9 copy-start.21
  529.4 3.9 copy-start.22
  552.6 40.6 %all-to-all-start.1 = ((bf16[4,192,2048]{2,1,0:T(8,128)(2,1)}), bf16[4,192,2048]{2,1,0:T(8,128)(2,1)S(1)}, u32[]{:S(2)}, u32[]{:S(2)}) async-start(bf16[4,192,2048]{2,1,0:T(8,128)(2,1)} %bitcast.100), calls=%async_computation.2 | async-start | bytes 6291456 | tf_op jit(solution)/shard_map/all_to_all | solution.py:2260
  564.5 7.6 %copy-start.19 = (bf16[48]{0:T(256)(128)(2,1)S(1)}, bf16[48]{0:T(256)(128)(2,1)}, u32[]{:S(2)}) copy-start(bf16[48]{0:T(256)(128)(2,1)} %param.20) | copy-start | bytes 292
  569.9 5.0 copy-start.14
  580.3 16.4 %collective-permute-start.3 = (bf16[48,896]{0,1:T(8,128)(2,1)}, bf16[48,896]{0,1:T(8,128)(2,1)}, u32[]{:S(2)}, u32[]{:S(2)}) collective-permute-start(bf16[48,896]{0,1:T(8,128)(2,1)} %copy.122), channel_id=1, source_target_pairs={{0,16},{16,0},{1,17},{17,1},{2,18},{18,2},{3,19},{19,3},{4,20},{20... | collective-permute-start | bytes 258056 | tf_op jit(solution)/shard_map/ppermute | solution.py:2103
  593.2 6.6 %copy-start.1 = (bf16[48,2048]{1,0:T(8,128)(2,1)S(1)}, bf16[48,2048]{1,0:T(8,128)(2,1)}, u32[]{:S(2)}) copy-start(bf16[48,2048]{1,0:T(8,128)(2,1)} %param.27) | copy-start | bytes 589828
  (10 other events, 20.2 us)
Sparse Core Ops, SparseCore 0:
  10.3 50.8 all-gather.3
  64.1 129.9 all-gather.5
  245.6 154.0 reduce-scatter.4
  404.3 65.2 reduce-scatter.6

commit v6 on v5

--- a/solution.py
+++ b/solution.py
@@ -1869,6 +1869,7 @@
     y_ref,
     dgate_ref,
     dup_ref,
+    dup_late_ref,
     sum_ref,
     other_up_ref,
     got_ref,
@@ -1990,10 +1991,14 @@
         acc[...] += dot_nt(hidden, down_ref[...])
         dgate_ref[...] = dot32(x_feat[...], gate_all[here]).astype(BF16)
         dup = dot32(x_feat[...], up_all[here]).astype(BF16)
-        dup_ref[...] = dup
+
+        @pl.when(here >= tiles // 2)
+        def _():
+            dup_late_ref[...] = dup
 
         @pl.when(here < tiles // 2)
         def _():
+            dup_ref[...] = dup
             up_sent[here] = dup
             up_to_dp(here).start()
 
@@ -2044,15 +2049,19 @@
     early = pl.BlockSpec((width, tile), lambda i: (0, jnp.minimum(i, tiles - 1)))
     both = pl.BlockSpec((width, tile), lambda i: (0, lax.rem(i, tiles)))
     late = pl.BlockSpec((width, tile), lambda i: (0, jnp.clip(i - tiles, 0, tiles - 1)))
+    half = tiles // 2
+    late_first = pl.BlockSpec((width, tile), lambda i: (0, jnp.clip(i - tiles, 0, half - 1)))
+    late_last = pl.BlockSpec((width, tile), lambda i: (0, jnp.clip(i - tiles - half, 0, half - 1)))
     return pl.pallas_call(
         expert_kernel,
         grid=(2 * tiles,),
         in_specs=[whole, whole, whole_note, early, early, both],
         out_specs=[pl.BlockSpec(rows.shape, lambda i: (0, 0, 0), pipeline_mode=once)]
-        + [late, late]
+        + [late, late_first, late_last]
         + [IN_PLACE] * 4,
         out_shape=[jax.ShapeDtypeStruct(rows.shape, BF16)]
-        + [jax.ShapeDtypeStruct((width, hidden), BF16)] * 2
+        + [jax.ShapeDtypeStruct((width, hidden), BF16)]
+        + [jax.ShapeDtypeStruct((width, hidden // 2), BF16)] * 2
         + [
             jax.ShapeDtypeStruct((width, hidden), BF16),
             jax.ShapeDtypeStruct((width, hidden // 2), BF16),
@@ -2238,7 +2247,7 @@
         down_crossed,
     )
     grad_shared = lax.psum_scatter(grad_shared, ("sp", "fs"), scatter_dimension=0)
-    expert_out, dgate, dup, sum_down, other_up_half, grad_returned, dots = expert_pass(
+    expert_out, dgate, dup, dup_late, sum_down, other_up_half, grad_returned, dots = expert_pass(
         rows,
         arrived_cots,
         notes,
@@ -2259,7 +2268,7 @@
     def spread(parts):
         return lax.all_to_all(parts, "sp", split_axis=0, concat_axis=0, tiled=True).astype(F32)
 
-    other_gate, other_up = to_dp(dgate), to_dp(dup[:, other_up_half.shape[1] :])
+    other_gate, other_up = to_dp(dgate), to_dp(dup_late)
 
     grad_result = cot_rows.astype(F32)
     grad_gates = jnp.stack(
@@ -2308,7 +2317,10 @@
     dense = lax.psum_scatter(dense, ("sp", "fs"), scatter_dimension=0, tiled=True)
     parts_up, tail, sum_down, returned, grad_normed = lax.optimization_barrier(
         (
-            sum_of(dup, jnp.concatenate([other_up_half, other_up], axis=1)),
+            sum_of(
+                jnp.concatenate([dup, dup_late], axis=1),
+                jnp.concatenate([other_up_half, other_up], axis=1),
+            ),
             tail,
             sum_down,
             returned,

time: 617 us -> 619 us (level)
  transfers between devices with their start and end apart: 11 -> 11, of which waited for: 3 -> 3; matrix products, arithmetic and copies ran while one was open for 15% -> 14% of each run, Pallas kernels for 67% -> 67%
where the time goes in v6:
time: 619 us; the launch traced here: 608 us
  Pallas kernels  461 us (74%)
  other arithmetic  43.3 us (7%)
  local copies, waits for them, and re-layouts  28.8 us (5%)
  waiting for transfers between devices  24.1 us (4%)
  matrix products  18.4 us (3%)
  starting transfers between devices  17.8 us (3%)
  between operations  14.7 us (2%)
    pallas_call x1, Pallas kernels, front(): pl.pallas_call(functools.partial(front_kernel, score_scale), in_specs=[IN...  168 us
    pallas_call x1, Pallas kernels, attend_grad(): pl.pallas_call(functools.partial(attend_grad_kernel, block, score_scale),...  127 us
    pallas_call x1, Pallas kernels, expert_pass(): pl.pallas_call(expert_kernel, grid=(2 * tiles,), in_specs=[whole, whole,...  115 us
    pallas_call x1, Pallas kernels, dispatch(): pl.pallas_call(dispatch_kernel, grid=(tiles,), in_specs=[whole, whole, pl...  51.3 us
    all_to_all x2, waiting for transfers between devices, spread(): lax.all_to_all(parts, 'sp', split_axis=0, concat_axis=0, tiled=True)  22.9 us
  transfers between devices with their start and end apart: 11, of which 3 were waited for; matrix products, arithmetic and copies ran while one was open for 14% of the time, Pallas kernels for 67%

profile of v6, /device:TPU:12, one launch (start us, length us, event | category | flops | bytes accessed | tf_op | source)
XLA Modules:
  0.0 608.3 jit_solution(11309504640550962669)
XLA Ops:
  14.1 167.6 %front.1 = (s32[2,512]{1,0:T(2,128)}, bf16[1152,512]{1,0:T(8,128)(2,1)}, bf16[2048,768]{1,0:T(8,128)(2,1)}, bf16[768,640]{1,0:T(8,128)(2,1)}, bf16[576,2048]{1,0...) custom-call(bf16[4,128,768]{2,1,0:T(8,128)(2,1)} %tokens_ref.1, ...), custom_call_target="tpu_custom_call" | custom-call | flops 99999997952 | bytes 4000000 | tf_op jit(solution)/shard_map/front/pallas_call | solution.py:1241
  181.7 1.9 convert_reduce_fusion
  184.4 2.4 multiply_reduce_fusion.2
  190.1 3.6 convolution_convert_fusion
  194.2 51.3 %dispatch.1 = (f32[512,768]{1,0:T(8,128)}, f32[512,768]{1,0:T(8,128)}, bf16[16,2304,128]{2,1,0:T(8,128)(2,1)}, bf16[16,72,768]{2,1,0:T(8,128)(2,1)}, f32[16,8,12...) custom-call(bf16[512,768]{1,0:T(8,128)(2,1)} %copy-done.4, ...), custom_call_target="tpu_custom_call", output_to_operand_aliasing={{5}: (7, {})} | custom-call | flops 40000000000 | bytes 20000000 | tf_op jit(solution)/shard_map/dispatch/pallas_call | solution.py:1809
  245.7 115.4 %expert_pass.1 = (bf16[16,72,768]{2,1,0:T(8,128)(2,1)}, bf16[768,2048]{1,0:T(8,128)(2,1)}, bf16[768,1024]{1,0:T(8,128)(2,1)}, bf16[768,1024]{1,0:T(8,128)(2,1)},...) custom-call(bf16[1152,768]{1,0:T(8,128)(2,1)} %bitcast.147, ...), custom_call_target="tpu_custom_call" | custom-call | flops 80000000000 | bytes 30000000 | tf_op jit(solution)/shard_map/expert_pass/pallas_call | solution.py:2055
  363.0 2.8 fusion.21
  365.9 1.9 multiply_reduce_fusion
  371.2 2.7 copy.121
  376.0 3.0 fusion.6.ga_ref
  379.0 126.8 %attend_grad.1 = (bf16[512,768]{1,0:T(8,128)(2,1)}, bf16[4,192,2048]{2,1,0:T(8,128)(2,1)}, bf16[16,72,768]{2,1,0:T(8,128)(2,1)}, bf16[16,48,640]{2,1,0:T(8,128)(2,1)}) custom-call(bf16[576,2048]{1,0:T(8,128)(2,1)} %get-tuple-element.73.qkv_ref, f32[32,2048]{1,0:T(8,128)} %get-tuple-element.192.cos_ref, f32[32,2048]{1,0:T(8,128)} %get-tuple-element.191.sin_ref, ...), custom_call_target="tpu_custom_call" | custom-call | flops 60000002048 | bytes 8000000 | tf_op jit(solution)/shard_map/attend_grad/pallas_call | solution.py:1617
  505.8 6.1 %add_convert_fusion = bf16[768,2048]{1,0:T(8,128)(2,1)} fusion(bf16[768,2048]{1,0:T(8,128)(2,1)} %collective-permute-done, bf16[768,2048]{1,0:T(8,128)(2,1)} %get-tuple-element.71), kind=kLoop, calls=%fused_computation | loop fusion | flops 6291456 | bytes 9437184 | tf_op jit(solution)/shard_map/convert_element_type | solution.py:2265
  511.9 6.5 %all-to-all-start = ((bf16[4,192,2048]{2,1,0:T(8,128)(2,1)}), bf16[4,192,2048]{2,1,0:T(8,128)(2,1)}, u32[]{:S(2)}, u32[]{:S(2)}) async-start(bf16[4,192,2048]{2,1,0:T(8,128)(2,1)} %bitcast.103), calls=%async_computation.1 | async-start | bytes 6291456 | tf_op jit(solution)/shard_map/all_to_all | solution.py:2269
  521.6 4.8 add_convert_fusion.1
  529.2 3.6 convert_element_type.175
  534.0 2.1 add_convert_fusion.2
  537.7 16.1 %all-to-all-done = bf16[4,192,2048]{2,1,0:T(8,128)(2,1)} async-done(((bf16[4,192,2048]{2,1,0:T(8,128)(2,1)}), bf16[4,192,2048]{2,1,0:T(8,128)(2,1)}, u32[]{:S(2)}, u32[]{:S(2)}) %all-to-all-start) | async-done | bytes 3145760 | tf_op jit(solution)/shard_map/all_to_all | solution.py:2269
  553.9 5.6 all-to-all-start.1
  561.3 2.2 reshape.263
  563.6 2.5 fusion.17
  576.4 5.4 convert_element_type.169
  584.1 1.9 copy.117
  587.9 6.7 %all-to-all-done.1 = bf16[4,192,2048]{2,1,0:T(8,128)(2,1)S(1)} async-done(((bf16[4,192,2048]{2,1,0:T(8,128)(2,1)}), bf16[4,192,2048]{2,1,0:T(8,128)(2,1)S(1)}, u32[]{:S(2)}, u32[]{:S(2)}) %all-to-all-start.1) | async-done | bytes 3145760 | tf_op jit(solution)/shard_map/all_to_all | solution.py:2269
  594.7 3.5 convert_element_type.174
  (138 shorter events, 47.1 us)
Async XLA Ops:
  7.2 177.2 %all-gather.4.cloned.1.call-start = ((), (), s32[]{:S(2)}) async-start(), calls=%async_computation.4 | async-start | bytes 1253376 | tf_op jit(solution)/shard_map/all_gather | solution.py:2163
  7.9 186.2 %all-gather.6.cloned.1.call-start = ((), (), s32[]{:S(2)}) async-start(), calls=%async_computation.6 | async-start | bytes 10027008 | tf_op jit(solution)/shard_map/all_gather | solution.py:2163
  11.2 494.7 %reduce-scatter.5.cloned.1.call-start = ((), (), s32[]{:S(2)}) async-start(), calls=%async_computation.5 | async-start | bytes 10027008 | tf_op jit(solution)/shard_map/reduce_scatter | solution.py:2249
  14.1 170.3 %copy-start.2 = (bf16[4,128,768]{2,1,0:T(8,128)(2,1)S(1)}, bf16[4,128,768]{2,1,0:T(8,128)(2,1)}, u32[]{:S(2)}) copy-start(bf16[4,128,768]{2,1,0:T(8,128)(2,1)} %tokens_ref.1) | copy-start | bytes 2359300
  187.1 6.6 %copy-start.4 = (bf16[512,768]{1,0:T(8,128)(2,1)}, bf16[512,768]{1,0:T(8,128)(2,1)S(1)}, u32[]{:S(2)}) copy-start(bf16[512,768]{1,0:T(8,128)(2,1)S(1)} %multiply_convert_fusion.x_ref) | copy-start | bytes 2359300
  245.4 274.4 %reduce-scatter.7.cloned.1.call-start = ((), (), s32[]{:S(2)}) async-start(), calls=%async_computation.7 | async-start | bytes 1462272
  245.7 117.3 %copy-start.9 = (bf16[1152,512]{1,0:T(8,128)(2,1)S(1)}, bf16[1152,512]{1,0:T(8,128)(2,1)}, u32[]{:S(2)}) copy-start(bf16[1152,512]{1,0:T(8,128)(2,1)} %get-tuple-element.58) | copy-start | bytes 3538948
  373.9 131.9 %collective-permute-start.1 = (bf16[768,1024]{1,0:T(8,128)(2,1)}, bf16[768,1024]{1,0:T(8,128)(2,1)}, u32[]{:S(2)}, u32[]{:S(2)}) collective-permute-start(bf16[768,1024]{1,0:T(8,128)(2,1)} %get-tuple-element.69), channel_id=1, source_target_pairs={{0,16},{16,0},{1,17},{17,1},{2,18},{18,2},{3,19},{19,3},{4,20},{20... | collective-permute-start | bytes 4718600 | tf_op jit(solution)/shard_map/ppermute | solution.py:2262
  375.4 130.4 %collective-permute-start = (bf16[768,2048]{1,0:T(8,128)(2,1)}, bf16[768,2048]{1,0:T(8,128)(2,1)}, u32[]{:S(2)}, u32[]{:S(2)}) collective-permute-start(bf16[768,2048]{1,0:T(8,128)(2,1)} %get-tuple-element.71), channel_id=1, source_target_pairs={{0,16},{16,0},{1,17},{17,1},{2,18},{18,2},{3,19},{19,3},{4,20},{20... | collective-permute-start | bytes 9437192 | tf_op jit(solution)/shard_map/ppermute | solution.py:2262
  511.9 41.9 %all-to-all-start = ((bf16[4,192,2048]{2,1,0:T(8,128)(2,1)}), bf16[4,192,2048]{2,1,0:T(8,128)(2,1)}, u32[]{:S(2)}, u32[]{:S(2)}) async-start(bf16[4,192,2048]{2,1,0:T(8,128)(2,1)} %bitcast.103), calls=%async_computation.1 | async-start | bytes 6291456 | tf_op jit(solution)/shard_map/all_to_all | solution.py:2269
  521.6 4.8 copy-start.11
  521.6 7.6 %copy-start.7 = (bf16[4,192,2048]{2,1,0:T(8,128)(2,1)S(1)}, bf16[4,192,2048]{2,1,0:T(8,128)(2,1)}, u32[]{:S(2)}) copy-start(bf16[4,192,2048]{2,1,0:T(8,128)(2,1)} %get-tuple-element.96) | copy-start | bytes 9437188
  527.2 5.6 copy-start.3
  527.2 5.6 copy-start.6
  527.2 5.6 copy-start.15
  527.2 32.3 %collective-permute-start.2 = (bf16[4,48,576]{2,1,0:T(8,128)(2,1)}, bf16[4,48,576]{2,1,0:T(8,128)(2,1)}, u32[]{:S(2)}, u32[]{:S(2)}) collective-permute-start(bf16[4,48,576]{2,1,0:T(8,128)(2,1)} %slice_reduce_fusion), channel_id=1, source_target_pairs={{0,16},{16,0},{1,17},{17,1},{2,18},{18,2},{3,19},{19,3},{4,20},{20... | collective-permute-start | bytes 663560 | tf_op jit(solution)/shard_map/ppermute | solution.py:2112
  528.5 45.7 %collective-permute-start.4 = (bf16[2304,128]{1,0:T(8,128)(2,1)}, bf16[2304,128]{1,0:T(8,128)(2,1)}, u32[]{:S(2)}, u32[]{:S(2)}) collective-permute-start(bf16[2304,128]{1,0:T(8,128)(2,1)} %bitcast.28), channel_id=1, source_target_pairs={{0,16},{16,0},{1,17},{17,1},{2,18},{18,2},{3,19},{19,3},{4,20},{20... | collective-permute-start | bytes 1769480 | tf_op jit(solution)/shard_map/ppermute | solution.py:2112
  529.2 3.9 copy-start.21
  529.2 3.9 copy-start.22
  553.9 40.8 %all-to-all-start.1 = ((bf16[4,192,2048]{2,1,0:T(8,128)(2,1)}), bf16[4,192,2048]{2,1,0:T(8,128)(2,1)S(1)}, u32[]{:S(2)}, u32[]{:S(2)}) async-start(bf16[4,192,2048]{2,1,0:T(8,128)(2,1)} %add_convert_fusion.1), calls=%async_computation.2 | async-start | bytes 6291456 | tf_op jit(solution)/shard_map/all_to_all | solution.py:2269
  566.1 7.6 %copy-start.19 = (bf16[48]{0:T(256)(128)(2,1)S(1)}, bf16[48]{0:T(256)(128)(2,1)}, u32[]{:S(2)}) copy-start(bf16[48]{0:T(256)(128)(2,1)} %param.20) | copy-start | bytes 292
  571.4 5.0 copy-start.14
  581.9 16.4 %collective-permute-start.3 = (bf16[48,896]{0,1:T(8,128)(2,1)}, bf16[48,896]{0,1:T(8,128)(2,1)}, u32[]{:S(2)}, u32[]{:S(2)}) collective-permute-start(bf16[48,896]{0,1:T(8,128)(2,1)} %copy.122), channel_id=1, source_target_pairs={{0,16},{16,0},{1,17},{17,1},{2,18},{18,2},{3,19},{19,3},{4,20},{20... | collective-permute-start | bytes 258056 | tf_op jit(solution)/shard_map/ppermute | solution.py:2112
  594.7 6.6 %copy-start.1 = (bf16[48,2048]{1,0:T(8,128)(2,1)S(1)}, bf16[48,2048]{1,0:T(8,128)(2,1)}, u32[]{:S(2)}) copy-start(bf16[48,2048]{1,0:T(8,128)(2,1)} %param.27) | copy-start | bytes 589828
  (10 other events, 20.2 us)
Sparse Core Ops, SparseCore 0:
  10.3 50.8 all-gather.3
  64.1 129.9 all-gather.5
  245.6 156.6 reduce-scatter.4
  406.9 70.8 reduce-scatter.6
